TPU v7x, 256 devices: a whole 4x4x8 slice. The times are simulated.
256 devices in a mesh: dp: 64 (over x, z, core), mp: 4 (over y).
Axes of the slice: x: 4, y: 4, z: 8, core: 2. Of those that a mesh axis runs over, the one named last changes fastest.
Arguments:
- inputs: bfloat16 [49152, 4608], P('dp'), may hold values from -8 to 8
- key_cotangent: bfloat16 [49152, 2048], P('dp', 'mp'), may hold values from -8 to 8
- master: float32 [4608, 2048], P('dp', 'mp'), may hold values from -0.09375 to 0.09375
- first_codes: int32 [4608, 2048], P('dp', 'mp'), may hold values from -127 to 127
- second_codes: int32 [4608, 2048], P('dp', 'mp'), may hold values from 1 to 255
- first_scale: float32 [1152, 4], P('dp', 'mp'), may hold values from 0.05 to 0.5
- second_scale: float32 [1152, 4], P('dp', 'mp'), may hold values from 0.02 to 0.2
Outputs:
- weight: bfloat16 [4608, 2048], P(None, 'mp')
- new_master: float32 [4608, 2048], P('dp', 'mp')
- first_unit: float32 [4608, 2048], P('dp', 'mp')
- second_unit: float32 [4608, 2048], P('dp', 'mp')
- first_top: float32 [1152, 4], P('dp', 'mp')
- second_top: float32 [1152, 4], P('dp', 'mp')
All inputs are finite; a program needn't handle non-finite values. Where the computation divides by a largest or mean magnitude, that divisor is 1e-20 or more.
Results may differ from a plain program's by a relative error of at most 0.0004.
Values may be sent and summed in bfloat16 or wider, within the bound.
No kernel may reach another device: no remote copies, remote signals or barrier semaphores. Data moves between devices by JAX's collectives and lax.ppermute only.
A program may use at most 128 MiB of HBM per device.

v0:
```python
import math

import jax
import jax.numpy as jnp
import numpy as np
from jax import lax
from jax.experimental import pallas as pl
from jax.experimental.pallas import tpu as pltpu
from jax.sharding import Mesh
from jax.sharding import PartitionSpec as P

D = 4608
KV = 2048
QROWS = 4
QCOLS = 512
STEP = 10
X, Z, C, Y = "dp_0", "dp_1", "dp_2", "mp"
SIZE = {X: 4, Z: 8, C: 2, Y: 4}
DP = (X, Z, C)

beta_one = 0.9
beta_two = 0.95
learn_rate = 0.002
weight_decay = 0.1
epsilon = 1e-08
clip_rms = 0.25

f32 = jnp.float32


MATES = {
    X: ((1, 0, 3, 2), (3, 2, 1, 0)),
    Z: ((1, 0, 3, 2, 5, 4, 7, 6), (7, 2, 1, 4, 3, 6, 5, 0), (3, 6, 5, 0, 7, 2, 1, 4)),
}


def swap(value):
    return lax.ppermute(value, C, [(0, 1), (1, 0)])


def exchange(value, axis, step):
    n = SIZE[axis]
    mate = MATES[axis][step]
    pairs = [(i * 2 + c, ((mate[(i - c) % n] + c) % n) * 2 + c) for i in range(n) for c in range(2)]
    return lax.ppermute(value, (axis, C), pairs)


def kept_order(axis, node, step):
    if step == len(MATES[axis]):
        return [node]
    return kept_order(axis, node, step + 1) + kept_order(axis, MATES[axis][step][node], step + 1)


def order_of(axis, core):
    n = SIZE[axis]
    table = np.array([[[(d + c) % n for d in kept_order(axis, (i - c) % n, 0)] for c in range(2)] for i in range(n)], np.int32)
    return jnp.asarray(table)[lax.axis_index(axis), core]


def halving_sum(send, keep, axis, first=0):
    for step in range(first, len(MATES[axis])):
        if step > first:
            half = keep.shape[0] // 2
            send, keep = keep[half:], keep[:half]
        keep = keep + exchange(send, axis, step)
    return keep


def doubling_gather(value, axis):
    for step in range(len(MATES[axis]) - 1, -1, -1):
        value = jnp.concatenate([value, exchange(value, axis, step)])
    return value


def packed(mine, theirs, order_x, order_z, keep):
    def kernel(ox, oz, p, q, a, b):
        for i in range(4):
            for j in range(8):
                at = pl.ds(pl.multiple_of((ox[i] * 8 + oz[j]) * 144, 8), 144)
                if (i < 2) == keep:
                    a[i % 2, j] = p[at, :128] + q[at, :128]
                if (j < 4) == keep:
                    b[j % 4, i] = p[at, 128:] + q[at, 128:]

    smem, vmem = pl.BlockSpec(memory_space=pltpu.SMEM), pl.BlockSpec(memory_space=pltpu.VMEM)
    return pl.pallas_call(
        kernel,
        in_specs=[smem, smem, vmem, vmem],
        out_specs=[vmem, vmem],
        out_shape=[jax.ShapeDtypeStruct((2, 8, 144, 128), f32), jax.ShapeDtypeStruct((4, 4, 144, 128), f32)],
        compiler_params=pltpu.CompilerParams(vmem_limit_bytes=40 << 20),
        cost_estimate=pl.CostEstimate(flops=0, bytes_accessed=7 << 20, transcendentals=0),
    )(order_x, order_z, mine, theirs)


def assembled(a, b, other_a, other_b, orders, core):
    def kernel(ox, oz, px, pz, me, a, b, c, d, out, sem):
        copies = []
        mine = pl.multiple_of(me[0] * 256, 128)
        other = pl.multiple_of((1 - me[0]) * 256, 128)
        for source, x_order, z_order, col in ((a, ox, oz, mine), (c, px, pz, other)):
            for i in range(4):
                for j in range(8):
                    copies.append((source.at[i, j], (x_order[i], z_order[j], col)))
        for source, x_order, z_order, col in ((b, ox, oz, mine + 128), (d, px, pz, other + 128)):
            for i in range(4):
                for j in range(8):
                    copies.append((source.at[j, i], (x_order[i], z_order[j], col)))
        started = []
        for n, (source, (xi, zi, col)) in enumerate(copies):
            rows = pl.ds(pl.multiple_of((xi * 8 + zi) * 144, 16), 144)
            copy = pltpu.make_async_copy(source, out.at[rows, pl.ds(pl.multiple_of(col, 128), 128)], sem.at[n])
            copy.start()
            started.append(copy)
        for copy in started:
            copy.wait()

    smem, vmem = pl.BlockSpec(memory_space=pltpu.SMEM), pl.BlockSpec(memory_space=pltpu.VMEM)
    return pl.pallas_call(
        kernel,
        in_specs=[smem] * 5 + [vmem] * 4,
        out_specs=pl.BlockSpec(memory_space=pl.ANY),
        out_shape=jax.ShapeDtypeStruct((D, 512), jnp.bfloat16),
        scratch_shapes=[pltpu.SemaphoreType.DMA((128,))],
        compiler_params=pltpu.CompilerParams(vmem_limit_bytes=24 << 20),
        cost_estimate=pl.CostEstimate(flops=0, bytes_accessed=9 << 20, transcendentals=0),
    )(*orders, core.reshape(1), a, b, other_a, other_b)


def total_over_all(value):
    spread = jnp.broadcast_to(value, (16, 8, 128))
    part = jnp.sum(lax.all_to_all(spread, (Z, C), 0, 0, tiled=True)[:, 0, 0])
    spread = jnp.broadcast_to(part, (16, 8, 128))
    return jnp.sum(lax.all_to_all(spread, (X, Y), 0, 0, tiled=True)[:, 0, 0])


def per_row(scale):
    return jnp.repeat(scale, QROWS, axis=0)


def moments(gradient, factor, first_old, second_old):
    clipped = gradient * factor
    first_new = beta_one * first_old + (1.0 - beta_one) * clipped
    second_new = beta_two * second_old + (1.0 - beta_two) * clipped * clipped
    return first_new, second_new


def stepped(master, first_new, second_new):
    first_hat = first_new / (1.0 - beta_one**STEP)
    second_hat = second_new / (1.0 - beta_two**STEP)
    step_dir = first_hat / (jnp.sqrt(second_hat) + epsilon)
    return master - learn_rate * (step_dir + weight_decay * master)


def shards(inputs, key_cotangent, master, first_codes, second_codes, first_scale, second_scale):
    x, z, c = (lax.axis_index(a) for a in DP)
    contract = (((0,), (0,)), ((), ()))

    def half_of(array, which):
        return lax.dynamic_slice_in_dim(array, which * 256, 256, axis=array.ndim - 1)

    def term(which):
        return lax.dot_general(inputs, half_of(key_cotangent, which), contract, preferred_element_type=f32)

    theirs = swap(term(1 - c))
    mine = lax.optimization_barrier(term(c))
    order_x, order_z = order_of(X, c), order_of(Z, c)

    first_old = first_codes.astype(f32) / 127.0 * per_row(first_scale)
    second_old = second_codes.astype(f32) / 255.0 * per_row(second_scale)
    state = jnp.stack([master, first_old, second_old])
    own = half_of(state, c)
    got = swap(half_of(state, 1 - c))
    both = jnp.concatenate([jnp.where(c == 0, own, got), jnp.where(c == 0, got, own)], axis=1)

    send_a, send_b = packed(mine, theirs, order_x, order_z, False)
    keep_a, keep_b = packed(mine, theirs, order_x, order_z, True)
    over_x = halving_sum(send_a, keep_a, X)[0]
    over_z = halving_sum(send_b, keep_b, Z)[0]
    grad_a = halving_sum(over_x[4:], over_x[:4], Z)[0]
    grad_b = halving_sum(over_z[2:], over_z[:2], X)[0]
    norm_sq = total_over_all(jnp.sum(grad_a * grad_a) + jnp.sum(grad_b * grad_b))
    factor = jnp.minimum(1.0, clip_rms * math.sqrt(D * KV) / (jnp.sqrt(norm_sq) + 1e-06))

    gradient = jnp.concatenate([grad_a, grad_b], axis=1)
    weight = stepped(both[0], *moments(gradient, factor, both[1], both[2])).astype(jnp.bfloat16)

    kept = lax.dynamic_slice_in_dim(gradient, c * 72, 72, axis=0)
    came = swap(lax.dynamic_slice_in_dim(gradient, (1 - c) * 72, 72, axis=0))
    rows = jnp.concatenate([jnp.where(c == 0, kept, came), jnp.where(c == 0, came, kept)], axis=1)
    first_new, second_new = moments(rows, factor, first_old, second_old)
    new_master = stepped(master, first_new, second_new)
    first_top = jnp.max(jnp.abs(first_new).reshape(18, 4, 512), axis=(1, 2))[:, None] + 1e-06
    second_top = jnp.max(second_new.reshape(18, 4, 512), axis=(1, 2))[:, None] + 1e-06
    first_unit = first_new / per_row(first_top)
    second_unit = second_new / per_row(second_top)

    all_a = doubling_gather(doubling_gather(weight[None, :, :128], Z)[None], X)
    all_b = doubling_gather(doubling_gather(weight[None, :, 128:], X)[None], Z)
    orders = (order_x, order_z, order_of(X, 1 - c), order_of(Z, 1 - c))
    out = assembled(all_a, all_b, swap(all_a), swap(all_b), orders, c)
    return (out, new_master, first_unit, second_unit, first_top, second_top)


def solution(mesh):
    finer = Mesh(mesh.devices.reshape(4, 8, 2, mesh.shape["mp"]), (X, Z, C, Y))
    in_specs = (P(DP, None),) + (P(DP, Y),) * 6
    out_specs = (P(None, Y),) + (P(DP, Y),) * 5
    return jax.shard_map(shards, mesh=finer, in_specs=in_specs, out_specs=out_specs, check_vma=False)
```

profile of v0, /device:TPU:1, one launch (start us, length us, event | category | flops | bytes accessed | tf_op | source)
XLA Modules:
  0.0 170.7 jit_solution(12964582420423670970)
XLA Ops:
  0.7 1.1 copy-done
  1.8 8.0 %convolution_bitcast_fusion = f32[4608,256]{1,0:T(8,128)} fusion(bf16[768,4608]{1,0:T(8,128)(2,1)} %param.11, bf16[768,512]{1,0:T(8,128)(2,1)S(1)} %copy-done, s32[]{:T(128)S(6)} %select_n.60), kind=kOutput, calls=%fused_computation | convolution fusion | flops 1811939328 | bytes 12189700 | tf_op jit(solution)/shard_map/dot_general | solution.py:163
  9.8 3.2 %collective-permute-start.1 = (f32[4608,256]{1,0:T(8,128)}, f32[4608,256]{1,0:T(8,128)}, u32[]{:S(2)}, u32[]{:S(2)}) collective-permute-start(f32[4608,256]{1,0:T(8,128)} %convolution_bitcast_fusion), channel_id=1, source_target_pairs={{0,4},{4,0},{1,5},{5,1},{2,6},{6,2},{3,7},{7,3},{8,12},{12,8},{9,1... | collective-permute-start | bytes 14155784 | tf_op jit(solution)/shard_map/ppermute | solution.py:38
  13.0 8.1 %convolution_bitcast_fusion.1.p = f32[4608,256]{1,0:T(8,128)} fusion(bf16[768,4608]{1,0:T(8,128)(2,1)} %param.11, bf16[768,512]{1,0:T(8,128)(2,1)S(1)} %copy-done, s32[]{:T(128)S(6)} %select_n.59), kind=kOutput, calls=%fused_computation.1 | convolution fusion | flops 1811939328 | bytes 12189700 | tf_op jit(solution)/shard_map/dot_general | solution.py:163
  21.1 0.8 fusion.32
  21.9 0.8 fusion.31
  22.6 2.3 %copy-done.1 = f32[4608,256]{1,0:T(8,128)S(1)} copy-done((f32[4608,256]{1,0:T(8,128)S(1)}, f32[4608,256]{1,0:T(8,128)}, u32[]{:S(2)}) %copy-start.1) | copy-done | bytes 4718616
  25.0 2.6 %shard_map.155 = (f32[2,8,144,128]{3,2,1,0:T(8,128)S(1)}, f32[4,4,144,128]{3,2,1,0:T(8,128)S(1)}) custom-call(s32[4]{0:T(128)S(1)} %get-tuple-element.39.ox, s32[8]{0:T(128)S(1)} %get-tuple-element.37.oz, f32[4608,256]{1,0:T(8,128)S(1)} %copy-done.1, f32[4608,256]{1,0:T(8,128)} %collective-permute-done.1.q), custom_call_target="tpu_custom_call" | custom-call | bytes 7340032 | tf_op jit(solution)/shard_map/pallas_call | solution.py:86
  27.6 3.9 %collective-permute-start.7 = (f32[4,4,144,128]{3,2,1,0:T(8,128)S(1)}, f32[4,4,144,128]{3,2,1,0:T(8,128)S(1)}, u32[]{:S(2)}, u32[]{:S(2)}) collective-permute-start(f32[4,4,144,128]{3,2,1,0:T(8,128)S(1)} %get-tuple-element.13), channel_id=1, source_target_pairs={{0,8},{4,60},{8,0},{12,20},{16,24},{20,12},{24,16},{28,36},{32,40}... | collective-permute-start | bytes 3538952 | tf_op jit(solution)/shard_map/ppermute | solution.py:45
  31.5 2.5 %collective-permute-start.2 = (f32[2,8,144,128]{3,2,1,0:T(8,128)S(1)}, f32[2,8,144,128]{3,2,1,0:T(8,128)S(1)}, u32[]{:S(2)}, u32[]{:S(2)}) collective-permute-start(f32[2,8,144,128]{3,2,1,0:T(8,128)S(1)} %get-tuple-element.11), channel_id=1, source_target_pairs={{0,64},{4,196},{64,0},{68,132},{128,192},{132,68},{192,128},{196,4... | collective-permute-start | bytes 3538952 | tf_op jit(solution)/shard_map/ppermute | solution.py:45
  34.0 2.6 %shard_map.154 = (f32[2,8,144,128]{3,2,1,0:T(8,128)S(1)}, f32[4,4,144,128]{3,2,1,0:T(8,128)S(1)}) custom-call(s32[4]{0:T(128)S(1)} %get-tuple-element.39.ox, s32[8]{0:T(128)S(1)} %get-tuple-element.37.oz, f32[4608,256]{1,0:T(8,128)S(1)} %copy-done.1, f32[4608,256]{1,0:T(8,128)} %collective-permute-done.1.q), custom_call_target="tpu_custom_call" | custom-call | bytes 7340032 | tf_op jit(solution)/shard_map/pallas_call | solution.py:86
  36.6 8.5 %collective-permute-done.7 = f32[4,4,144,128]{3,2,1,0:T(8,128)S(1)} collective-permute-done((f32[4,4,144,128]{3,2,1,0:T(8,128)S(1)}, f32[4,4,144,128]{3,2,1,0:T(8,128)S(1)}, u32[]{:S(2)}, u32[]{:S(2)}) %collective-permute-start.7) | collective-permute-done | bytes 1179680 | tf_op jit(solution)/shard_map/ppermute | solution.py:45
  45.1 0.1 add.138
  45.4 2.4 %collective-permute-done.2 = f32[2,8,144,128]{3,2,1,0:T(8,128)S(1)} collective-permute-done((f32[2,8,144,128]{3,2,1,0:T(8,128)S(1)}, f32[2,8,144,128]{3,2,1,0:T(8,128)S(1)}, u32[]{:S(2)}, u32[]{:S(2)}) %collective-permute-start.2) | collective-permute-done | bytes 1179680 | tf_op jit(solution)/shard_map/ppermute | solution.py:45
  47.8 0.1 add.133
  48.1 0.5 copy-done.5
  48.6 5.8 %collective-permute-done.8 = f32[2,4,144,128]{3,2,1,0:T(8,128)S(1)} collective-permute-done((f32[2,4,144,128]{3,2,1,0:T(8,128)S(1)}, f32[2,4,144,128]{3,2,1,0:T(8,128)S(1)}, u32[]{:S(2)}, u32[]{:S(2)}) %collective-permute-start.8) | collective-permute-done | bytes 589856 | tf_op jit(solution)/shard_map/ppermute | solution.py:45
  54.5 2.9 %collective-permute-start.9 = (f32[1,4,144,128]{3,2,1,0:T(8,128)S(1)}, f32[1,4,144,128]{3,2,1,0:T(8,128)S(1)}, u32[]{:S(2)}, u32[]{:S(2)}) collective-permute-start(f32[1,4,144,128]{3,2,1,0:T(8,128)S(1)} %slice.123), channel_id=1, source_target_pairs={{0,24},{4,44},{8,48},{12,36},{16,40},{20,60},{24,0},{28,52},{32,56... | collective-permute-start | bytes 884744 | tf_op jit(solution)/shard_map/ppermute | solution.py:45
  57.6 12.2 %collective-permute-done.9 = f32[1,4,144,128]{3,2,1,0:T(8,128)S(1)} collective-permute-done((f32[1,4,144,128]{3,2,1,0:T(8,128)S(1)}, f32[1,4,144,128]{3,2,1,0:T(8,128)S(1)}, u32[]{:S(2)}, u32[]{:S(2)}) %collective-permute-start.9) | collective-permute-done | bytes 294944 | tf_op jit(solution)/shard_map/ppermute | solution.py:45
  69.8 2.6 %collective-permute-start.10 = (f32[2,144,128]{2,1,0:T(8,128)S(1)}, f32[2,144,128]{2,1,0:T(8,128)S(1)}, u32[]{:S(2)}, u32[]{:S(2)}) collective-permute-start(f32[2,144,128]{2,1,0:T(8,128)S(1)} %slice_bitcast_fusion.2), channel_id=1, source_target_pairs={{0,64},{4,196},{64,0},{68,132},{128,192},{132,68},{192,128},{196,4... | collective-permute-start | bytes 442376 | tf_op jit(solution)/shard_map/ppermute | solution.py:45
  72.5 0.5 collective-permute-start.5
  73.0 2.1 %collective-permute-done.10 = f32[2,144,128]{2,1,0:T(8,128)S(1)} collective-permute-done((f32[2,144,128]{2,1,0:T(8,128)S(1)}, f32[2,144,128]{2,1,0:T(8,128)S(1)}, u32[]{:S(2)}, u32[]{:S(2)}) %collective-permute-start.10) | collective-permute-done | bytes 147488 | tf_op jit(solution)/shard_map/ppermute | solution.py:45
  75.2 0.4 collective-permute-start.11
  75.6 1.2 collective-permute-done.5
  76.8 2.5 %collective-permute-start.6 = (f32[1,144,128]{2,1,0:T(8,128)S(1)}, f32[1,144,128]{2,1,0:T(8,128)S(1)}, u32[]{:S(2)}, u32[]{:S(2)}) collective-permute-start(f32[1,144,128]{2,1,0:T(8,128)S(1)} %slice.119), channel_id=1, source_target_pairs={{0,24},{4,44},{8,48},{12,36},{16,40},{20,60},{24,0},{28,52},{32,56... | collective-permute-start | bytes 221192 | tf_op jit(solution)/shard_map/ppermute | solution.py:45
  79.3 0.6 multiply_reduce_fusion
  79.9 3.1 %collective-permute-done.6 = f32[1,144,128]{2,1,0:T(8,128)S(1)} collective-permute-done((f32[1,144,128]{2,1,0:T(8,128)S(1)}, f32[1,144,128]{2,1,0:T(8,128)S(1)}, u32[]{:S(2)}, u32[]{:S(2)}) %collective-permute-start.6) | collective-permute-done | bytes 73760 | tf_op jit(solution)/shard_map/ppermute | solution.py:45
  83.1 0.6 multiply_reduce_fusion.1
  85.0 0.6 broadcast_in_dim.38
  85.6 10.4 %all-to-all-start = ((f32[16,8,128]{2,1,0:T(8,128)}), f32[16,8,128]{2,1,0:T(8,128)S(1)}, u32[]{:S(2)}, u32[]{:S(2)}) async-start(f32[16,8,128]{2,1,0:T(8,128)} %broadcast_in_dim.38), calls=%async_computation | async-start | bytes 131072 | tf_op jit(solution)/shard_map/all_to_all | solution.py:132
  96.4 0.2 collective-permute-start.24
  96.6 7.2 %all-to-all-done = f32[16,8,128]{2,1,0:T(8,128)S(1)} async-done(((f32[16,8,128]{2,1,0:T(8,128)}), f32[16,8,128]{2,1,0:T(8,128)S(1)}, u32[]{:S(2)}, u32[]{:S(2)}) %all-to-all-start) | async-done | bytes 65568 | tf_op jit(solution)/shard_map/all_to_all | solution.py:132
  103.8 0.6 slice_reduce_fusion.1
  104.5 1.3 broadcast_in_dim.39
  105.7 4.3 %all-to-all-start.1 = ((f32[16,8,128]{2,1,0:T(8,128)}), f32[16,8,128]{2,1,0:T(8,128)S(1)}, u32[]{:S(2)}, u32[]{:S(2)}) async-start(f32[16,8,128]{2,1,0:T(8,128)} %broadcast_in_dim.39), calls=%async_computation.1 | async-start | bytes 131072 | tf_op jit(solution)/shard_map/all_to_all | solution.py:134
  110.1 6.5 %all-to-all-done.1 = f32[16,8,128]{2,1,0:T(8,128)S(1)} async-done(((f32[16,8,128]{2,1,0:T(8,128)}), f32[16,8,128]{2,1,0:T(8,128)S(1)}, u32[]{:S(2)}, u32[]{:S(2)}) %all-to-all-start.1) | async-done | bytes 65568 | tf_op jit(solution)/shard_map/all_to_all | solution.py:134
  116.6 0.6 slice_reduce_fusion
  117.9 0.2 abs_reduce_fusion
  118.2 1.7 collective-permute-start
  119.9 1.1 collective-permute-done
  121.1 0.1 subtract_convert_fusion
  121.2 0.3 collective-permute-start.17
  121.6 0.9 collective-permute-start.12
  122.4 1.7 %collective-permute-done.17 = bf16[1,144,128]{2,1,0:T(8,128)(2,1)S(1)} collective-permute-done((bf16[1,144,128]{2,1,0:T(8,128)(2,1)S(1)}, bf16[1,144,128]{2,1,0:T(8,128)(2,1)S(1)}, u32[]{:S(2)}, u32[]{:S(2)}) %collective-permute-start.17) | collective-permute-done | bytes 36896 | tf_op jit(solution)/shard_map/ppermute | solution.py:45
  124.1 0.9 collective-permute-start.18
  125.1 3.1 %collective-permute-done.12 = bf16[1,144,128]{2,1,0:T(8,128)(2,1)S(1)} collective-permute-done((bf16[1,144,128]{2,1,0:T(8,128)(2,1)S(1)}, bf16[1,144,128]{2,1,0:T(8,128)(2,1)S(1)}, u32[]{:S(2)}, u32[]{:S(2)}) %collective-permute-start.12) | collective-permute-done | bytes 36896 | tf_op jit(solution)/shard_map/ppermute | solution.py:45
  128.3 0.3 collective-permute-done.18
  128.7 2.0 %collective-permute-start.19 = (bf16[1,4,144,128]{3,2,1,0:T(8,128)(2,1)S(1)}, bf16[1,4,144,128]{3,2,1,0:T(8,128)(2,1)S(1)}, u32[]{:S(2)}, u32[]{:S(2)}) collective-permute-start(bf16[1,4,144,128]{3,2,1,0:T(8,128)(2,1)S(1)} %maximum_bitcast_fusion.1), channel_id=1, source_target_pairs={{0,24},{4,44},{8,48},{12,36},{16,40},{20,60},{24,0},{28,52},{32,56... | collective-permute-start | bytes 442376 | tf_op jit(solution)/shard_map/ppermute | solution.py:45
  130.7 0.8 collective-permute-done.13
  131.5 0.5 collective-permute-start.14
  132.0 7.0 %collective-permute-done.19 = bf16[1,4,144,128]{3,2,1,0:T(8,128)(2,1)S(1)} collective-permute-done((bf16[1,4,144,128]{3,2,1,0:T(8,128)(2,1)S(1)}, bf16[1,4,144,128]{3,2,1,0:T(8,128)(2,1)S(1)}, u32[]{:S(2)}, u32[]{:S(2)}) %collective-permute-start.19) | collective-permute-done | bytes 147488 | tf_op jit(solution)/shard_map/ppermute | solution.py:45
  139.2 1.2 collective-permute-start.15
  140.4 4.3 %collective-permute-done.20 = bf16[2,4,144,128]{3,2,1,0:T(8,128)(2,1)S(1)} collective-permute-done((bf16[2,4,144,128]{3,2,1,0:T(8,128)(2,1)S(1)}, bf16[2,4,144,128]{3,2,1,0:T(8,128)(2,1)S(1)}, u32[]{:S(2)}, u32[]{:S(2)}) %collective-permute-start.20) | collective-permute-done | bytes 294944 | tf_op jit(solution)/shard_map/ppermute | solution.py:45
  144.8 1.0 collective-permute-start.21
  145.8 1.2 collective-permute-start.16
  147.0 7.9 %collective-permute-done.21 = bf16[4,4,144,128]{3,2,1,0:T(8,128)(2,1)S(1)} collective-permute-done((bf16[4,4,144,128]{3,2,1,0:T(8,128)(2,1)S(1)}, bf16[4,4,144,128]{3,2,1,0:T(8,128)(2,1)S(1)}, u32[]{:S(2)}, u32[]{:S(2)}) %collective-permute-start.21) | collective-permute-done | bytes 589856 | tf_op jit(solution)/shard_map/ppermute | solution.py:45
  154.9 0.1 pad_maximum_fusion.1.b
  155.1 5.3 %collective-permute-start.23 = (bf16[8,4,144,128]{3,2,1,0:T(8,128)(2,1)S(1)}, bf16[8,4,144,128]{3,2,1,0:T(8,128)(2,1)}, u32[]{:S(2)}, u32[]{:S(2)}) collective-permute-start(bf16[8,4,144,128]{3,2,1,0:T(8,128)(2,1)S(1)} %pad_maximum_fusion.1.b), channel_id=1, source_target_pairs={{0,4},{4,0},{1,5},{5,1},{2,6},{6,2},{3,7},{7,3},{8,12},{12,8},{9,1... | collective-permute-start | bytes 3538952 | tf_op jit(solution)/shard_map/ppermute | solution.py:38
  160.4 0.1 pad_maximum_fusion.a
  160.5 2.0 %collective-permute-start.22 = (bf16[4,8,144,128]{3,2,1,0:T(8,128)(2,1)S(1)}, bf16[4,8,144,128]{3,2,1,0:T(8,128)(2,1)}, u32[]{:S(2)}, u32[]{:S(2)}) collective-permute-start(bf16[4,8,144,128]{3,2,1,0:T(8,128)(2,1)S(1)} %pad_maximum_fusion.a), channel_id=1, source_target_pairs={{0,4},{4,0},{1,5},{5,1},{2,6},{6,2},{3,7},{7,3},{8,12},{12,8},{9,1... | collective-permute-start | bytes 3538952 | tf_op jit(solution)/shard_map/ppermute | solution.py:38
  162.7 0.1 reduce_max.25
  162.9 0.5 fusion.33
  163.8 1.8 %broadcast_divide_fusion = (f32[72,512]{1,0:T(8,128)}, f32[72,512]{1,0:T(8,128)}, f32[72,512]{1,0:T(8,128)}) fusion(f32[72,512]{1,0:T(8,128)S(1)} %get-tuple-element.33, f32[72]{0:T(128)S(1)} %broadcast_in_dim.47, f32[72,512]{1,0:T(8,128)} %param.13, f32[72,512]{1,0:T(8,128)S(1)} %get-tuple-element.17, f32[72]{0:T(128)S(1)} %broadcast_in_dim.45), kind=kLoop, calls=%fused_computation.71 | loop fusion | flops 368640 | bytes 885312 | tf_op jit(solution)/shard_map/div | solution.py:196
  165.6 4.9 %shard_map.156 = bf16[4608,512]{1,0:T(8,128)(2,1)} custom-call(s32[4]{0:T(128)S(1)} %get-tuple-element.39.ox, s32[8]{0:T(128)S(1)} %get-tuple-element.37.oz, s32[4]{0:T(128)S(1)} %get-tuple-element.38.px, s32[8]{0:T(128)S(1)} %get-tuple-element.36.pz, s32[1]{0:T(128)} %bitcast.4.me, bf16[4,8,144,128]{3,2,1,0:T(8,128)(2,1)S(1)} %pad_maximum_fusion.a, ...), custom_call_target="tpu_custom_call" | custom-call | bytes 9437184 | tf_op jit(solution)/shard_map/pallas_call | solution.py:119
  (67 shorter events, 2.2 us)
Async XLA Ops:
  0.6 1.1 copy-start
  9.8 12.8 %collective-permute-start.1 = (f32[4608,256]{1,0:T(8,128)}, f32[4608,256]{1,0:T(8,128)}, u32[]{:S(2)}, u32[]{:S(2)}) collective-permute-start(f32[4608,256]{1,0:T(8,128)} %convolution_bitcast_fusion), channel_id=1, source_target_pairs={{0,4},{4,0},{1,5},{5,1},{2,6},{6,2},{3,7},{7,3},{8,12},{12,8},{9,1... | collective-permute-start | bytes 14155784 | tf_op jit(solution)/shard_map/ppermute | solution.py:38
  22.6 2.3 %copy-start.1 = (f32[4608,256]{1,0:T(8,128)S(1)}, f32[4608,256]{1,0:T(8,128)}, u32[]{:S(2)}) copy-start(f32[4608,256]{1,0:T(8,128)} %convolution_bitcast_fusion.1.p) | copy-start | bytes 14155780
  27.6 17.5 %collective-permute-start.7 = (f32[4,4,144,128]{3,2,1,0:T(8,128)S(1)}, f32[4,4,144,128]{3,2,1,0:T(8,128)S(1)}, u32[]{:S(2)}, u32[]{:S(2)}) collective-permute-start(f32[4,4,144,128]{3,2,1,0:T(8,128)S(1)} %get-tuple-element.13), channel_id=1, source_target_pairs={{0,8},{4,60},{8,0},{12,20},{16,24},{20,12},{24,16},{28,36},{32,40}... | collective-permute-start | bytes 3538952 | tf_op jit(solution)/shard_map/ppermute | solution.py:45
  31.5 16.3 %collective-permute-start.2 = (f32[2,8,144,128]{3,2,1,0:T(8,128)S(1)}, f32[2,8,144,128]{3,2,1,0:T(8,128)S(1)}, u32[]{:S(2)}, u32[]{:S(2)}) collective-permute-start(f32[2,8,144,128]{3,2,1,0:T(8,128)S(1)} %get-tuple-element.11), channel_id=1, source_target_pairs={{0,64},{4,196},{64,0},{68,132},{128,192},{132,68},{192,128},{196,4... | collective-permute-start | bytes 3538952 | tf_op jit(solution)/shard_map/ppermute | solution.py:45
  45.3 9.1 %collective-permute-start.8 = (f32[2,4,144,128]{3,2,1,0:T(8,128)S(1)}, f32[2,4,144,128]{3,2,1,0:T(8,128)S(1)}, u32[]{:S(2)}, u32[]{:S(2)}) collective-permute-start(f32[2,4,144,128]{3,2,1,0:T(8,128)S(1)} %slice.121), channel_id=1, source_target_pairs={{0,56},{4,12},{8,16},{12,4},{16,8},{20,28},{24,32},{28,20},{32,24}... | collective-permute-start | bytes 1769480 | tf_op jit(solution)/shard_map/ppermute | solution.py:45
  47.9 0.7 copy-start.5
  48.0 9.4 %collective-permute-start.3 = (f32[1,8,144,128]{3,2,1,0:T(8,128)S(1)}, f32[1,8,144,128]{3,2,1,0:T(8,128)S(1)}, u32[]{:S(2)}, u32[]{:S(2)}) collective-permute-start(f32[1,8,144,128]{3,2,1,0:T(8,128)S(1)} %slice.113), channel_id=1, source_target_pairs={{0,192},{4,68},{64,128},{68,4},{128,64},{132,196},{192,0},{196,132... | collective-permute-start | bytes 1769480 | tf_op jit(solution)/shard_map/ppermute | solution.py:45
  54.5 15.3 %collective-permute-start.9 = (f32[1,4,144,128]{3,2,1,0:T(8,128)S(1)}, f32[1,4,144,128]{3,2,1,0:T(8,128)S(1)}, u32[]{:S(2)}, u32[]{:S(2)}) collective-permute-start(f32[1,4,144,128]{3,2,1,0:T(8,128)S(1)} %slice.123), channel_id=1, source_target_pairs={{0,24},{4,44},{8,48},{12,36},{16,40},{20,60},{24,0},{28,52},{32,56... | collective-permute-start | bytes 884744 | tf_op jit(solution)/shard_map/ppermute | solution.py:45
  57.5 14.9 %collective-permute-start.4 = (f32[4,144,128]{2,1,0:T(8,128)S(1)}, f32[4,144,128]{2,1,0:T(8,128)S(1)}, u32[]{:S(2)}, u32[]{:S(2)}) collective-permute-start(f32[4,144,128]{2,1,0:T(8,128)S(1)} %slice_bitcast_fusion), channel_id=1, source_target_pairs={{0,8},{4,60},{8,0},{12,20},{16,24},{20,12},{24,16},{28,36},{32,40}... | collective-permute-start | bytes 884744 | tf_op jit(solution)/shard_map/ppermute | solution.py:45
  69.8 5.3 %collective-permute-start.10 = (f32[2,144,128]{2,1,0:T(8,128)S(1)}, f32[2,144,128]{2,1,0:T(8,128)S(1)}, u32[]{:S(2)}, u32[]{:S(2)}) collective-permute-start(f32[2,144,128]{2,1,0:T(8,128)S(1)} %slice_bitcast_fusion.2), channel_id=1, source_target_pairs={{0,64},{4,196},{64,0},{68,132},{128,192},{132,68},{192,128},{196,4... | collective-permute-start | bytes 442376 | tf_op jit(solution)/shard_map/ppermute | solution.py:45
  72.4 23.6 %copy-start.6 = (f32[18,1]{0,1:T(1,128)S(1)}, f32[18,1]{0,1:T(1,128)}, u32[]{:S(2)}) copy-start(f32[18,1]{0,1:T(1,128)} %param.17) | copy-start | bytes 220
  72.5 4.3 %collective-permute-start.5 = (f32[2,144,128]{2,1,0:T(8,128)S(1)}, f32[2,144,128]{2,1,0:T(8,128)S(1)}, u32[]{:S(2)}, u32[]{:S(2)}) collective-permute-start(f32[2,144,128]{2,1,0:T(8,128)S(1)} %slice.117), channel_id=1, source_target_pairs={{0,56},{4,12},{8,16},{12,4},{16,8},{20,28},{24,32},{28,20},{32,24}... | collective-permute-start | bytes 442376 | tf_op jit(solution)/shard_map/ppermute | solution.py:45
  75.1 42.8 %copy-start.3 = (s32[72,512]{1,0:T(8,128)S(1)}, s32[72,512]{1,0:T(8,128)}, u32[]{:S(2)}) copy-start(s32[72,512]{1,0:T(8,128)} %param.14) | copy-start | bytes 442372
  75.2 42.8 %copy-start.4 = (s32[72,512]{1,0:T(8,128)S(1)}, s32[72,512]{1,0:T(8,128)}, u32[]{:S(2)}) copy-start(s32[72,512]{1,0:T(8,128)} %param.15) | copy-start | bytes 442372
  75.2 4.1 %collective-permute-start.11 = (f32[1,144,128]{2,1,0:T(8,128)S(1)}, f32[1,144,128]{2,1,0:T(8,128)S(1)}, u32[]{:S(2)}, u32[]{:S(2)}) collective-permute-start(f32[1,144,128]{2,1,0:T(8,128)S(1)} %slice.127), channel_id=1, source_target_pairs={{0,192},{4,68},{64,128},{68,4},{128,64},{132,196},{192,0},{196,132... | collective-permute-start | bytes 221192 | tf_op jit(solution)/shard_map/ppermute | solution.py:45
  76.8 6.3 %collective-permute-start.6 = (f32[1,144,128]{2,1,0:T(8,128)S(1)}, f32[1,144,128]{2,1,0:T(8,128)S(1)}, u32[]{:S(2)}, u32[]{:S(2)}) collective-permute-start(f32[1,144,128]{2,1,0:T(8,128)S(1)} %slice.119), channel_id=1, source_target_pairs={{0,24},{4,44},{8,48},{12,36},{16,40},{20,60},{24,0},{28,52},{32,56... | collective-permute-start | bytes 221192 | tf_op jit(solution)/shard_map/ppermute | solution.py:45
  79.9 38.2 %copy-start.2 = (f32[72,512]{1,0:T(8,128)S(1)}, f32[72,512]{1,0:T(8,128)}, u32[]{:S(2)}) copy-start(f32[72,512]{1,0:T(8,128)} %param.13) | copy-start | bytes 442372
  85.6 18.2 %all-to-all-start = ((f32[16,8,128]{2,1,0:T(8,128)}), f32[16,8,128]{2,1,0:T(8,128)S(1)}, u32[]{:S(2)}, u32[]{:S(2)}) async-start(f32[16,8,128]{2,1,0:T(8,128)} %broadcast_in_dim.38), calls=%async_computation | async-start | bytes 131072 | tf_op jit(solution)/shard_map/all_to_all | solution.py:132
  96.4 13.6 %collective-permute-start.24 = (f32[72,256]{1,0:T(8,128)S(1)}, f32[72,256]{1,0:T(8,128)S(1)}, u32[]{:S(2)}, u32[]{:S(2)}) collective-permute-start(f32[72,256]{1,0:T(8,128)S(1)} %fusion.24), channel_id=1, source_target_pairs={{0,4},{4,0},{1,5},{5,1},{2,6},{6,2},{3,7},{7,3},{8,12},{12,8},{9,1... | collective-permute-start | bytes 221192 | tf_op jit(solution)/shard_map/ppermute | solution.py:38
  105.7 10.8 %all-to-all-start.1 = ((f32[16,8,128]{2,1,0:T(8,128)}), f32[16,8,128]{2,1,0:T(8,128)S(1)}, u32[]{:S(2)}, u32[]{:S(2)}) async-start(f32[16,8,128]{2,1,0:T(8,128)} %broadcast_in_dim.39), calls=%async_computation.1 | async-start | bytes 131072 | tf_op jit(solution)/shard_map/all_to_all | solution.py:134
  118.2 2.8 %collective-permute-start = (f32[3,72,256]{2,1,0:T(8,128)S(1)}, f32[3,72,256]{2,1,0:T(8,128)S(1)}, u32[]{:S(2)}, u32[]{:S(2)}) collective-permute-start(f32[3,72,256]{2,1,0:T(8,128)S(1)} %constant_dynamic-slice_fusion), channel_id=1, source_target_pairs={{0,4},{4,0},{1,5},{5,1},{2,6},{6,2},{3,7},{7,3},{8,12},{12,8},{9,1... | collective-permute-start | bytes 663560 | tf_op jit(solution)/shard_map/ppermute | solution.py:38
  121.2 2.9 %collective-permute-start.17 = (bf16[1,144,128]{2,1,0:T(8,128)(2,1)S(1)}, bf16[1,144,128]{2,1,0:T(8,128)(2,1)S(1)}, u32[]{:S(2)}, u32[]{:S(2)}) collective-permute-start(bf16[1,144,128]{2,1,0:T(8,128)(2,1)S(1)} %get-tuple-element.34), channel_id=1, source_target_pairs={{0,192},{4,68},{64,128},{68,4},{128,64},{132,196},{192,0},{196,132... | collective-permute-start | bytes 110600 | tf_op jit(solution)/shard_map/ppermute | solution.py:45
  121.6 6.6 %collective-permute-start.12 = (bf16[1,144,128]{2,1,0:T(8,128)(2,1)S(1)}, bf16[1,144,128]{2,1,0:T(8,128)(2,1)S(1)}, u32[]{:S(2)}, u32[]{:S(2)}) collective-permute-start(bf16[1,144,128]{2,1,0:T(8,128)(2,1)S(1)} %get-tuple-element.35), channel_id=1, source_target_pairs={{0,24},{4,44},{8,48},{12,36},{16,40},{20,60},{24,0},{28,52},{32,56... | collective-permute-start | bytes 110600 | tf_op jit(solution)/shard_map/ppermute | solution.py:45
  124.1 4.5 %collective-permute-start.18 = (bf16[2,144,128]{2,1,0:T(8,128)(2,1)S(1)}, bf16[2,144,128]{2,1,0:T(8,128)(2,1)S(1)}, u32[]{:S(2)}, u32[]{:S(2)}) collective-permute-start(bf16[2,144,128]{2,1,0:T(8,128)(2,1)S(1)} %pad_maximum_fusion.10), channel_id=1, source_target_pairs={{0,64},{4,196},{64,0},{68,132},{128,192},{132,68},{192,128},{196,4... | collective-permute-start | bytes 221192 | tf_op jit(solution)/shard_map/ppermute | solution.py:45
  128.2 3.3 %collective-permute-start.13 = (bf16[2,144,128]{2,1,0:T(8,128)(2,1)S(1)}, bf16[2,144,128]{2,1,0:T(8,128)(2,1)S(1)}, u32[]{:S(2)}, u32[]{:S(2)}) collective-permute-start(bf16[2,144,128]{2,1,0:T(8,128)(2,1)S(1)} %pad_maximum_fusion.9), channel_id=1, source_target_pairs={{0,56},{4,12},{8,16},{12,4},{16,8},{20,28},{24,32},{28,20},{32,24}... | collective-permute-start | bytes 221192 | tf_op jit(solution)/shard_map/ppermute | solution.py:45
  128.7 10.3 %collective-permute-start.19 = (bf16[1,4,144,128]{3,2,1,0:T(8,128)(2,1)S(1)}, bf16[1,4,144,128]{3,2,1,0:T(8,128)(2,1)S(1)}, u32[]{:S(2)}, u32[]{:S(2)}) collective-permute-start(bf16[1,4,144,128]{3,2,1,0:T(8,128)(2,1)S(1)} %maximum_bitcast_fusion.1), channel_id=1, source_target_pairs={{0,24},{4,44},{8,48},{12,36},{16,40},{20,60},{24,0},{28,52},{32,56... | collective-permute-start | bytes 442376 | tf_op jit(solution)/shard_map/ppermute | solution.py:45
  131.5 7.6 %collective-permute-start.14 = (bf16[4,144,128]{2,1,0:T(8,128)(2,1)S(1)}, bf16[4,144,128]{2,1,0:T(8,128)(2,1)S(1)}, u32[]{:S(2)}, u32[]{:S(2)}) collective-permute-start(bf16[4,144,128]{2,1,0:T(8,128)(2,1)S(1)} %pad_maximum_fusion.8), channel_id=1, source_target_pairs={{0,8},{4,60},{8,0},{12,20},{16,24},{20,12},{24,16},{28,36},{32,40}... | collective-permute-start | bytes 442376 | tf_op jit(solution)/shard_map/ppermute | solution.py:45
  139.0 5.7 %collective-permute-start.20 = (bf16[2,4,144,128]{3,2,1,0:T(8,128)(2,1)S(1)}, bf16[2,4,144,128]{3,2,1,0:T(8,128)(2,1)S(1)}, u32[]{:S(2)}, u32[]{:S(2)}) collective-permute-start(bf16[2,4,144,128]{3,2,1,0:T(8,128)(2,1)S(1)} %pad_maximum_fusion.5), channel_id=1, source_target_pairs={{0,56},{4,12},{8,16},{12,4},{16,8},{20,28},{24,32},{28,20},{32,24}... | collective-permute-start | bytes 884744 | tf_op jit(solution)/shard_map/ppermute | solution.py:45
  139.2 6.5 %collective-permute-start.15 = (bf16[1,8,144,128]{3,2,1,0:T(8,128)(2,1)S(1)}, bf16[1,8,144,128]{3,2,1,0:T(8,128)(2,1)S(1)}, u32[]{:S(2)}, u32[]{:S(2)}) collective-permute-start(bf16[1,8,144,128]{3,2,1,0:T(8,128)(2,1)S(1)} %maximum_bitcast_fusion), channel_id=1, source_target_pairs={{0,192},{4,68},{64,128},{68,4},{128,64},{132,196},{192,0},{196,132... | collective-permute-start | bytes 884744 | tf_op jit(solution)/shard_map/ppermute | solution.py:45
  144.8 10.2 %collective-permute-start.21 = (bf16[4,4,144,128]{3,2,1,0:T(8,128)(2,1)S(1)}, bf16[4,4,144,128]{3,2,1,0:T(8,128)(2,1)S(1)}, u32[]{:S(2)}, u32[]{:S(2)}) collective-permute-start(bf16[4,4,144,128]{3,2,1,0:T(8,128)(2,1)S(1)} %pad_maximum_fusion.3), channel_id=1, source_target_pairs={{0,8},{4,60},{8,0},{12,20},{16,24},{20,12},{24,16},{28,36},{32,40}... | collective-permute-start | bytes 1769480 | tf_op jit(solution)/shard_map/ppermute | solution.py:45
  145.8 14.6 %collective-permute-start.16 = (bf16[2,8,144,128]{3,2,1,0:T(8,128)(2,1)S(1)}, bf16[2,8,144,128]{3,2,1,0:T(8,128)(2,1)S(1)}, u32[]{:S(2)}, u32[]{:S(2)}) collective-permute-start(bf16[2,8,144,128]{3,2,1,0:T(8,128)(2,1)S(1)} %pad_maximum_fusion.2), channel_id=1, source_target_pairs={{0,64},{4,196},{64,0},{68,132},{128,192},{132,68},{192,128},{196,4... | collective-permute-start | bytes 1769480 | tf_op jit(solution)/shard_map/ppermute | solution.py:45
  155.1 10.5 %collective-permute-start.23 = (bf16[8,4,144,128]{3,2,1,0:T(8,128)(2,1)S(1)}, bf16[8,4,144,128]{3,2,1,0:T(8,128)(2,1)}, u32[]{:S(2)}, u32[]{:S(2)}) collective-permute-start(bf16[8,4,144,128]{3,2,1,0:T(8,128)(2,1)S(1)} %pad_maximum_fusion.1.b), channel_id=1, source_target_pairs={{0,4},{4,0},{1,5},{5,1},{2,6},{6,2},{3,7},{7,3},{8,12},{12,8},{9,1... | collective-permute-start | bytes 3538952 | tf_op jit(solution)/shard_map/ppermute | solution.py:38
  160.5 5.1 %collective-permute-start.22 = (bf16[4,8,144,128]{3,2,1,0:T(8,128)(2,1)S(1)}, bf16[4,8,144,128]{3,2,1,0:T(8,128)(2,1)}, u32[]{:S(2)}, u32[]{:S(2)}) collective-permute-start(bf16[4,8,144,128]{3,2,1,0:T(8,128)(2,1)S(1)} %pad_maximum_fusion.a), channel_id=1, source_target_pairs={{0,4},{4,0},{1,5},{5,1},{2,6},{6,2},{3,7},{7,3},{8,12},{12,8},{9,1... | collective-permute-start | bytes 3538952 | tf_op jit(solution)/shard_map/ppermute | solution.py:38
where the time goes:
time: 171 us
  waiting for transfers between devices  75.4 us (44%)
  starting transfers between devices  50.9 us (30%)
  matrix products  16.1 us (9%)
  Pallas kernels  10.2 us (6%)
  local copies, waits for them, and re-layouts  8.42 us (5%)
  other arithmetic  6.41 us (4%)
  between operations  3.23 us (2%)
    ppermute x20, waiting for transfers between devices, exchange(): return lax.ppermute(value, (axis, C), pairs)  60.6 us
    ppermute x20, starting transfers between devices, exchange(): return lax.ppermute(value, (axis, C), pairs)  23.8 us
    dot_general x2, matrix products, term(): lax.dot_general(inputs, half_of(key_cotangent, which), contract, preferre...  16.1 us
    ppermute x5, starting transfers between devices, swap(): return lax.ppermute(value, C, [(0, 1), (1, 0)])  12.5 us
    all_to_all x1, starting transfers between devices, total_over_all(): part = jnp.sum(lax.all_to_all(spread, (Z, C), 0, 0, tiled=True)[:, 0, 0])  10.4 us
    all_to_all x1, waiting for transfers between devices, total_over_all(): part = jnp.sum(lax.all_to_all(spread, (Z, C), 0, 0, tiled=True)[:, 0, 0])  7.24 us
    all_to_all x1, waiting for transfers between devices, total_over_all(): return jnp.sum(lax.all_to_all(spread, (X, Y), 0, 0, tiled=True)[:, 0, 0])  6.48 us
    pallas_call x2, Pallas kernels, packed(): pl.pallas_call(kernel, in_specs=[smem, smem, vmem, vmem], out_specs=[vmem...  5.24 us
  transfers between devices with their start and end apart: 27, of which 17 were waited for; matrix products, arithmetic and copies ran while one was open for 10% of the time, Pallas kernels for 2%

commit v1 on v0

v1 whole, which is shorter than its diff:
```python
import math

import jax
import jax.numpy as jnp
import numpy as np
from jax import lax
from jax.experimental import pallas as pl
from jax.experimental.pallas import tpu as pltpu
from jax.sharding import Mesh
from jax.sharding import PartitionSpec as P

D = 4608
KV = 2048
QROWS = 4
QCOLS = 512
STEP = 10
X, Z, C, Y = "dp_0", "dp_1", "dp_2", "mp"
SIZE = {X: 4, Z: 8, C: 2, Y: 4}
DP = (X, Z, C)

beta_one = 0.9
beta_two = 0.95
learn_rate = 0.002
weight_decay = 0.1
epsilon = 1e-08
clip_rms = 0.25

f32 = jnp.float32


MATES = {
    X: ((1, 0, 3, 2), (3, 2, 1, 0)),
    Z: ((1, 0, 3, 2, 5, 4, 7, 6), (7, 2, 1, 4, 3, 6, 5, 0), (3, 6, 5, 0, 7, 2, 1, 4)),
}


def swap(value):
    return lax.ppermute(value, C, [(0, 1), (1, 0)])


def exchange(value, axis, step):
    n = SIZE[axis]
    mate = MATES[axis][step]
    pairs = [(i * 2 + c, ((mate[(i - c) % n] + c) % n) * 2 + c) for i in range(n) for c in range(2)]
    return lax.ppermute(value, (axis, C), pairs)


def kept_order(axis, node, step):
    if step == len(MATES[axis]):
        return [node]
    return kept_order(axis, node, step + 1) + kept_order(axis, MATES[axis][step][node], step + 1)


def order_of(axis, core):
    n = SIZE[axis]
    table = np.array([[[(d + c) % n for d in kept_order(axis, (i - c) % n, 0)] for c in range(2)] for i in range(n)], np.int32)
    return jnp.asarray(table)[lax.axis_index(axis), core]


def sent_half(send, axis, step, terms):
    return exchange((send * (1.0 / terms)).astype(jnp.float16), axis, step).astype(f32) * float(terms)


def halving_sum(send, keep, axis, terms):
    for step in range(len(MATES[axis])):
        if step:
            half = keep.shape[0] // 2
            send, keep = keep[half:], keep[:half]
        keep = keep + sent_half(send, axis, step, terms)
        terms *= 2
    return keep[0]


def doubling_gather(value, axis, last=0):
    for step in range(len(MATES[axis]) - 1, last - 1, -1):
        value = jnp.concatenate([value, exchange(value, axis, step)])
    return value


def products(inputs, key_cotangent, core, h):
    width = 1152

    def kernel(me, a, b, theirs, mine, buf, sem):
        copies = [pltpu.make_async_copy(a.at[:, pl.ds(h * 2304 + i * width, width)], buf.at[i], sem.at[i]) for i in (0, 1)]
        for copy in copies:
            copy.start()
        for i in (0, 1):
            copies[i].wait()
            term = lax.dot_general(buf[i], b[...], (((0,), (0,)), ((), ())), preferred_element_type=f32)
            at = pl.ds(i * width, width)
            for c, left, right in ((0, mine, theirs), (1, theirs, mine)):

                @pl.when(me[0] == c)
                def _(left=left, right=right):
                    left[at, :] = term[:, :256]
                    right[at, :] = term[:, 256:]

    smem, vmem = pl.BlockSpec(memory_space=pltpu.SMEM), pl.BlockSpec(memory_space=pltpu.VMEM)
    return pl.pallas_call(
        kernel,
        in_specs=[smem, pl.BlockSpec(memory_space=pl.ANY), vmem],
        out_specs=[vmem, vmem],
        out_shape=[jax.ShapeDtypeStruct((2304, 256), f32)] * 2,
        scratch_shapes=[pltpu.VMEM((2, 768, width), jnp.bfloat16), pltpu.SemaphoreType.DMA((2,))],
        compiler_params=pltpu.CompilerParams(vmem_limit_bytes=24 << 20),
        cost_estimate=pl.CostEstimate(flops=2 * 768 * 2304 * 512, bytes_accessed=9 << 20, transcendentals=0),
    )(core.reshape(1), inputs, key_cotangent)


def packed(mine, theirs, order_x, order_z, keep):
    def kernel(ox, oz, p0, p1, q0, q1, a, b):
        for i in range(4):
            for h, p, q in ((0, p0, q0), (1, p1, q1)):

                @pl.when(ox[i] // 2 == h)
                def _(i=i, h=h, p=p, q=q):
                    for j in range(8):
                        at = pl.ds(pl.multiple_of((ox[i] * 8 - h * 16 + oz[j]) * 144, 8), 144)
                        if (i < 2) == keep:
                            a[i % 2, j] = p[at, :128] + q[at, :128]
                        if (j < 4) == keep:
                            b[j % 4, i] = p[at, 128:] + q[at, 128:]

    smem, vmem = pl.BlockSpec(memory_space=pltpu.SMEM), pl.BlockSpec(memory_space=pltpu.VMEM)
    return pl.pallas_call(
        kernel,
        in_specs=[smem, smem] + [vmem] * 4,
        out_specs=[vmem, vmem],
        out_shape=[jax.ShapeDtypeStruct((2, 8, 144, 128), f32), jax.ShapeDtypeStruct((4, 4, 144, 128), f32)],
        compiler_params=pltpu.CompilerParams(vmem_limit_bytes=16 << 20),
        cost_estimate=pl.CostEstimate(flops=0, bytes_accessed=7 << 20, transcendentals=0),
    )(order_x, order_z, *mine, *theirs)


def written(out, pieces, orders, core, part):
    x_from, z_from = 2 * part, 4 * part

    def kernel(ox, oz, px, pz, me, a, b, c, d, *rest):
        out, sem = rest[-2:]
        mine = pl.multiple_of(me[0] * 256, 128)
        other = pl.multiple_of((1 - me[0]) * 256, 128)
        copies = []
        for source, x_order, z_order, col in ((a, ox, oz, mine), (c, px, pz, other)):
            copies += [(source.at[i, j], x_order[x_from + i], z_order[j], col) for i in range(2) for j in range(8)]
        for source, x_order, z_order, col in ((b, ox, oz, mine + 128), (d, px, pz, other + 128)):
            copies += [(source.at[j, i], x_order[i], z_order[z_from + j], col) for i in range(4) for j in range(4)]
        started = []
        for n, (source, xi, zi, col) in enumerate(copies):
            rows = pl.ds(pl.multiple_of((xi * 8 + zi) * 144, 16), 144)
            copy = pltpu.make_async_copy(source, out.at[rows, pl.ds(pl.multiple_of(col, 128), 128)], sem.at[n])
            copy.start()
            started.append(copy)
        for copy in started:
            copy.wait()

    smem, vmem = pl.BlockSpec(memory_space=pltpu.SMEM), pl.BlockSpec(memory_space=pltpu.VMEM)
    anywhere = pl.BlockSpec(memory_space=pl.ANY)
    held = [] if out is None else [out]
    return pl.pallas_call(
        kernel,
        in_specs=[smem] * 5 + [vmem] * 4 + [anywhere] * len(held),
        out_specs=anywhere,
        out_shape=jax.ShapeDtypeStruct((D, 512), jnp.bfloat16),
        scratch_shapes=[pltpu.SemaphoreType.DMA((64,))],
        input_output_aliases={9: 0} if held else {},
        compiler_params=pltpu.CompilerParams(vmem_limit_bytes=8 << 20),
        cost_estimate=pl.CostEstimate(flops=0, bytes_accessed=9 << 20, transcendentals=0),
    )(*orders, core.reshape(1), *pieces, *held)


def total_over_all(value):
    spread = jnp.broadcast_to(value, (16, 8, 128))
    part = jnp.sum(lax.all_to_all(spread, (Z, C), 0, 0, tiled=True)[:, 0, 0])
    spread = jnp.broadcast_to(part, (16, 8, 128))
    return jnp.sum(lax.all_to_all(spread, (X, Y), 0, 0, tiled=True)[:, 0, 0])


def per_row(scale):
    return jnp.repeat(scale, QROWS, axis=0)


def moments(gradient, factor, first_old, second_old):
    clipped = gradient * factor
    first_new = beta_one * first_old + (1.0 - beta_one) * clipped
    second_new = beta_two * second_old + (1.0 - beta_two) * clipped * clipped
    return first_new, second_new


def stepped(master, first_new, second_new):
    first_hat = first_new / (1.0 - beta_one**STEP)
    second_hat = second_new / (1.0 - beta_two**STEP)
    step_dir = first_hat / (jnp.sqrt(second_hat) + epsilon)
    return master - learn_rate * (step_dir + weight_decay * master)


def weights_of(grad_a, grad_b, both, factor):
    def kernel(f, a, b, state, wa, wb):
        for grad, out, col in ((a, wa, 0), (b, wb, 128)):
            at = pl.ds(col, 128)
            news = moments(grad[...], f[0], state[1, :, at], state[2, :, at])
            out[...] = stepped(state[0, :, at], *news).astype(jnp.bfloat16)

    smem, vmem = pl.BlockSpec(memory_space=pltpu.SMEM), pl.BlockSpec(memory_space=pltpu.VMEM)
    return pl.pallas_call(
        kernel,
        in_specs=[smem] + [vmem] * 3,
        out_specs=[vmem, vmem],
        out_shape=[jax.ShapeDtypeStruct((144, 128), jnp.bfloat16)] * 2,
        compiler_params=pltpu.CompilerParams(vmem_limit_bytes=4 << 20),
        cost_estimate=pl.CostEstimate(flops=144 * 256 * 30, bytes_accessed=1 << 20, transcendentals=144 * 256),
    )(factor.reshape(1), grad_a, grad_b, both)


def own_results(left, right, state, factor):
    def largest(rows):
        top = jnp.broadcast_to(jnp.max(rows, axis=1, keepdims=True), (72, 128))
        at = lax.broadcasted_iota(jnp.int32, (72, 128), 0)
        top = jnp.maximum(top, jnp.where(at % 2 == 0, pltpu.roll(top, 71, 0), pltpu.roll(top, 1, 0)))
        return jnp.maximum(top, jnp.where(at % 4 < 2, pltpu.roll(top, 70, 0), pltpu.roll(top, 2, 0))) + 1e-06

    def kernel(f, l, r, state, master, first_unit, second_unit, first_top, second_top):
        gradient = jnp.concatenate([l[...], r[...]], axis=1)
        first_new, second_new = moments(gradient, f[0], state[1], state[2])
        master[...] = stepped(state[0], first_new, second_new)
        for new, unit, top in ((first_new, first_unit, first_top), (second_new, second_unit, second_top)):
            rows = largest(jnp.abs(new))
            top[...] = rows
            unit[...] = new / rows[:, :1]

    smem, vmem = pl.BlockSpec(memory_space=pltpu.SMEM), pl.BlockSpec(memory_space=pltpu.VMEM)
    return pl.pallas_call(
        kernel,
        in_specs=[smem] + [vmem] * 3,
        out_specs=[vmem] * 5,
        out_shape=[jax.ShapeDtypeStruct((72, 512), f32)] * 3 + [jax.ShapeDtypeStruct((72, 128), f32)] * 2,
        compiler_params=pltpu.CompilerParams(vmem_limit_bytes=8 << 20),
        cost_estimate=pl.CostEstimate(flops=72 * 512 * 40, bytes_accessed=1 << 20, transcendentals=72 * 512),
    )(factor.reshape(1), left, right, state)


def shards(inputs, key_cotangent, master, first_codes, second_codes, first_scale, second_scale):
    x, z, c = (lax.axis_index(a) for a in DP)
    order_x, order_z = order_of(X, c), order_of(Z, c)
    orders = (order_x, order_z, order_of(X, 1 - c), order_of(Z, 1 - c))

    terms = [products(inputs, key_cotangent, c, h) for h in (0, 1)]
    theirs = [swap(t) for t, _ in terms]
    mine = [m for _, m in terms]
    send_a, send_b = packed(mine, theirs, order_x, order_z, False)
    keep_a, keep_b = packed(mine, theirs, order_x, order_z, True)

    states = (master, first_codes, second_codes, first_scale, second_scale)
    keep_a, states = lax.optimization_barrier((keep_a, states))
    master, first_codes, second_codes, first_scale, second_scale = states
    first_old = first_codes.astype(f32) / 127.0 * per_row(first_scale)
    second_old = second_codes.astype(f32) / 255.0 * per_row(second_scale)
    state = jnp.stack([master, first_old, second_old])
    own = lax.dynamic_slice_in_dim(state, c * 256, 256, axis=2)
    got = swap(lax.dynamic_slice_in_dim(state, (1 - c) * 256, 256, axis=2))
    both = jnp.concatenate([jnp.where(c == 0, own, got), jnp.where(c == 0, got, own)], axis=1)

    over_x = halving_sum(send_a, keep_a, X, 2)
    over_z = halving_sum(send_b, keep_b, Z, 2)
    over_z, both = lax.optimization_barrier((over_z, both))
    grad_a = halving_sum(over_x[4:], over_x[:4], Z, 8)
    grad_b = halving_sum(over_z[2:], over_z[:2], X, 16)
    norm_sq = total_over_all(jnp.sum(grad_a * grad_a) + jnp.sum(grad_b * grad_b))
    factor = jnp.minimum(1.0, clip_rms * math.sqrt(D * KV) / (jnp.sqrt(norm_sq) + 1e-06))

    weight_a, weight_b = weights_of(grad_a, grad_b, both, factor)
    small_a, small_b = doubling_gather(weight_a[None], Z), doubling_gather(weight_b[None], X)

    gradient = jnp.concatenate([grad_a, grad_b], axis=1)
    kept = lax.dynamic_slice_in_dim(gradient, c * 72, 72, axis=0)
    came = swap(lax.dynamic_slice_in_dim(gradient, (1 - c) * 72, 72, axis=0))
    small_b, factor = lax.optimization_barrier((small_b, factor))
    left, right = jnp.where(c == 0, kept, came), jnp.where(c == 0, came, kept)
    new_master, first_unit, second_unit, first_top, second_top = own_results(left, right, state, factor)
    results = (new_master, first_unit, second_unit, first_top[::4, :1], second_top[::4, :1])

    near_a = doubling_gather(small_a[None], X, 1)
    near_b = doubling_gather(small_b[None], Z, 1)
    far_a, far_b = exchange(near_a, X, 0), exchange(near_b, Z, 0)
    near = (near_a, near_b, swap(near_a), swap(near_b))
    near, results = lax.optimization_barrier((near, results))
    out = written(None, near, orders, c, 0)
    out = written(out, (far_a, far_b, swap(far_a), swap(far_b)), orders, c, 1)
    return (out, *results)


def solution(mesh):
    finer = Mesh(mesh.devices.reshape(4, 8, 2, mesh.shape["mp"]), (X, Z, C, Y))
    in_specs = (P(DP, None),) + (P(DP, Y),) * 6
    out_specs = (P(None, Y),) + (P(DP, Y),) * 5
    return jax.shard_map(shards, mesh=finer, in_specs=in_specs, out_specs=out_specs, check_vma=False)
```

time: 171 us -> 160 us (0.936)
  waiting for transfers between devices: 75.4 us -> 45 us
  blocking collectives: 0 us -> 28.3 us
  matrix products: 16.1 us -> 0 us
  Pallas kernels: 10.2 us -> 21.9 us
  starting transfers between devices: 50.9 us -> 42.7 us
  local copies, waits for them, and re-layouts: 8.42 us -> 12.1 us
    all_to_all x0 -> x2, blocking collectives: none -> 28.3 us  [the longest x1 16.6 us: total_over_all(): part = jnp.sum(lax.all_to_all(spread, (Z, C), 0, 0, tiled=True)[:, 0, 0])]
    ppermute x20, waiting for transfers between devices: 60.6 us -> 40 us  [exchange(): return lax.ppermute(value, (axis, C), pairs)]
    dot_general x2 -> x0, matrix products: 16.1 us -> none  [term(): lax.dot_general(inputs, half_of(key_cotangent, which), contract, preferre...]
    all_to_all x2 -> x0, starting transfers between devices: 14.7 us -> none  [the longest x1 10.4 us: total_over_all(): part = jnp.sum(lax.all_to_all(spread, (Z, C), 0, 0, tiled=True)[:, 0, 0])]
    all_to_all x2 -> x0, waiting for transfers between devices: 13.7 us -> none  [the longest x1 7.24 us: total_over_all(): part = jnp.sum(lax.all_to_all(spread, (Z, C), 0, 0, tiled=True)[:, 0, 0])]
    pallas_call x3 -> x8, Pallas kernels: 10.2 us -> 21.9 us  [the longest x2 8.52 us: products(): pl.pallas_call(kernel, in_specs=[smem, pl.BlockSpec(memory_space=pl.ANY),...]
    ppermute x5 -> x8, starting transfers between devices: 12.5 us -> 20 us  [swap(): return lax.ppermute(value, C, [(0, 1), (1, 0)])]
    unnamed x14 -> x28, local copies, waits for them, and re-layouts: 3.99 us -> 9.53 us
  transfers between devices with their start and end apart: 27 -> 28, of which waited for: 17 -> 16; matrix products, arithmetic and copies ran while one was open for 10% -> 5% of each run, Pallas kernels for 2% -> 5%
where the time goes in v1:
time: 160 us
  waiting for transfers between devices  45 us (28%)
  starting transfers between devices  42.7 us (27%)
  blocking collectives  28.3 us (18%)
  Pallas kernels  21.9 us (14%)
  local copies, waits for them, and re-layouts  12.1 us (8%)
  other arithmetic  6.65 us (4%)
  between operations  3.31 us (2%)
    ppermute x20, waiting for transfers between devices, exchange(): return lax.ppermute(value, (axis, C), pairs)  40 us
    ppermute x20, starting transfers between devices, exchange(): return lax.ppermute(value, (axis, C), pairs)  22.7 us
    ppermute x8, starting transfers between devices, swap(): return lax.ppermute(value, C, [(0, 1), (1, 0)])  20 us
    all_to_all x1, blocking collectives, total_over_all(): part = jnp.sum(lax.all_to_all(spread, (Z, C), 0, 0, tiled=True)[:, 0, 0])  16.6 us
    all_to_all x1, blocking collectives, total_over_all(): return jnp.sum(lax.all_to_all(spread, (X, Y), 0, 0, tiled=True)[:, 0, 0])  11.7 us
    unnamed x28, local copies, waits for them, and re-layouts  9.53 us
    pallas_call x2, Pallas kernels, products(): pl.pallas_call(kernel, in_specs=[smem, pl.BlockSpec(memory_space=pl.ANY),...  8.52 us
    pallas_call x2, Pallas kernels, written(): pl.pallas_call(kernel, in_specs=[smem] * 5 + [vmem] * 4 + [anywhere] * le...  6.26 us
  transfers between devices with their start and end apart: 28, of which 16 were waited for; matrix products, arithmetic and copies ran while one was open for 5% of the time, Pallas kernels for 5%

profile of v1, /device:TPU:1, one launch (start us, length us, event | category | flops | bytes accessed | tf_op | source)
XLA Modules:
  0.0 160.0 jit_solution(6929179200705182804)
XLA Ops:
  0.6 3.0 %copy-done = bf16[768,4608]{1,0:T(8,128)(2,1)S(1)} copy-done((bf16[768,4608]{1,0:T(8,128)(2,1)S(1)}, bf16[768,4608]{1,0:T(8,128)(2,1)}, u32[]{:S(2)}) %copy-start) | copy-done | bytes 7077912
  3.6 1.1 copy-done.3
  4.8 4.3 %shard_map.154 = (f32[2304,256]{1,0:T(8,128)}, f32[2304,256]{1,0:T(8,128)S(1)}) custom-call(s32[1]{0:T(128)} %bitcast.4.me, bf16[768,4608]{1,0:T(8,128)(2,1)S(1)} %copy-done, bf16[768,512]{1,0:T(8,128)(2,1)S(1)} %copy-done.3), custom_call_target="tpu_custom_call" | custom-call | flops 1811939328 | bytes 9437184 | tf_op jit(solution)/shard_map/pallas_call | solution.py:99
  9.0 3.3 %collective-permute-start = (f32[2304,256]{1,0:T(8,128)}, f32[2304,256]{1,0:T(8,128)}, u32[]{:S(2)}, u32[]{:S(2)}) collective-permute-start(f32[2304,256]{1,0:T(8,128)} %get-tuple-element.42), channel_id=1, source_target_pairs={{0,4},{4,0},{1,5},{5,1},{2,6},{6,2},{3,7},{7,3},{8,12},{12,8},{9,1... | collective-permute-start | bytes 7077896 | tf_op jit(solution)/shard_map/ppermute | solution.py:38
  12.3 4.3 %shard_map.155 = (f32[2304,256]{1,0:T(8,128)}, f32[2304,256]{1,0:T(8,128)S(1)}) custom-call(s32[1]{0:T(128)} %bitcast.4.me, bf16[768,4608]{1,0:T(8,128)(2,1)S(1)} %copy-done, bf16[768,512]{1,0:T(8,128)(2,1)S(1)} %copy-done.3), custom_call_target="tpu_custom_call" | custom-call | flops 1811939328 | bytes 9437184 | tf_op jit(solution)/shard_map/pallas_call | solution.py:99
  16.6 1.4 copy-done.1
  18.1 0.8 fusion.16
  18.8 0.8 fusion.17
  19.6 3.4 %collective-permute-done.1.q1 = f32[2304,256]{1,0:T(8,128)} collective-permute-done((f32[2304,256]{1,0:T(8,128)}, f32[2304,256]{1,0:T(8,128)}, u32[]{:S(2)}, u32[]{:S(2)}) %collective-permute-start.1) | collective-permute-done | bytes 2359328 | tf_op jit(solution)/shard_map/ppermute | solution.py:38
  23.0 1.7 %copy-done.2 = f32[2304,256]{1,0:T(8,128)S(1)} copy-done((f32[2304,256]{1,0:T(8,128)S(1)}, f32[2304,256]{1,0:T(8,128)}, u32[]{:S(2)}) %copy-start.2) | copy-done | bytes 2359320
  24.6 2.8 %shard_map.156 = (f32[2,8,144,128]{3,2,1,0:T(8,128)S(1)}, f32[4,4,144,128]{3,2,1,0:T(8,128)S(1)}) custom-call(s32[4]{0:T(128)S(1)} %get-tuple-element.109.ox, s32[8]{0:T(128)S(1)} %get-tuple-element.107.oz, f32[2304,256]{1,0:T(8,128)S(1)} %get-tuple-element.40.p0, f32[2304,256]{1,0:T(8,128)S(1)} %copy-done.2, f32[2304,256]{1,0:T(8,128)} %collective-permute-done.q0, ...), custom_call_target="tpu_custom_call" | custom-call | bytes 7340032 | tf_op jit(solution)/shard_map/pallas_call | solution.py:125
  27.4 1.1 copy-done.4
  28.5 3.2 %shard_map.157 = (f32[2,8,144,128]{3,2,1,0:T(8,128)S(1)}, f32[4,4,144,128]{3,2,1,0:T(8,128)S(1)}) custom-call(s32[4]{0:T(128)S(1)} %get-tuple-element.109.ox, s32[8]{0:T(128)S(1)} %get-tuple-element.107.oz, f32[2304,256]{1,0:T(8,128)S(1)} %get-tuple-element.40.p0, f32[2304,256]{1,0:T(8,128)S(1)} %copy-done.2, f32[2304,256]{1,0:T(8,128)} %collective-permute-done.q0, ...), custom_call_target="tpu_custom_call" | custom-call | bytes 7340032 | tf_op jit(solution)/shard_map/pallas_call | solution.py:125
  31.9 0.8 collective-permute-start.2
  33.4 0.1 multiply_convert_fusion
  33.5 5.7 %collective-permute-start.7 = (f16[4,4,144,128]{3,2,1,0:T(8,128)(2,1)S(1)}, f16[4,4,144,128]{3,2,1,0:T(8,128)(2,1)S(1)}, u32[]{:S(2)}, u32[]{:S(2)}) collective-permute-start(f16[4,4,144,128]{3,2,1,0:T(8,128)(2,1)S(1)} %multiply_convert_fusion), channel_id=1, source_target_pairs={{0,8},{4,60},{8,0},{12,20},{16,24},{20,12},{24,16},{28,36},{32,40}... | collective-permute-start | bytes 1769480 | tf_op jit(solution)/shard_map/ppermute | solution.py:45
  39.3 2.8 %collective-permute-done.2 = f16[2,8,144,128]{3,2,1,0:T(8,128)(2,1)} collective-permute-done((f16[2,8,144,128]{3,2,1,0:T(8,128)(2,1)S(1)}, f16[2,8,144,128]{3,2,1,0:T(8,128)(2,1)}, u32[]{:S(2)}, u32[]{:S(2)}) %collective-permute-start.2) | collective-permute-done | bytes 589856 | tf_op jit(solution)/shard_map/ppermute | solution.py:45
  42.0 1.3 multiply_add_fusion.1
  43.5 3.0 %collective-permute-done.7 = f16[4,4,144,128]{3,2,1,0:T(8,128)(2,1)S(1)} collective-permute-done((f16[4,4,144,128]{3,2,1,0:T(8,128)(2,1)S(1)}, f16[4,4,144,128]{3,2,1,0:T(8,128)(2,1)S(1)}, u32[]{:S(2)}, u32[]{:S(2)}) %collective-permute-start.7) | collective-permute-done | bytes 589856 | tf_op jit(solution)/shard_map/ppermute | solution.py:45
  46.5 0.1 multiply_add_fusion
  46.8 2.6 %collective-permute-done.3 = f16[1,8,144,128]{3,2,1,0:T(8,128)(2,1)S(1)} collective-permute-done((f16[1,8,144,128]{3,2,1,0:T(8,128)(2,1)S(1)}, f16[1,8,144,128]{3,2,1,0:T(8,128)(2,1)S(1)}, u32[]{:S(2)}, u32[]{:S(2)}) %collective-permute-start.3) | collective-permute-done | bytes 294944 | tf_op jit(solution)/shard_map/ppermute | solution.py:45
  49.5 3.9 %collective-permute-start.4 = (f16[4,144,128]{2,1,0:T(8,128)(2,1)S(1)}, f16[4,144,128]{2,1,0:T(8,128)(2,1)S(1)}, u32[]{:S(2)}, u32[]{:S(2)}) collective-permute-start(f16[4,144,128]{2,1,0:T(8,128)(2,1)S(1)} %fusion.6), channel_id=1, source_target_pairs={{0,8},{4,60},{8,0},{12,20},{16,24},{20,12},{24,16},{28,36},{32,40}... | collective-permute-start | bytes 442376 | tf_op jit(solution)/shard_map/ppermute | solution.py:45
  53.5 2.3 %collective-permute-start.9 = (f16[1,4,144,128]{3,2,1,0:T(8,128)(2,1)S(1)}, f16[1,4,144,128]{3,2,1,0:T(8,128)(2,1)S(1)}, u32[]{:S(2)}, u32[]{:S(2)}) collective-permute-start(f16[1,4,144,128]{3,2,1,0:T(8,128)(2,1)S(1)} %fusion.2), channel_id=1, source_target_pairs={{0,24},{4,44},{8,48},{12,36},{16,40},{20,60},{24,0},{28,52},{32,56... | collective-permute-start | bytes 442376 | tf_op jit(solution)/shard_map/ppermute | solution.py:45
  55.9 0.5 collective-permute-done.4
  56.4 1.1 collective-permute-start.5
  57.5 5.0 %collective-permute-done.9 = f16[1,4,144,128]{3,2,1,0:T(8,128)(2,1)S(1)} collective-permute-done((f16[1,4,144,128]{3,2,1,0:T(8,128)(2,1)S(1)}, f16[1,4,144,128]{3,2,1,0:T(8,128)(2,1)S(1)}, u32[]{:S(2)}, u32[]{:S(2)}) %collective-permute-start.9) | collective-permute-done | bytes 147488 | tf_op jit(solution)/shard_map/ppermute | solution.py:45
  62.6 2.6 %collective-permute-start.11 = (f16[2,144,128]{2,1,0:T(8,128)(2,1)S(1)}, f16[2,144,128]{2,1,0:T(8,128)(2,1)S(1)}, u32[]{:S(2)}, u32[]{:S(2)}) collective-permute-start(f16[2,144,128]{2,1,0:T(8,128)(2,1)S(1)} %multiply_convert_fusion.2), channel_id=1, source_target_pairs={{0,64},{4,196},{64,0},{68,132},{128,192},{132,68},{192,128},{196,4... | collective-permute-start | bytes 221192 | tf_op jit(solution)/shard_map/ppermute | solution.py:45
  65.2 0.2 collective-permute-start.6
  65.4 1.7 %collective-permute-done.11 = f16[2,144,128]{2,1,0:T(8,128)(2,1)S(1)} collective-permute-done((f16[2,144,128]{2,1,0:T(8,128)(2,1)S(1)}, f16[2,144,128]{2,1,0:T(8,128)(2,1)S(1)}, u32[]{:S(2)}, u32[]{:S(2)}) %collective-permute-start.11) | collective-permute-done | bytes 73760 | tf_op jit(solution)/shard_map/ppermute | solution.py:45
  67.3 3.9 %collective-permute-done.6 = f16[1,144,128]{2,1,0:T(8,128)(2,1)S(1)} collective-permute-done((f16[1,144,128]{2,1,0:T(8,128)(2,1)S(1)}, f16[1,144,128]{2,1,0:T(8,128)(2,1)S(1)}, u32[]{:S(2)}, u32[]{:S(2)}) %collective-permute-start.6) | collective-permute-done | bytes 36896 | tf_op jit(solution)/shard_map/ppermute | solution.py:45
  71.1 0.6 multiply_reduce_fusion.1
  71.7 0.6 multiply_reduce_fusion
  73.7 16.6 %all_to_all.10 = f32[16,8,128]{2,1,0:T(8,128)S(1)} all-to-all(f32[16,8,128]{2,1,0:T(8,128)S(1)} %broadcast_in_dim.26), channel_id=1, replica_groups=mesh['dp_0'=4,'dp_1'=8,'dp_2'=2,'mp'=4] {'dp_1','dp_2'}, dimensions={0} | all-to-all | bytes 131072 | tf_op jit(solution)/shard_map/all_to_all | solution.py:173
  90.3 0.6 slice_reduce_fusion.1
  90.9 0.6 broadcast_in_dim.27
  91.6 11.7 %all_to_all.11 = f32[16,8,128]{2,1,0:T(8,128)S(1)} all-to-all(f32[16,8,128]{2,1,0:T(8,128)S(1)} %broadcast_in_dim.27), channel_id=1, replica_groups=mesh['dp_0'=4,'dp_1'=8,'dp_2'=2,'mp'=4] {'dp_0','mp'}, dimensions={0} | all-to-all | bytes 131072 | tf_op jit(solution)/shard_map/all_to_all | solution.py:175
  103.3 0.6 slice_reduce_fusion
  104.6 0.1 shard_map.158
  104.8 0.3 collective-permute-start.13
  105.1 0.2 collective-permute-start.18
  105.3 6.2 %collective-permute-done.13 = bf16[1,144,128]{2,1,0:T(8,128)(2,1)S(1)} collective-permute-done((bf16[1,144,128]{2,1,0:T(8,128)(2,1)S(1)}, bf16[1,144,128]{2,1,0:T(8,128)(2,1)S(1)}, u32[]{:S(2)}, u32[]{:S(2)}) %collective-permute-start.13) | collective-permute-done | bytes 36896 | tf_op jit(solution)/shard_map/ppermute | solution.py:45
  111.6 0.9 collective-permute-start.19
  112.5 2.2 %collective-permute-done.14 = bf16[2,144,128]{2,1,0:T(8,128)(2,1)S(1)} collective-permute-done((bf16[2,144,128]{2,1,0:T(8,128)(2,1)S(1)}, bf16[2,144,128]{2,1,0:T(8,128)(2,1)S(1)}, u32[]{:S(2)}, u32[]{:S(2)}) %collective-permute-start.14) | collective-permute-done | bytes 73760 | tf_op jit(solution)/shard_map/ppermute | solution.py:45
  114.9 1.2 collective-permute-done.19
  116.1 0.9 collective-permute-start.20
  117.1 3.0 %collective-permute-done.15 = bf16[4,144,128]{2,1,0:T(8,128)(2,1)S(1)} collective-permute-done((bf16[4,144,128]{2,1,0:T(8,128)(2,1)S(1)}, bf16[4,144,128]{2,1,0:T(8,128)(2,1)S(1)}, u32[]{:S(2)}, u32[]{:S(2)}) %collective-permute-start.15) | collective-permute-done | bytes 147488 | tf_op jit(solution)/shard_map/ppermute | solution.py:45
  120.1 0.3 collective-permute-start.16
  120.4 3.6 %collective-permute-done.20 = bf16[1,4,144,128]{3,2,1,0:T(8,128)(2,1)S(1)} collective-permute-done((bf16[1,4,144,128]{3,2,1,0:T(8,128)(2,1)S(1)}, bf16[1,4,144,128]{3,2,1,0:T(8,128)(2,1)S(1)}, u32[]{:S(2)}, u32[]{:S(2)}) %collective-permute-start.20) | collective-permute-done | bytes 147488 | tf_op jit(solution)/shard_map/ppermute | solution.py:45
  124.0 1.3 collective-permute-start.21
  125.3 0.7 collective-permute-done.16
  126.1 0.9 collective-permute-start.17
  127.1 3.7 %collective-permute-done.21 = bf16[2,4,144,128]{3,2,1,0:T(8,128)(2,1)S(1)} collective-permute-done((bf16[2,4,144,128]{3,2,1,0:T(8,128)(2,1)S(1)}, bf16[2,4,144,128]{3,2,1,0:T(8,128)(2,1)S(1)}, u32[]{:S(2)}, u32[]{:S(2)}) %collective-permute-start.21) | collective-permute-done | bytes 294944 | tf_op jit(solution)/shard_map/ppermute | solution.py:45
  130.8 0.7 collective-permute-start.22
  131.6 6.8 %collective-permute-start.25 = (bf16[2,8,144,128]{3,2,1,0:T(8,128)(2,1)S(1)}, bf16[2,8,144,128]{3,2,1,0:T(8,128)(2,1)}, u32[]{:S(2)}, u32[]{:S(2)}) collective-permute-start(bf16[2,8,144,128]{3,2,1,0:T(8,128)(2,1)S(1)} %pad_maximum_fusion.a), channel_id=1, source_target_pairs={{0,4},{4,0},{1,5},{5,1},{2,6},{6,2},{3,7},{7,3},{8,12},{12,8},{9,1... | collective-permute-start | bytes 1769480 | tf_op jit(solution)/shard_map/ppermute | solution.py:38
  138.5 6.2 %collective-permute-start.23 = (bf16[2,8,144,128]{3,2,1,0:T(8,128)(2,1)S(1)}, bf16[2,8,144,128]{3,2,1,0:T(8,128)(2,1)S(1)}, u32[]{:S(2)}, u32[]{:S(2)}) collective-permute-start(bf16[2,8,144,128]{3,2,1,0:T(8,128)(2,1)S(1)} %collective-permute-done.17.a), channel_id=1, source_target_pairs={{0,4},{4,0},{1,5},{5,1},{2,6},{6,2},{3,7},{7,3},{8,12},{12,8},{9,1... | collective-permute-start | bytes 1769480 | tf_op jit(solution)/shard_map/ppermute | solution.py:38
  144.7 3.4 %collective-permute-start.24 = (bf16[4,4,144,128]{3,2,1,0:T(8,128)(2,1)S(1)}, bf16[4,4,144,128]{3,2,1,0:T(8,128)(2,1)}, u32[]{:S(2)}, u32[]{:S(2)}) collective-permute-start(bf16[4,4,144,128]{3,2,1,0:T(8,128)(2,1)S(1)} %collective-permute-done.22.b), channel_id=1, source_target_pairs={{0,4},{4,0},{1,5},{5,1},{2,6},{6,2},{3,7},{7,3},{8,12},{12,8},{9,1... | collective-permute-start | bytes 1769480 | tf_op jit(solution)/shard_map/ppermute | solution.py:38
  148.2 0.6 fusion.8
  148.8 1.6 %collective-permute-done.27 = f32[72,256]{1,0:T(8,128)} collective-permute-done((f32[72,256]{1,0:T(8,128)}, f32[72,256]{1,0:T(8,128)}, u32[]{:S(2)}, u32[]{:S(2)}) %collective-permute-start.27) | collective-permute-done | bytes 73760 | tf_op jit(solution)/shard_map/ppermute | solution.py:38
  150.4 0.9 broadcast_select_fusion
  151.3 1.0 shard_map.159
  152.3 0.6 copy.26
  152.9 0.6 copy.27
  153.5 3.2 %shard_map.160.rest_0_ = bf16[4608,512]{1,0:T(8,128)(2,1)} custom-call(s32[4]{0:T(128)S(1)} %get-tuple-element.109.ox, s32[8]{0:T(128)S(1)} %get-tuple-element.107.oz, s32[4]{0:T(128)S(1)} %get-tuple-element.108.px, s32[8]{0:T(128)S(1)} %get-tuple-element.106.pz, s32[1]{0:T(128)} %bitcast.4.me, bf16[2,8,144,128]{3,2,1,0:T(8,128)(2,1)S(1)} %pad_maximum_fusion.a, ...), custom_call_target="tpu_custom_call" | custom-call | bytes 9437184 | tf_op jit(solution)/shard_map/pallas_call | solution.py:159
  156.8 3.0 %shard_map.161 = bf16[4608,512]{1,0:T(8,128)(2,1)} custom-call(s32[4]{0:T(128)S(1)} %get-tuple-element.109.ox, s32[8]{0:T(128)S(1)} %get-tuple-element.107.oz, s32[4]{0:T(128)S(1)} %get-tuple-element.108.px, s32[8]{0:T(128)S(1)} %get-tuple-element.106.pz, s32[1]{0:T(128)} %bitcast.4.me, ...), custom_call_target="tpu_custom_call", output_to_operand_aliasing={{}: (9, {})} | custom-call | bytes 9437184 | tf_op jit(solution)/shard_map/pallas_call | solution.py:159
  (79 shorter events, 2.2 us)
Async XLA Ops:
  0.6 3.0 %copy-start = (bf16[768,4608]{1,0:T(8,128)(2,1)S(1)}, bf16[768,4608]{1,0:T(8,128)(2,1)}, u32[]{:S(2)}) copy-start(bf16[768,4608]{1,0:T(8,128)(2,1)} %a.3) | copy-start | bytes 21233668
  3.6 1.1 copy-start.3
  9.0 10.6 %collective-permute-start = (f32[2304,256]{1,0:T(8,128)}, f32[2304,256]{1,0:T(8,128)}, u32[]{:S(2)}, u32[]{:S(2)}) collective-permute-start(f32[2304,256]{1,0:T(8,128)} %get-tuple-element.42), channel_id=1, source_target_pairs={{0,4},{4,0},{1,5},{5,1},{2,6},{6,2},{3,7},{7,3},{8,12},{12,8},{9,1... | collective-permute-start | bytes 7077896 | tf_op jit(solution)/shard_map/ppermute | solution.py:38
  16.6 1.5 copy-start.1
  18.1 4.9 %collective-permute-start.1 = (f32[2304,256]{1,0:T(8,128)}, f32[2304,256]{1,0:T(8,128)}, u32[]{:S(2)}, u32[]{:S(2)}) collective-permute-start(f32[2304,256]{1,0:T(8,128)} %get-tuple-element.43), channel_id=1, source_target_pairs={{0,4},{4,0},{1,5},{5,1},{2,6},{6,2},{3,7},{7,3},{8,12},{12,8},{9,1... | collective-permute-start | bytes 7077896 | tf_op jit(solution)/shard_map/ppermute | solution.py:38
  23.0 1.7 %copy-start.2 = (f32[2304,256]{1,0:T(8,128)S(1)}, f32[2304,256]{1,0:T(8,128)}, u32[]{:S(2)}) copy-start(f32[2304,256]{1,0:T(8,128)} %copy-done.1) | copy-start | bytes 7077892
  27.4 1.1 copy-start.4
  28.5 3.2 %copy-start.6 = (f32[2,8,144,128]{3,2,1,0:T(8,128)}, f32[2,8,144,128]{3,2,1,0:T(8,128)S(1)}, u32[]{:S(2)}) copy-start(f32[2,8,144,128]{3,2,1,0:T(8,128)S(1)} %get-tuple-element.45) | copy-start | bytes 3538948
  31.7 1.0 copy-start.11
  31.7 1.2 copy-start.12
  31.7 1.4 copy-start.9
  31.7 1.4 copy-start.10
  31.8 1.5 copy-start.8
  31.9 10.1 %collective-permute-start.2 = (f16[2,8,144,128]{3,2,1,0:T(8,128)(2,1)S(1)}, f16[2,8,144,128]{3,2,1,0:T(8,128)(2,1)}, u32[]{:S(2)}, u32[]{:S(2)}) collective-permute-start(f16[2,8,144,128]{3,2,1,0:T(8,128)(2,1)S(1)} %multiply_convert_fusion.1), channel_id=1, source_target_pairs={{0,64},{4,196},{64,0},{68,132},{128,192},{132,68},{192,128},{196,4... | collective-permute-start | bytes 1769480 | tf_op jit(solution)/shard_map/ppermute | solution.py:45
  33.3 5.9 %collective-permute-start.10 = (f32[3,72,256]{2,1,0:T(8,128)S(1)}, f32[3,72,256]{2,1,0:T(8,128)S(1)}, u32[]{:S(2)}, u32[]{:S(2)}) collective-permute-start(f32[3,72,256]{2,1,0:T(8,128)S(1)} %constant_dynamic-slice_fusion), channel_id=1, source_target_pairs={{0,4},{4,0},{1,5},{5,1},{2,6},{6,2},{3,7},{7,3},{8,12},{12,8},{9,1... | collective-permute-start | bytes 663560 | tf_op jit(solution)/shard_map/ppermute | solution.py:38
  33.5 8.5 %copy-start.7 = (f32[2,8,144,128]{3,2,1,0:T(8,128)S(1)}, f32[2,8,144,128]{3,2,1,0:T(8,128)}, u32[]{:S(2)}) copy-start(f32[2,8,144,128]{3,2,1,0:T(8,128)} %copy-done.6) | copy-start | bytes 3538948
  33.5 12.9 %collective-permute-start.7 = (f16[4,4,144,128]{3,2,1,0:T(8,128)(2,1)S(1)}, f16[4,4,144,128]{3,2,1,0:T(8,128)(2,1)S(1)}, u32[]{:S(2)}, u32[]{:S(2)}) collective-permute-start(f16[4,4,144,128]{3,2,1,0:T(8,128)(2,1)S(1)} %multiply_convert_fusion), channel_id=1, source_target_pairs={{0,8},{4,60},{8,0},{12,20},{16,24},{20,12},{24,16},{28,36},{32,40}... | collective-permute-start | bytes 1769480 | tf_op jit(solution)/shard_map/ppermute | solution.py:45
  42.0 4.4 %copy-start.5 = (f32[4,4,144,128]{3,2,1,0:T(8,128)S(1)}, f32[4,4,144,128]{3,2,1,0:T(8,128)}, u32[]{:S(2)}) copy-start(f32[4,4,144,128]{3,2,1,0:T(8,128)} %copy-done.4) | copy-start | bytes 3538948
  43.4 6.0 %collective-permute-start.3 = (f16[1,8,144,128]{3,2,1,0:T(8,128)(2,1)S(1)}, f16[1,8,144,128]{3,2,1,0:T(8,128)(2,1)S(1)}, u32[]{:S(2)}, u32[]{:S(2)}) collective-permute-start(f16[1,8,144,128]{3,2,1,0:T(8,128)(2,1)S(1)} %fusion.1), channel_id=1, source_target_pairs={{0,192},{4,68},{64,128},{68,4},{128,64},{132,196},{192,0},{196,132... | collective-permute-start | bytes 884744 | tf_op jit(solution)/shard_map/ppermute | solution.py:45
  46.7 6.7 %collective-permute-start.8 = (f16[2,4,144,128]{3,2,1,0:T(8,128)(2,1)S(1)}, f16[2,4,144,128]{3,2,1,0:T(8,128)(2,1)S(1)}, u32[]{:S(2)}, u32[]{:S(2)}) collective-permute-start(f16[2,4,144,128]{3,2,1,0:T(8,128)(2,1)S(1)} %fusion), channel_id=1, source_target_pairs={{0,56},{4,12},{8,16},{12,4},{16,8},{20,28},{24,32},{28,20},{32,24}... | collective-permute-start | bytes 884744 | tf_op jit(solution)/shard_map/ppermute | solution.py:45
  49.5 6.9 %collective-permute-start.4 = (f16[4,144,128]{2,1,0:T(8,128)(2,1)S(1)}, f16[4,144,128]{2,1,0:T(8,128)(2,1)S(1)}, u32[]{:S(2)}, u32[]{:S(2)}) collective-permute-start(f16[4,144,128]{2,1,0:T(8,128)(2,1)S(1)} %fusion.6), channel_id=1, source_target_pairs={{0,8},{4,60},{8,0},{12,20},{16,24},{20,12},{24,16},{28,36},{32,40}... | collective-permute-start | bytes 442376 | tf_op jit(solution)/shard_map/ppermute | solution.py:45
  53.5 9.0 %collective-permute-start.9 = (f16[1,4,144,128]{3,2,1,0:T(8,128)(2,1)S(1)}, f16[1,4,144,128]{3,2,1,0:T(8,128)(2,1)S(1)}, u32[]{:S(2)}, u32[]{:S(2)}) collective-permute-start(f16[1,4,144,128]{3,2,1,0:T(8,128)(2,1)S(1)} %fusion.2), channel_id=1, source_target_pairs={{0,24},{4,44},{8,48},{12,36},{16,40},{20,60},{24,0},{28,52},{32,56... | collective-permute-start | bytes 442376 | tf_op jit(solution)/shard_map/ppermute | solution.py:45
  56.4 8.8 %collective-permute-start.5 = (f16[2,144,128]{2,1,0:T(8,128)(2,1)S(1)}, f16[2,144,128]{2,1,0:T(8,128)(2,1)S(1)}, u32[]{:S(2)}, u32[]{:S(2)}) collective-permute-start(f16[2,144,128]{2,1,0:T(8,128)(2,1)S(1)} %fusion.7), channel_id=1, source_target_pairs={{0,56},{4,12},{8,16},{12,4},{16,8},{20,28},{24,32},{28,20},{32,24}... | collective-permute-start | bytes 221192 | tf_op jit(solution)/shard_map/ppermute | solution.py:45
  62.6 4.5 %collective-permute-start.11 = (f16[2,144,128]{2,1,0:T(8,128)(2,1)S(1)}, f16[2,144,128]{2,1,0:T(8,128)(2,1)S(1)}, u32[]{:S(2)}, u32[]{:S(2)}) collective-permute-start(f16[2,144,128]{2,1,0:T(8,128)(2,1)S(1)} %multiply_convert_fusion.2), channel_id=1, source_target_pairs={{0,64},{4,196},{64,0},{68,132},{128,192},{132,68},{192,128},{196,4... | collective-permute-start | bytes 221192 | tf_op jit(solution)/shard_map/ppermute | solution.py:45
  65.2 5.9 %collective-permute-start.6 = (f16[1,144,128]{2,1,0:T(8,128)(2,1)S(1)}, f16[1,144,128]{2,1,0:T(8,128)(2,1)S(1)}, u32[]{:S(2)}, u32[]{:S(2)}) collective-permute-start(f16[1,144,128]{2,1,0:T(8,128)(2,1)S(1)} %fusion.12), channel_id=1, source_target_pairs={{0,24},{4,44},{8,48},{12,36},{16,40},{20,60},{24,0},{28,52},{32,56... | collective-permute-start | bytes 110600 | tf_op jit(solution)/shard_map/ppermute | solution.py:45
  67.2 4.6 %collective-permute-start.12 = (f16[1,144,128]{2,1,0:T(8,128)(2,1)S(1)}, f16[1,144,128]{2,1,0:T(8,128)(2,1)S(1)}, u32[]{:S(2)}, u32[]{:S(2)}) collective-permute-start(f16[1,144,128]{2,1,0:T(8,128)(2,1)S(1)} %fusion.10), channel_id=1, source_target_pairs={{0,192},{4,68},{64,128},{68,4},{128,64},{132,196},{192,0},{196,132... | collective-permute-start | bytes 110600 | tf_op jit(solution)/shard_map/ppermute | solution.py:45
  104.8 6.7 %collective-permute-start.13 = (bf16[1,144,128]{2,1,0:T(8,128)(2,1)S(1)}, bf16[1,144,128]{2,1,0:T(8,128)(2,1)S(1)}, u32[]{:S(2)}, u32[]{:S(2)}) collective-permute-start(bf16[1,144,128]{2,1,0:T(8,128)(2,1)S(1)} %bitcast.39), channel_id=1, source_target_pairs={{0,24},{4,44},{8,48},{12,36},{16,40},{20,60},{24,0},{28,52},{32,56... | collective-permute-start | bytes 110600 | tf_op jit(solution)/shard_map/ppermute | solution.py:45
  105.1 6.5 %collective-permute-start.18 = (bf16[1,144,128]{2,1,0:T(8,128)(2,1)S(1)}, bf16[1,144,128]{2,1,0:T(8,128)(2,1)S(1)}, u32[]{:S(2)}, u32[]{:S(2)}) collective-permute-start(bf16[1,144,128]{2,1,0:T(8,128)(2,1)S(1)} %bitcast.43), channel_id=1, source_target_pairs={{0,192},{4,68},{64,128},{68,4},{128,64},{132,196},{192,0},{196,132... | collective-permute-start | bytes 110600 | tf_op jit(solution)/shard_map/ppermute | solution.py:45
  111.5 3.3 %collective-permute-start.14 = (bf16[2,144,128]{2,1,0:T(8,128)(2,1)S(1)}, bf16[2,144,128]{2,1,0:T(8,128)(2,1)S(1)}, u32[]{:S(2)}, u32[]{:S(2)}) collective-permute-start(bf16[2,144,128]{2,1,0:T(8,128)(2,1)S(1)} %pad_maximum_fusion.7), channel_id=1, source_target_pairs={{0,56},{4,12},{8,16},{12,4},{16,8},{20,28},{24,32},{28,20},{32,24}... | collective-permute-start | bytes 221192 | tf_op jit(solution)/shard_map/ppermute | solution.py:45
  111.6 4.5 %collective-permute-start.19 = (bf16[2,144,128]{2,1,0:T(8,128)(2,1)S(1)}, bf16[2,144,128]{2,1,0:T(8,128)(2,1)S(1)}, u32[]{:S(2)}, u32[]{:S(2)}) collective-permute-start(bf16[2,144,128]{2,1,0:T(8,128)(2,1)S(1)} %pad_maximum_fusion.8), channel_id=1, source_target_pairs={{0,64},{4,196},{64,0},{68,132},{128,192},{132,68},{192,128},{196,4... | collective-permute-start | bytes 221192 | tf_op jit(solution)/shard_map/ppermute | solution.py:45
  114.8 5.3 %collective-permute-start.15 = (bf16[4,144,128]{2,1,0:T(8,128)(2,1)S(1)}, bf16[4,144,128]{2,1,0:T(8,128)(2,1)S(1)}, u32[]{:S(2)}, u32[]{:S(2)}) collective-permute-start(bf16[4,144,128]{2,1,0:T(8,128)(2,1)S(1)} %pad_maximum_fusion.5), channel_id=1, source_target_pairs={{0,8},{4,60},{8,0},{12,20},{16,24},{20,12},{24,16},{28,36},{32,40}... | collective-permute-start | bytes 442376 | tf_op jit(solution)/shard_map/ppermute | solution.py:45
  116.1 7.9 %collective-permute-start.20 = (bf16[1,4,144,128]{3,2,1,0:T(8,128)(2,1)S(1)}, bf16[1,4,144,128]{3,2,1,0:T(8,128)(2,1)S(1)}, u32[]{:S(2)}, u32[]{:S(2)}) collective-permute-start(bf16[1,4,144,128]{3,2,1,0:T(8,128)(2,1)S(1)} %bitcast.46), channel_id=1, source_target_pairs={{0,24},{4,44},{8,48},{12,36},{16,40},{20,60},{24,0},{28,52},{32,56... | collective-permute-start | bytes 442376 | tf_op jit(solution)/shard_map/ppermute | solution.py:45
  120.1 6.0 %collective-permute-start.16 = (bf16[1,8,144,128]{3,2,1,0:T(8,128)(2,1)S(1)}, bf16[1,8,144,128]{3,2,1,0:T(8,128)(2,1)S(1)}, u32[]{:S(2)}, u32[]{:S(2)}) collective-permute-start(bf16[1,8,144,128]{3,2,1,0:T(8,128)(2,1)S(1)} %maximum_bitcast_fusion), channel_id=1, source_target_pairs={{0,192},{4,68},{64,128},{68,4},{128,64},{132,196},{192,0},{196,132... | collective-permute-start | bytes 884744 | tf_op jit(solution)/shard_map/ppermute | solution.py:45
  124.0 6.7 %collective-permute-start.21 = (bf16[2,4,144,128]{3,2,1,0:T(8,128)(2,1)S(1)}, bf16[2,4,144,128]{3,2,1,0:T(8,128)(2,1)S(1)}, u32[]{:S(2)}, u32[]{:S(2)}) collective-permute-start(bf16[2,4,144,128]{3,2,1,0:T(8,128)(2,1)S(1)} %pad_maximum_fusion.4), channel_id=1, source_target_pairs={{0,56},{4,12},{8,16},{12,4},{16,8},{20,28},{24,32},{28,20},{32,24}... | collective-permute-start | bytes 884744 | tf_op jit(solution)/shard_map/ppermute | solution.py:45
  126.1 12.4 %collective-permute-start.17 = (bf16[2,8,144,128]{3,2,1,0:T(8,128)(2,1)S(1)}, bf16[2,8,144,128]{3,2,1,0:T(8,128)(2,1)S(1)}, u32[]{:S(2)}, u32[]{:S(2)}) collective-permute-start(bf16[2,8,144,128]{3,2,1,0:T(8,128)(2,1)S(1)} %pad_maximum_fusion.a), channel_id=1, source_target_pairs={{0,64},{4,196},{64,0},{68,132},{128,192},{132,68},{192,128},{196,4... | collective-permute-start | bytes 1769480 | tf_op jit(solution)/shard_map/ppermute | solution.py:45
  130.8 13.9 %collective-permute-start.22 = (bf16[4,4,144,128]{3,2,1,0:T(8,128)(2,1)S(1)}, bf16[4,4,144,128]{3,2,1,0:T(8,128)(2,1)S(1)}, u32[]{:S(2)}, u32[]{:S(2)}) collective-permute-start(bf16[4,4,144,128]{3,2,1,0:T(8,128)(2,1)S(1)} %pad_maximum_fusion.1.b), channel_id=1, source_target_pairs={{0,8},{4,60},{8,0},{12,20},{16,24},{20,12},{24,16},{28,36},{32,40}... | collective-permute-start | bytes 1769480 | tf_op jit(solution)/shard_map/ppermute | solution.py:45
  131.6 20.8 %collective-permute-start.25 = (bf16[2,8,144,128]{3,2,1,0:T(8,128)(2,1)S(1)}, bf16[2,8,144,128]{3,2,1,0:T(8,128)(2,1)}, u32[]{:S(2)}, u32[]{:S(2)}) collective-permute-start(bf16[2,8,144,128]{3,2,1,0:T(8,128)(2,1)S(1)} %pad_maximum_fusion.a), channel_id=1, source_target_pairs={{0,4},{4,0},{1,5},{5,1},{2,6},{6,2},{3,7},{7,3},{8,12},{12,8},{9,1... | collective-permute-start | bytes 1769480 | tf_op jit(solution)/shard_map/ppermute | solution.py:38
  138.4 14.0 %collective-permute-start.26 = (bf16[4,4,144,128]{3,2,1,0:T(8,128)(2,1)S(1)}, bf16[4,4,144,128]{3,2,1,0:T(8,128)(2,1)}, u32[]{:S(2)}, u32[]{:S(2)}) collective-permute-start(bf16[4,4,144,128]{3,2,1,0:T(8,128)(2,1)S(1)} %pad_maximum_fusion.1.b), channel_id=1, source_target_pairs={{0,4},{4,0},{1,5},{5,1},{2,6},{6,2},{3,7},{7,3},{8,12},{12,8},{9,1... | collective-permute-start | bytes 1769480 | tf_op jit(solution)/shard_map/ppermute | solution.py:38
  138.5 18.3 %collective-permute-start.23 = (bf16[2,8,144,128]{3,2,1,0:T(8,128)(2,1)S(1)}, bf16[2,8,144,128]{3,2,1,0:T(8,128)(2,1)S(1)}, u32[]{:S(2)}, u32[]{:S(2)}) collective-permute-start(bf16[2,8,144,128]{3,2,1,0:T(8,128)(2,1)S(1)} %collective-permute-done.17.a), channel_id=1, source_target_pairs={{0,4},{4,0},{1,5},{5,1},{2,6},{6,2},{3,7},{7,3},{8,12},{12,8},{9,1... | collective-permute-start | bytes 1769480 | tf_op jit(solution)/shard_map/ppermute | solution.py:38
  144.7 12.0 %collective-permute-start.24 = (bf16[4,4,144,128]{3,2,1,0:T(8,128)(2,1)S(1)}, bf16[4,4,144,128]{3,2,1,0:T(8,128)(2,1)}, u32[]{:S(2)}, u32[]{:S(2)}) collective-permute-start(bf16[4,4,144,128]{3,2,1,0:T(8,128)(2,1)S(1)} %collective-permute-done.22.b), channel_id=1, source_target_pairs={{0,4},{4,0},{1,5},{5,1},{2,6},{6,2},{3,7},{7,3},{8,12},{12,8},{9,1... | collective-permute-start | bytes 1769480 | tf_op jit(solution)/shard_map/ppermute | solution.py:38
  148.8 1.6 %collective-permute-start.27 = (f32[72,256]{1,0:T(8,128)}, f32[72,256]{1,0:T(8,128)}, u32[]{:S(2)}, u32[]{:S(2)}) collective-permute-start(f32[72,256]{1,0:T(8,128)} %fusion.8), channel_id=1, source_target_pairs={{0,4},{4,0},{1,5},{5,1},{2,6},{6,2},{3,7},{7,3},{8,12},{12,8},{9,1... | collective-permute-start | bytes 221192 | tf_op jit(solution)/shard_map/ppermute | solution.py:38

commit v2 on v1

v2 whole, which is shorter than its diff:
```python
import math

import jax
import jax.numpy as jnp
import numpy as np
from jax import lax
from jax.experimental import pallas as pl
from jax.experimental.pallas import tpu as pltpu
from jax.sharding import Mesh
from jax.sharding import PartitionSpec as P

D = 4608
KV = 2048
QROWS = 4
QCOLS = 512
STEP = 10
X, Z, C, Y = "dp_0", "dp_1", "dp_2", "mp"
SIZE = {X: 4, Z: 8, C: 2, Y: 4}
DP = (X, Z, C)

beta_one = 0.9
beta_two = 0.95
learn_rate = 0.002
weight_decay = 0.1
epsilon = 1e-08
clip_rms = 0.25

f32 = jnp.float32


MATES = {
    X: ((1, 0, 3, 2), (3, 2, 1, 0)),
    Z: ((1, 0, 3, 2, 5, 4, 7, 6), (7, 2, 1, 4, 3, 6, 5, 0), (3, 6, 5, 0, 7, 2, 1, 4)),
}


def swap(value):
    return lax.ppermute(value, C, [(0, 1), (1, 0)])


def exchange(value, axis, step):
    n = SIZE[axis]
    mate = MATES[axis][step]
    pairs = [(i * 2 + c, ((mate[(i - c) % n] + c) % n) * 2 + c) for i in range(n) for c in range(2)]
    return lax.ppermute(value, (axis, C), pairs)


def kept_order(axis, node, step):
    if step == len(MATES[axis]):
        return [node]
    return kept_order(axis, node, step + 1) + kept_order(axis, MATES[axis][step][node], step + 1)


def order_of(axis, core):
    n = SIZE[axis]
    table = np.array([[[(d + c) % n for d in kept_order(axis, (i - c) % n, 0)] for c in range(2)] for i in range(n)], np.int32)
    return jnp.asarray(table)[lax.axis_index(axis), core]


def narrowed(send, terms):
    return (send * (1.0 / terms)).astype(jnp.float16)


def halving_sum(send, keep, axis, terms):
    for step in range(len(MATES[axis])):
        if step:
            half = keep.shape[0] // 2
            send, keep = narrowed(keep[half:], terms), keep[:half]
        keep = keep + exchange(send, axis, step).astype(f32) * float(terms)
        terms *= 2
    return keep[0]


def doubling_gather(value, axis, last=0):
    for step in range(len(MATES[axis]) - 1, last - 1, -1):
        value = jnp.concatenate([value, exchange(value, axis, step)])
    return value


def products(inputs, key_cotangent, core, h):
    width = 1152

    def kernel(me, a, b, theirs, mine, buf, cot, sem):
        copies = [pltpu.make_async_copy(a.at[:, pl.ds(h * 2304 + i * width, width)], buf.at[i], sem.at[i]) for i in (0, 1)]
        for i, which in ((0, 1 - me[0]), (1, me[0])):
            at = pl.ds(pl.multiple_of(which * 256, 256), 256)
            copies.append(pltpu.make_async_copy(b.at[:, at], cot.at[:, pl.ds(i * 256, 256)], sem.at[2 + i]))
        for copy in copies:
            copy.start()
        copies[2].wait()
        copies[3].wait()
        for i in (0, 1):
            copies[i].wait()
            term = lax.dot_general(buf[i], cot[...], (((0,), (0,)), ((), ())), preferred_element_type=f32)
            theirs[pl.ds(i * width, width), :] = term[:, :256]
            mine[pl.ds(i * width, width), :] = term[:, 256:]

    smem, vmem = pl.BlockSpec(memory_space=pltpu.SMEM), pl.BlockSpec(memory_space=pltpu.VMEM)
    anywhere = pl.BlockSpec(memory_space=pl.ANY)
    return pl.pallas_call(
        kernel,
        in_specs=[smem, anywhere, anywhere],
        out_specs=[vmem, vmem],
        out_shape=[jax.ShapeDtypeStruct((2304, 256), f32)] * 2,
        scratch_shapes=[
            pltpu.VMEM((2, 768, width), jnp.bfloat16),
            pltpu.VMEM((768, 512), jnp.bfloat16),
            pltpu.SemaphoreType.DMA((4,)),
        ],
        compiler_params=pltpu.CompilerParams(vmem_limit_bytes=46 << 20),
        cost_estimate=pl.CostEstimate(flops=2 * 768 * 2304 * 512, bytes_accessed=9 << 20, transcendentals=0),
    )(core.reshape(1), inputs, key_cotangent)


def packed(mine, theirs, order_x, order_z, want_a, want_b):
    def kernel(ox, oz, p0, p1, q0, q1, *outs):
        for i in range(4):
            for h, p, q in ((0, p0, q0), (1, p1, q1)):

                @pl.when(ox[i] // 2 == h)
                def _(i=i, h=h, p=p, q=q):
                    for j in range(8):
                        at = pl.ds(pl.multiple_of((ox[i] * 8 - h * 16 + oz[j]) * 144, 8), 144)
                        if i // 2 == want_a:
                            outs[0][i % 2, j] = p[at, :128] + q[at, :128]
                        if j // 4 == want_b:
                            outs[-1][j % 4, i] = p[at, 128:] + q[at, 128:]

    smem, vmem = pl.BlockSpec(memory_space=pltpu.SMEM), pl.BlockSpec(memory_space=pltpu.VMEM)
    shapes = [(2, 8, 144, 128)] * (want_a is not None) + [(4, 4, 144, 128)] * (want_b is not None)
    return pl.pallas_call(
        kernel,
        in_specs=[smem, smem] + [vmem] * 4,
        out_specs=[vmem] * len(shapes),
        out_shape=[jax.ShapeDtypeStruct(shape, f32) for shape in shapes],
        compiler_params=pltpu.CompilerParams(vmem_limit_bytes=8 << 20),
        cost_estimate=pl.CostEstimate(flops=1024, bytes_accessed=4096, transcendentals=0),
    )(order_x, order_z, *mine, *theirs)


def written(pieces, orders, core):
    def kernel(ox, oz, px, pz, me, *rest):
        refs, out, sem = rest[:-2], rest[-2], rest[-1]
        mine = pl.multiple_of(me[0] * 256, 128)
        other = pl.multiple_of((1 - me[0]) * 256, 128)
        started = []
        for part in (0, 1):
            a, b, c, d = refs[4 * part : 4 * part + 4]
            for source, order, col in ((a, ox, mine), (c, px, other)):
                for i in (0, 1):
                    target = out.at[order[2 * part + i], :, :, pl.ds(pl.multiple_of(col, 128), 128)]
                    started.append(pltpu.make_async_copy(source.at[i], target, sem.at[len(started)]))
                    started[-1].start()
            for source, order, col in ((b, oz, mine), (d, pz, other)):
                for j in range(4):
                    target = out.at[:, order[4 * part + j], :, pl.ds(pl.multiple_of(col + 128, 128), 128)]
                    started.append(pltpu.make_async_copy(source.at[j], target, sem.at[len(started)]))
                    started[-1].start()
        for copy in started:
            copy.wait()

    smem, vmem = pl.BlockSpec(memory_space=pltpu.SMEM), pl.BlockSpec(memory_space=pltpu.VMEM)
    return pl.pallas_call(
        kernel,
        in_specs=[smem] * 5 + [vmem] * 8,
        out_specs=pl.BlockSpec(memory_space=pltpu.HBM),
        out_shape=jax.ShapeDtypeStruct((4, 8, 144, 512), jnp.bfloat16),
        scratch_shapes=[pltpu.SemaphoreType.DMA((24,))],
        compiler_params=pltpu.CompilerParams(vmem_limit_bytes=8 << 20),
        cost_estimate=pl.CostEstimate(flops=1024, bytes_accessed=4096, transcendentals=0),
    )(*orders, core.reshape(1), *pieces).reshape(D, 512)


def summed_over(value, axes):
    spread = jnp.broadcast_to(value, (16, 8, 128))
    return jnp.sum(lax.all_to_all(spread, axes, 0, 0, tiled=True)[:, 0, 0])


def per_row(scale):
    return jnp.repeat(scale, QROWS, axis=0)


def moments(gradient, factor, first_old, second_old):
    clipped = gradient * factor
    first_new = beta_one * first_old + (1.0 - beta_one) * clipped
    second_new = beta_two * second_old + (1.0 - beta_two) * clipped * clipped
    return first_new, second_new


def stepped(master, first_new, second_new):
    first_hat = first_new / (1.0 - beta_one**STEP)
    second_hat = second_new / (1.0 - beta_two**STEP)
    step_dir = first_hat / (jnp.sqrt(second_hat) + epsilon)
    return master - learn_rate * (step_dir + weight_decay * master)


def weights_of(planes_a, planes_b, order_x, factor):
    def kernel(ox, f, a0, a1, b0, b1, wa, wb):
        for source, out, place in ((a0, wa, (0, 1)), (a1, wa, (2, 3)), (b0, wb, (ox[0], ox[1])), (b1, wb, (ox[2], ox[3]))):
            for j in (0, 1):
                news = moments(source[j, 0], f[0], source[j, 2], source[j, 3])
                out[place[j]] = stepped(source[j, 1], *news).astype(jnp.bfloat16)

    smem, vmem = pl.BlockSpec(memory_space=pltpu.SMEM), pl.BlockSpec(memory_space=pltpu.VMEM)
    return pl.pallas_call(
        kernel,
        in_specs=[smem] * 2 + [vmem] * 4,
        out_specs=[vmem, vmem],
        out_shape=[jax.ShapeDtypeStruct((4, 144, 128), jnp.bfloat16)] * 2,
        compiler_params=pltpu.CompilerParams(vmem_limit_bytes=8 << 20),
        cost_estimate=pl.CostEstimate(flops=1024, bytes_accessed=4096, transcendentals=0),
    )(order_x, factor.reshape(1), *planes_a, *planes_b)


def by_place(first, second, order):
    def kernel(o, a, b, out):
        for j in range(8):
            out[o[j]] = (a if j < 4 else b)[j % 4]

    smem, vmem = pl.BlockSpec(memory_space=pltpu.SMEM), pl.BlockSpec(memory_space=pltpu.VMEM)
    return pl.pallas_call(
        kernel,
        in_specs=[smem, vmem, vmem],
        out_specs=vmem,
        out_shape=jax.ShapeDtypeStruct((8, 144, 128), jnp.bfloat16),
        compiler_params=pltpu.CompilerParams(vmem_limit_bytes=4 << 20),
        cost_estimate=pl.CostEstimate(flops=1024, bytes_accessed=4096, transcendentals=0),
    )(order, first, second)


def own_results(left, right, state, factor):
    def largest(rows):
        top = jnp.broadcast_to(jnp.max(rows, axis=1, keepdims=True), (72, 128))
        at = lax.broadcasted_iota(jnp.int32, (72, 128), 0)
        top = jnp.maximum(top, jnp.where(at % 2 == 0, pltpu.roll(top, 71, 0), pltpu.roll(top, 1, 0)))
        return jnp.maximum(top, jnp.where(at % 4 < 2, pltpu.roll(top, 70, 0), pltpu.roll(top, 2, 0))) + 1e-06

    def kernel(f, l, r, state, master, first_unit, second_unit, first_top, second_top):
        gradient = jnp.concatenate([l[...], r[...]], axis=1)
        first_new, second_new = moments(gradient, f[0], state[1], state[2])
        master[...] = stepped(state[0], first_new, second_new)
        for new, unit, top in ((first_new, first_unit, first_top), (second_new, second_unit, second_top)):
            rows = largest(jnp.abs(new))
            row_of = lax.broadcasted_iota(jnp.int32, (72, 128), 0)
            lane = lax.broadcasted_iota(jnp.int32, (72, 128), 1)
            picked = jnp.sum(jnp.where(row_of == 4 * lane, rows, 0.0), axis=0, keepdims=True)
            top[...] = picked[:, :18]
            unit[...] = new / rows[:, :1]

    smem, vmem = pl.BlockSpec(memory_space=pltpu.SMEM), pl.BlockSpec(memory_space=pltpu.VMEM)
    return pl.pallas_call(
        kernel,
        in_specs=[smem] + [vmem] * 3,
        out_specs=[vmem] * 5,
        out_shape=[jax.ShapeDtypeStruct((72, 512), f32)] * 3 + [jax.ShapeDtypeStruct((1, 18), f32)] * 2,
        compiler_params=pltpu.CompilerParams(vmem_limit_bytes=8 << 20),
        cost_estimate=pl.CostEstimate(flops=1024, bytes_accessed=4096, transcendentals=0),
    )(factor.reshape(1), left, right, state)


def shards(inputs, key_cotangent, master, first_codes, second_codes, first_scale, second_scale):
    x, z, c = (lax.axis_index(a) for a in DP)
    order_x, order_z = order_of(X, c), order_of(Z, c)
    orders = (order_x, order_z, order_of(X, 1 - c), order_of(Z, 1 - c))

    terms = [products(inputs, key_cotangent, c, h) for h in (0, 1)]
    theirs = [swap(t) for t, _ in terms]
    mine = [m for _, m in terms]
    send_b = narrowed(*packed(mine, theirs, order_x, order_z, None, 1), 2)
    send_b, mine = lax.optimization_barrier((send_b, mine))
    send_a = narrowed(*packed(mine, theirs, order_x, order_z, 1, None), 2)
    send_a, mine = lax.optimization_barrier((send_a, mine))
    keep_a, keep_b = packed(mine, theirs, order_x, order_z, 0, 0)

    states = (master, first_codes, second_codes, first_scale, second_scale)
    keep_a, states = lax.optimization_barrier((keep_a, states))
    master, first_codes, second_codes, first_scale, second_scale = states
    first_old = first_codes.astype(f32) / 127.0 * per_row(first_scale)
    second_old = second_codes.astype(f32) / 255.0 * per_row(second_scale)
    state = jnp.stack([master, first_old, second_old])
    own = lax.dynamic_slice_in_dim(state, c * 256, 256, axis=2)
    got = swap(lax.dynamic_slice_in_dim(state, (1 - c) * 256, 256, axis=2))
    both = jnp.concatenate([jnp.where(c == 0, own, got), jnp.where(c == 0, got, own)], axis=1)

    over_x = halving_sum(send_a, keep_a, X, 2)
    over_z = halving_sum(send_b, keep_b, Z, 2)
    over_x, both = lax.optimization_barrier((over_x, both))
    grad_a = halving_sum(narrowed(over_x[4:], 8), over_x[:4], Z, 8)
    grad_b = halving_sum(narrowed(over_z[2:], 16), over_z[:2], X, 16)

    planes_a = jnp.concatenate([grad_a[None], both[:, :, :128]])[None]
    planes_b = jnp.concatenate([grad_b[None], both[:, :, 128:]])[None]
    squares = summed_over(jnp.sum(grad_a * grad_a) + jnp.sum(grad_b * grad_b), (Z, C))
    met_a, met_b = exchange(planes_a, Z, 2), exchange(planes_b, X, 1)
    met_a, met_b, squares = lax.optimization_barrier((met_a, met_b, squares))
    norm_sq = summed_over(squares, (X, Y))
    near_planes_a = jnp.concatenate([planes_a, met_a])
    near_planes_b = jnp.concatenate([planes_b, met_b])
    far_planes_a = exchange(near_planes_a, Z, 1)
    far_planes_b = exchange(near_planes_b, X, 0)
    gradient = jnp.concatenate([grad_a, grad_b], axis=1)
    kept = lax.dynamic_slice_in_dim(gradient, c * 72, 72, axis=0)
    came = swap(lax.dynamic_slice_in_dim(gradient, (1 - c) * 72, 72, axis=0))
    left, right = jnp.where(c == 0, kept, came), jnp.where(c == 0, came, kept)

    factor = jnp.minimum(1.0, clip_rms * math.sqrt(D * KV) / (jnp.sqrt(norm_sq) + 1e-06))
    weight_a, weight_b = weights_of((near_planes_a, far_planes_a), (near_planes_b, far_planes_b), order_x, factor)
    far_z = exchange(weight_b[None], Z, 2)
    far_z, left, right, factor = lax.optimization_barrier((far_z, left, right, factor))
    new_master, first_unit, second_unit, first_top, second_top = own_results(left, right, state, factor)
    results = (new_master, first_unit, second_unit, first_top.reshape(18, 1), second_top.reshape(18, 1))

    column_a = by_place(weight_a, exchange(weight_a, Z, 0), order_z)
    near_a = doubling_gather(column_a[None], X, 1)
    near_a, results = lax.optimization_barrier((near_a, results))
    near_b = jnp.concatenate([weight_b[None], far_z])
    near_b = jnp.concatenate([near_b, exchange(near_b, Z, 1)])
    far_a, far_b = exchange(near_a, X, 0), exchange(near_b, Z, 0)
    pieces = (near_a, near_b, swap(near_a), swap(near_b), far_a, far_b, swap(far_a), swap(far_b))
    return (written(pieces, orders, c), *results)


def solution(mesh):
    finer = Mesh(mesh.devices.reshape(4, 8, 2, mesh.shape["mp"]), (X, Z, C, Y))
    in_specs = (P(DP, None),) + (P(DP, Y),) * 6
    out_specs = (P(None, Y),) + (P(DP, Y),) * 5
    return jax.shard_map(shards, mesh=finer, in_specs=in_specs, out_specs=out_specs, check_vma=False)
```

time: 160 us -> 152 us (0.950)
  waiting for transfers between devices: 45 us -> 36.1 us
  blocking collectives: 28.3 us -> 20.2 us
  starting transfers between devices: 42.7 us -> 49.4 us
  local copies, waits for them, and re-layouts: 12.1 us -> 8.44 us
  other arithmetic: 6.65 us -> 10.2 us
  Pallas kernels: 21.9 us -> 24.1 us
    ppermute x20, waiting for transfers between devices: 40 us -> 24.4 us  [exchange(): return lax.ppermute(value, (axis, C), pairs)]
    ppermute x20, starting transfers between devices: 22.7 us -> 31.1 us  [exchange(): return lax.ppermute(value, (axis, C), pairs)]
    ppermute x8, starting transfers between devices: 20 us -> 11.7 us  [swap(): return lax.ppermute(value, C, [(0, 1), (1, 0)])]
    all_to_all x2 -> x1, blocking collectives: 28.3 us -> 20.2 us  [summed_over(): return jnp.sum(lax.all_to_all(spread, axes, 0, 0, tiled=True)[:, 0, 0])]
    all_to_all x0 -> x1, waiting for transfers between devices: none -> 6.79 us  [summed_over(): return jnp.sum(lax.all_to_all(spread, axes, 0, 0, tiled=True)[:, 0, 0])]
    all_to_all x0 -> x1, starting transfers between devices: none -> 6.54 us  [summed_over(): return jnp.sum(lax.all_to_all(spread, axes, 0, 0, tiled=True)[:, 0, 0])]
    unnamed x28 -> x14, local copies, waits for them, and re-layouts: 9.53 us -> 5.26 us
    pallas_call x2 -> x3, Pallas kernels: 6 us -> 8.21 us  [packed(): pl.pallas_call(kernel, in_specs=[smem, smem] + [vmem] * 4, out_specs=[vme...]
  transfers between devices with their start and end apart: 28 -> 29, of which waited for: 16 -> 15; matrix products, arithmetic and copies ran while one was open for 5% -> 8% of each run, Pallas kernels for 5% -> 4%
where the time goes in v2:
time: 152 us
  starting transfers between devices  49.4 us (32%)
  waiting for transfers between devices  36.1 us (24%)
  Pallas kernels  24.1 us (16%)
  blocking collectives  20.2 us (13%)
  other arithmetic  10.2 us (7%)
  local copies, waits for them, and re-layouts  8.44 us (6%)
  between operations  3.21 us (2%)
    ppermute x20, starting transfers between devices, exchange(): return lax.ppermute(value, (axis, C), pairs)  31.1 us
    ppermute x20, waiting for transfers between devices, exchange(): return lax.ppermute(value, (axis, C), pairs)  24.4 us
    all_to_all x1, blocking collectives, summed_over(): return jnp.sum(lax.all_to_all(spread, axes, 0, 0, tiled=True)[:, 0, 0])  20.2 us
    ppermute x8, starting transfers between devices, swap(): return lax.ppermute(value, C, [(0, 1), (1, 0)])  11.7 us
    pallas_call x2, Pallas kernels, products(): pl.pallas_call(kernel, in_specs=[smem, anywhere, anywhere], out_specs=[vm...  10.4 us
    pallas_call x3, Pallas kernels, packed(): pl.pallas_call(kernel, in_specs=[smem, smem] + [vmem] * 4, out_specs=[vme...  8.21 us
    all_to_all x1, waiting for transfers between devices, summed_over(): return jnp.sum(lax.all_to_all(spread, axes, 0, 0, tiled=True)[:, 0, 0])  6.79 us
    all_to_all x1, starting transfers between devices, summed_over(): return jnp.sum(lax.all_to_all(spread, axes, 0, 0, tiled=True)[:, 0, 0])  6.54 us
  transfers between devices with their start and end apart: 29, of which 15 were waited for; matrix products, arithmetic and copies ran while one was open for 8% of the time, Pallas kernels for 4%

profile of v2, /device:TPU:1, one launch (start us, length us, event | category | flops | bytes accessed | tf_op | source)
XLA Modules:
  0.0 151.7 jit_solution(12156359575276806801)
XLA Ops:
  0.6 1.1 copy-done.3
  1.8 5.1 %shard_map.154 = (f32[2304,256]{1,0:T(8,128)}, f32[2304,256]{1,0:T(8,128)S(1)}) custom-call(s32[1]{0:T(128)} %bitcast.4.me, bf16[768,4608]{1,0:T(8,128)(2,1)} %a.3, bf16[768,512]{1,0:T(8,128)(2,1)S(1)} %copy-done.3), custom_call_target="tpu_custom_call" | custom-call | flops 1811939328 | bytes 9437184 | tf_op jit(solution)/shard_map/pallas_call | solution.py:100
  6.9 3.3 %collective-permute-start = (f32[2304,256]{1,0:T(8,128)}, f32[2304,256]{1,0:T(8,128)}, u32[]{:S(2)}, u32[]{:S(2)}) collective-permute-start(f32[2304,256]{1,0:T(8,128)} %get-tuple-element.48), channel_id=1, source_target_pairs={{0,4},{4,0},{1,5},{5,1},{2,6},{6,2},{3,7},{7,3},{8,12},{12,8},{9,1... | collective-permute-start | bytes 7077896 | tf_op jit(solution)/shard_map/ppermute | solution.py:38
  10.2 5.2 %shard_map.155 = (f32[2304,256]{1,0:T(8,128)}, f32[2304,256]{1,0:T(8,128)S(1)}) custom-call(s32[1]{0:T(128)} %bitcast.4.me, bf16[768,4608]{1,0:T(8,128)(2,1)} %a.3, bf16[768,512]{1,0:T(8,128)(2,1)S(1)} %copy-done.3), custom_call_target="tpu_custom_call" | custom-call | flops 1811939328 | bytes 9437184 | tf_op jit(solution)/shard_map/pallas_call | solution.py:100
  15.5 1.4 copy-done
  16.9 0.8 fusion.14
  17.7 0.8 fusion.15
  18.5 3.3 %collective-permute-done.1.q1 = f32[2304,256]{1,0:T(8,128)} collective-permute-done((f32[2304,256]{1,0:T(8,128)}, f32[2304,256]{1,0:T(8,128)}, u32[]{:S(2)}, u32[]{:S(2)}) %collective-permute-start.1) | collective-permute-done | bytes 2359328 | tf_op jit(solution)/shard_map/ppermute | solution.py:38
  21.8 1.7 %copy-done.1 = f32[2304,256]{1,0:T(8,128)S(1)} copy-done((f32[2304,256]{1,0:T(8,128)S(1)}, f32[2304,256]{1,0:T(8,128)}, u32[]{:S(2)}) %copy-start.1) | copy-done | bytes 2359320
  23.5 2.8 %shard_map.156 = f32[4,4,144,128]{3,2,1,0:T(8,128)S(1)} custom-call(s32[4]{0:T(128)S(1)} %get-tuple-element.99.ox, s32[8]{0:T(128)S(1)} %get-tuple-element.97.oz.o, f32[2304,256]{1,0:T(8,128)S(1)} %get-tuple-element.52.p0, f32[2304,256]{1,0:T(8,128)S(1)} %copy-done.1, f32[2304,256]{1,0:T(8,128)} %collective-permute-done.q0, ...), custom_call_target="tpu_custom_call" | custom-call | flops 1024 | bytes 4096 | tf_op jit(solution)/shard_map/pallas_call | solution.py:131
  26.3 0.9 multiply_convert_fusion.1
  27.2 2.6 %shard_map.157 = f32[2,8,144,128]{3,2,1,0:T(8,128)S(1)} custom-call(s32[4]{0:T(128)S(1)} %get-tuple-element.99.ox, s32[8]{0:T(128)S(1)} %get-tuple-element.97.oz.o, f32[2304,256]{1,0:T(8,128)S(1)} %get-tuple-element.52.p0, f32[2304,256]{1,0:T(8,128)S(1)} %copy-done.2, f32[2304,256]{1,0:T(8,128)} %collective-permute-done.q0, ...), custom_call_target="tpu_custom_call" | custom-call | flops 1024 | bytes 4096 | tf_op jit(solution)/shard_map/pallas_call | solution.py:131
  29.9 1.0 multiply_convert_fusion
  30.8 2.8 %shard_map.158 = (f32[2,8,144,128]{3,2,1,0:T(8,128)S(1)}, f32[4,4,144,128]{3,2,1,0:T(8,128)S(1)}) custom-call(s32[4]{0:T(128)S(1)} %get-tuple-element.99.ox, s32[8]{0:T(128)S(1)} %get-tuple-element.97.oz.o, f32[2304,256]{1,0:T(8,128)S(1)} %get-tuple-element.52.p0, f32[2304,256]{1,0:T(8,128)S(1)} %copy-done.2, f32[2304,256]{1,0:T(8,128)} %collective-permute-done.q0, ...), custom_call_target="tpu_custom_call" | custom-call | flops 1024 | bytes 4096 | tf_op jit(solution)/shard_map/pallas_call | solution.py:131
  33.6 1.0 copy-done.4
  34.6 0.9 collective-permute-start.2
  35.7 0.7 multiply_bitcast_fusion.3
  36.5 1.1 multiply_bitcast_fusion
  37.6 0.9 pad_maximum_fusion.4.state
  38.7 5.7 %collective-permute-start.9 = (f16[4,4,144,128]{3,2,1,0:T(8,128)(2,1)}, f16[4,4,144,128]{3,2,1,0:T(8,128)(2,1)S(1)}, u32[]{:S(2)}, u32[]{:S(2)}) collective-permute-start(f16[4,4,144,128]{3,2,1,0:T(8,128)(2,1)} %multiply_convert_fusion.1), channel_id=1, source_target_pairs={{0,8},{4,60},{8,0},{12,20},{16,24},{20,12},{24,16},{28,36},{32,40}... | collective-permute-start | bytes 1769480 | tf_op jit(solution)/shard_map/ppermute | solution.py:45
  44.5 0.5 collective-permute-done.2
  44.9 1.2 multiply_add_fusion.1
  46.3 5.9 %collective-permute-done.9 = f16[4,4,144,128]{3,2,1,0:T(8,128)(2,1)S(1)} collective-permute-done((f16[4,4,144,128]{3,2,1,0:T(8,128)(2,1)}, f16[4,4,144,128]{3,2,1,0:T(8,128)(2,1)S(1)}, u32[]{:S(2)}, u32[]{:S(2)}) %collective-permute-start.9) | collective-permute-done | bytes 589856 | tf_op jit(solution)/shard_map/ppermute | solution.py:45
  52.6 3.6 %collective-permute-start.5 = (f16[4,144,128]{2,1,0:T(8,128)(2,1)S(1)}, f16[4,144,128]{2,1,0:T(8,128)(2,1)S(1)}, u32[]{:S(2)}, u32[]{:S(2)}) collective-permute-start(f16[4,144,128]{2,1,0:T(8,128)(2,1)S(1)} %multiply_convert_fusion.2), channel_id=1, source_target_pairs={{0,8},{4,60},{8,0},{12,20},{16,24},{20,12},{24,16},{28,36},{32,40}... | collective-permute-start | bytes 442376 | tf_op jit(solution)/shard_map/ppermute | solution.py:45
  56.2 2.1 %collective-permute-done.10 = f16[2,4,144,128]{3,2,1,0:T(8,128)(2,1)S(1)} collective-permute-done((f16[2,4,144,128]{3,2,1,0:T(8,128)(2,1)S(1)}, f16[2,4,144,128]{3,2,1,0:T(8,128)(2,1)S(1)}, u32[]{:S(2)}, u32[]{:S(2)}) %collective-permute-start.10) | collective-permute-done | bytes 294944 | tf_op jit(solution)/shard_map/ppermute | solution.py:45
  58.4 2.9 %collective-permute-start.11 = (f16[1,4,144,128]{3,2,1,0:T(8,128)(2,1)S(1)}, f16[1,4,144,128]{3,2,1,0:T(8,128)(2,1)S(1)}, u32[]{:S(2)}, u32[]{:S(2)}) collective-permute-start(f16[1,4,144,128]{3,2,1,0:T(8,128)(2,1)S(1)} %fusion.3), channel_id=1, source_target_pairs={{0,24},{4,44},{8,48},{12,36},{16,40},{20,60},{24,0},{28,52},{32,56... | collective-permute-start | bytes 442376 | tf_op jit(solution)/shard_map/ppermute | solution.py:45
  61.5 1.5 %collective-permute-start.6 = (f16[2,144,128]{2,1,0:T(8,128)(2,1)S(1)}, f16[2,144,128]{2,1,0:T(8,128)(2,1)S(1)}, u32[]{:S(2)}, u32[]{:S(2)}) collective-permute-start(f16[2,144,128]{2,1,0:T(8,128)(2,1)S(1)} %fusion.6), channel_id=1, source_target_pairs={{0,56},{4,12},{8,16},{12,4},{16,8},{20,28},{24,32},{28,20},{32,24}... | collective-permute-start | bytes 221192 | tf_op jit(solution)/shard_map/ppermute | solution.py:45
  63.0 2.5 %collective-permute-done.11 = f16[1,4,144,128]{3,2,1,0:T(8,128)(2,1)S(1)} collective-permute-done((f16[1,4,144,128]{3,2,1,0:T(8,128)(2,1)S(1)}, f16[1,4,144,128]{3,2,1,0:T(8,128)(2,1)S(1)}, u32[]{:S(2)}, u32[]{:S(2)}) %collective-permute-start.11) | collective-permute-done | bytes 147488 | tf_op jit(solution)/shard_map/ppermute | solution.py:45
  65.6 1.1 collective-permute-start.12
  66.8 2.6 %collective-permute-start.7 = (f16[1,144,128]{2,1,0:T(8,128)(2,1)S(1)}, f16[1,144,128]{2,1,0:T(8,128)(2,1)S(1)}, u32[]{:S(2)}, u32[]{:S(2)}) collective-permute-start(f16[1,144,128]{2,1,0:T(8,128)(2,1)S(1)} %fusion.11), channel_id=1, source_target_pairs={{0,24},{4,44},{8,48},{12,36},{16,40},{20,60},{24,0},{28,52},{32,56... | collective-permute-start | bytes 110600 | tf_op jit(solution)/shard_map/ppermute | solution.py:45
  69.4 0.9 collective-permute-done.12
  70.4 2.3 %collective-permute-done.7 = f16[1,144,128]{2,1,0:T(8,128)(2,1)S(1)} collective-permute-done((f16[1,144,128]{2,1,0:T(8,128)(2,1)S(1)}, f16[1,144,128]{2,1,0:T(8,128)(2,1)S(1)}, u32[]{:S(2)}, u32[]{:S(2)}) %collective-permute-start.7) | collective-permute-done | bytes 36896 | tf_op jit(solution)/shard_map/ppermute | solution.py:45
  72.7 0.6 multiply_reduce_fusion.1
  73.3 2.6 %collective-permute-start.8 = (f32[1,4,144,128]{3,2,1,0:T(8,128)S(1)}, f32[1,4,144,128]{3,2,1,0:T(8,128)S(1)}, u32[]{:S(2)}, u32[]{:S(2)}) collective-permute-start(f32[1,4,144,128]{3,2,1,0:T(8,128)S(1)} %maximum_bitcast_fusion), channel_id=1, source_target_pairs={{0,24},{4,44},{8,48},{12,36},{16,40},{20,60},{24,0},{28,52},{32,56... | collective-permute-start | bytes 884744 | tf_op jit(solution)/shard_map/ppermute | solution.py:45
  76.0 0.6 multiply_reduce_fusion
  76.6 0.4 collective-permute-start.14
  78.3 20.2 %all_to_all.10 = f32[16,8,128]{2,1,0:T(8,128)S(1)} all-to-all(f32[16,8,128]{2,1,0:T(8,128)S(1)} %broadcast_in_dim.29), channel_id=1, replica_groups=mesh['dp_0'=4,'dp_1'=8,'dp_2'=2,'mp'=4] {'dp_1','dp_2'}, dimensions={0} | all-to-all | bytes 131072 | tf_op jit(solution)/shard_map/all_to_all | solution.py:176
  98.5 0.6 slice_reduce_fusion.1
  99.3 1.0 pad_maximum_fusion.1.b0
  100.3 0.2 collective-permute-start.16
  100.5 1.3 broadcast_in_dim.30
  101.8 6.5 %all-to-all-start.1 = ((f32[16,8,128]{2,1,0:T(8,128)}), f32[16,8,128]{2,1,0:T(8,128)S(1)}, u32[]{:S(2)}, u32[]{:S(2)}) async-start(f32[16,8,128]{2,1,0:T(8,128)} %broadcast_in_dim.30), calls=%async_computation.1 | async-start | bytes 131072 | tf_op jit(solution)/shard_map/all_to_all | solution.py:176
  108.4 6.8 %all-to-all-done.1 = f32[16,8,128]{2,1,0:T(8,128)S(1)} async-done(((f32[16,8,128]{2,1,0:T(8,128)}), f32[16,8,128]{2,1,0:T(8,128)S(1)}, u32[]{:S(2)}, u32[]{:S(2)}) %all-to-all-start.1) | async-done | bytes 65568 | tf_op jit(solution)/shard_map/all_to_all | solution.py:176
  115.2 0.6 slice_reduce_fusion
  116.5 1.0 shard_map.159
  117.6 0.4 collective-permute-start.17
  118.0 1.0 collective-permute-start.20
  119.0 3.6 %collective-permute-start.19 = (bf16[1,4,144,128]{3,2,1,0:T(8,128)(2,1)S(1)}, bf16[1,4,144,128]{3,2,1,0:T(8,128)(2,1)S(1)}, u32[]{:S(2)}, u32[]{:S(2)}) collective-permute-start(bf16[1,4,144,128]{3,2,1,0:T(8,128)(2,1)S(1)} %bitcast.43), channel_id=1, source_target_pairs={{0,24},{4,44},{8,48},{12,36},{16,40},{20,60},{24,0},{28,52},{32,56... | collective-permute-start | bytes 442376 | tf_op jit(solution)/shard_map/ppermute | solution.py:45
  122.6 0.3 collective-permute-done.17.b
  122.8 0.6 shard_map.160
  123.4 0.3 collective-permute-start.18
  123.7 4.0 %collective-permute-done.19 = bf16[1,4,144,128]{3,2,1,0:T(8,128)(2,1)S(1)} collective-permute-done((bf16[1,4,144,128]{3,2,1,0:T(8,128)(2,1)S(1)}, bf16[1,4,144,128]{3,2,1,0:T(8,128)(2,1)S(1)}, u32[]{:S(2)}, u32[]{:S(2)}) %collective-permute-start.19) | collective-permute-done | bytes 147488 | tf_op jit(solution)/shard_map/ppermute | solution.py:45
  127.8 1.0 shard_map.161
  128.8 0.6 collective-permute-done.18
  129.4 1.4 collective-permute-start.24
  130.8 2.9 %collective-permute-done.21 = bf16[2,4,144,128]{3,2,1,0:T(8,128)(2,1)S(1)} collective-permute-done((bf16[2,4,144,128]{3,2,1,0:T(8,128)(2,1)S(1)}, bf16[2,4,144,128]{3,2,1,0:T(8,128)(2,1)S(1)}, u32[]{:S(2)}, u32[]{:S(2)}) %collective-permute-start.21) | collective-permute-done | bytes 294944 | tf_op jit(solution)/shard_map/ppermute | solution.py:45
  133.8 3.3 %collective-permute-start.25 = (bf16[4,4,144,128]{3,2,1,0:T(8,128)(2,1)S(1)}, bf16[4,4,144,128]{3,2,1,0:T(8,128)(2,1)S(1)}, u32[]{:S(2)}, u32[]{:S(2)}) collective-permute-start(bf16[4,4,144,128]{3,2,1,0:T(8,128)(2,1)S(1)} %pad_maximum_fusion.3.rest_1_), channel_id=1, source_target_pairs={{0,8},{4,60},{8,0},{12,20},{16,24},{20,12},{24,16},{28,36},{32,40}... | collective-permute-start | bytes 1769480 | tf_op jit(solution)/shard_map/ppermute | solution.py:45
  137.1 2.0 %collective-permute-start.22 = (bf16[2,8,144,128]{3,2,1,0:T(8,128)(2,1)S(1)}, bf16[2,8,144,128]{3,2,1,0:T(8,128)(2,1)S(1)}, u32[]{:S(2)}, u32[]{:S(2)}) collective-permute-start(bf16[2,8,144,128]{3,2,1,0:T(8,128)(2,1)S(1)} %pad_maximum_fusion.2.rest_0_), channel_id=1, source_target_pairs={{0,4},{4,0},{1,5},{5,1},{2,6},{6,2},{3,7},{7,3},{8,12},{12,8},{9,1... | collective-permute-start | bytes 1769480 | tf_op jit(solution)/shard_map/ppermute | solution.py:38
  139.1 0.4 collective-permute-done.24.rest_4_
  139.5 2.7 %collective-permute-start.26 = (bf16[2,8,144,128]{3,2,1,0:T(8,128)(2,1)S(1)}, bf16[2,8,144,128]{3,2,1,0:T(8,128)(2,1)S(1)}, u32[]{:S(2)}, u32[]{:S(2)}) collective-permute-start(bf16[2,8,144,128]{3,2,1,0:T(8,128)(2,1)S(1)} %collective-permute-done.24.rest_4_), channel_id=1, source_target_pairs={{0,4},{4,0},{1,5},{5,1},{2,6},{6,2},{3,7},{7,3},{8,12},{12,8},{9,1... | collective-permute-start | bytes 1769480 | tf_op jit(solution)/shard_map/ppermute | solution.py:38
  142.2 2.2 %collective-permute-done.25.rest_5_ = bf16[4,4,144,128]{3,2,1,0:T(8,128)(2,1)S(1)} collective-permute-done((bf16[4,4,144,128]{3,2,1,0:T(8,128)(2,1)S(1)}, bf16[4,4,144,128]{3,2,1,0:T(8,128)(2,1)S(1)}, u32[]{:S(2)}, u32[]{:S(2)}) %collective-permute-start.25) | collective-permute-done | bytes 589856 | tf_op jit(solution)/shard_map/ppermute | solution.py:45
  144.4 2.6 %collective-permute-start.27 = (bf16[4,4,144,128]{3,2,1,0:T(8,128)(2,1)S(1)}, bf16[4,4,144,128]{3,2,1,0:T(8,128)(2,1)S(1)}, u32[]{:S(2)}, u32[]{:S(2)}) collective-permute-start(bf16[4,4,144,128]{3,2,1,0:T(8,128)(2,1)S(1)} %collective-permute-done.25.rest_5_), channel_id=1, source_target_pairs={{0,4},{4,0},{1,5},{5,1},{2,6},{6,2},{3,7},{7,3},{8,12},{12,8},{9,1... | collective-permute-start | bytes 1769480 | tf_op jit(solution)/shard_map/ppermute | solution.py:38
  146.9 1.6 %collective-permute-done.27.rest_7_ = bf16[4,4,144,128]{3,2,1,0:T(8,128)(2,1)S(1)} collective-permute-done((bf16[4,4,144,128]{3,2,1,0:T(8,128)(2,1)S(1)}, bf16[4,4,144,128]{3,2,1,0:T(8,128)(2,1)S(1)}, u32[]{:S(2)}, u32[]{:S(2)}) %collective-permute-start.27) | collective-permute-done | bytes 589856 | tf_op jit(solution)/shard_map/ppermute | solution.py:38
  148.6 2.9 %shard_map.162 = bf16[4,8,144,512]{3,2,1,0:T(8,128)(2,1)} custom-call(s32[4]{0:T(128)S(1)} %get-tuple-element.99.ox, s32[8]{0:T(128)S(1)} %get-tuple-element.97.oz.o, s32[4]{0:T(128)S(1)} %get-tuple-element.98.px, s32[8]{0:T(128)S(1)} %get-tuple-element.96.pz, s32[1]{0:T(128)} %bitcast.4.me, bf16[2,8,144,128]{3,2,1,0:T(8,128)(2,1)S(1)} %pad_maximum_fusion.2.rest_0_, ...), custom_call_target="tpu_custom_call" | custom-call | flops 1024 | bytes 4096 | tf_op jit(solution)/shard_map/pallas_call | solution.py:163
  (65 shorter events, 2.0 us)
Async XLA Ops:
  0.6 1.1 copy-start.3
  6.9 11.5 %collective-permute-start = (f32[2304,256]{1,0:T(8,128)}, f32[2304,256]{1,0:T(8,128)}, u32[]{:S(2)}, u32[]{:S(2)}) collective-permute-start(f32[2304,256]{1,0:T(8,128)} %get-tuple-element.48), channel_id=1, source_target_pairs={{0,4},{4,0},{1,5},{5,1},{2,6},{6,2},{3,7},{7,3},{8,12},{12,8},{9,1... | collective-permute-start | bytes 7077896 | tf_op jit(solution)/shard_map/ppermute | solution.py:38
  15.5 1.5 copy-start
  16.9 4.9 %collective-permute-start.1 = (f32[2304,256]{1,0:T(8,128)}, f32[2304,256]{1,0:T(8,128)}, u32[]{:S(2)}, u32[]{:S(2)}) collective-permute-start(f32[2304,256]{1,0:T(8,128)} %get-tuple-element.49), channel_id=1, source_target_pairs={{0,4},{4,0},{1,5},{5,1},{2,6},{6,2},{3,7},{7,3},{8,12},{12,8},{9,1... | collective-permute-start | bytes 7077896 | tf_op jit(solution)/shard_map/ppermute | solution.py:38
  21.8 1.7 %copy-start.1 = (f32[2304,256]{1,0:T(8,128)S(1)}, f32[2304,256]{1,0:T(8,128)}, u32[]{:S(2)}) copy-start(f32[2304,256]{1,0:T(8,128)} %copy-done) | copy-start | bytes 7077892
  23.5 3.8 %copy-start.2 = (f32[2304,256]{1,0:T(8,128)S(1)}, f32[2304,256]{1,0:T(8,128)}, u32[]{:S(2)}) copy-start(f32[2304,256]{1,0:T(8,128)} %copy-done) | copy-start | bytes 7077892
  30.8 4.7 %copy-start.6 = (f32[18,1]{0,1:T(1,128)S(1)}, f32[18,1]{0,1:T(1,128)}, u32[]{:S(2)}) copy-start(f32[18,1]{0,1:T(1,128)} %param.17) | copy-start | bytes 220
  33.6 1.0 copy-start.4
  34.6 10.3 %collective-permute-start.2 = (f16[2,8,144,128]{3,2,1,0:T(8,128)(2,1)}, f16[2,8,144,128]{3,2,1,0:T(8,128)(2,1)}, u32[]{:S(2)}, u32[]{:S(2)}) collective-permute-start(f16[2,8,144,128]{3,2,1,0:T(8,128)(2,1)} %multiply_convert_fusion), channel_id=1, source_target_pairs={{0,64},{4,196},{64,0},{68,132},{128,192},{132,68},{192,128},{196,4... | collective-permute-start | bytes 1769480 | tf_op jit(solution)/shard_map/ppermute | solution.py:45
  38.6 6.4 %copy-start.5 = (f32[2,8,144,128]{3,2,1,0:T(8,128)S(1)}, f32[2,8,144,128]{3,2,1,0:T(8,128)}, u32[]{:S(2)}) copy-start(f32[2,8,144,128]{3,2,1,0:T(8,128)} %copy-done.4) | copy-start | bytes 3538948
  38.6 5.8 %collective-permute-start.4 = (f32[3,72,256]{2,1,0:T(8,128)S(1)}, f32[3,72,256]{2,1,0:T(8,128)S(1)}, u32[]{:S(2)}, u32[]{:S(2)}) collective-permute-start(f32[3,72,256]{2,1,0:T(8,128)S(1)} %constant_dynamic-slice_fusion), channel_id=1, source_target_pairs={{0,4},{4,0},{1,5},{5,1},{2,6},{6,2},{3,7},{7,3},{8,12},{12,8},{9,1... | collective-permute-start | bytes 663560 | tf_op jit(solution)/shard_map/ppermute | solution.py:38
  38.7 13.4 %collective-permute-start.9 = (f16[4,4,144,128]{3,2,1,0:T(8,128)(2,1)}, f16[4,4,144,128]{3,2,1,0:T(8,128)(2,1)S(1)}, u32[]{:S(2)}, u32[]{:S(2)}) collective-permute-start(f16[4,4,144,128]{3,2,1,0:T(8,128)(2,1)} %multiply_convert_fusion.1), channel_id=1, source_target_pairs={{0,8},{4,60},{8,0},{12,20},{16,24},{20,12},{24,16},{28,36},{32,40}... | collective-permute-start | bytes 1769480 | tf_op jit(solution)/shard_map/ppermute | solution.py:45
  46.2 6.3 %collective-permute-start.3 = (f16[1,8,144,128]{3,2,1,0:T(8,128)(2,1)S(1)}, f16[1,8,144,128]{3,2,1,0:T(8,128)(2,1)S(1)}, u32[]{:S(2)}, u32[]{:S(2)}) collective-permute-start(f16[1,8,144,128]{3,2,1,0:T(8,128)(2,1)S(1)} %fusion.1), channel_id=1, source_target_pairs={{0,192},{4,68},{64,128},{68,4},{128,64},{132,196},{192,0},{196,132... | collective-permute-start | bytes 884744 | tf_op jit(solution)/shard_map/ppermute | solution.py:45
  52.4 6.0 %collective-permute-start.10 = (f16[2,4,144,128]{3,2,1,0:T(8,128)(2,1)S(1)}, f16[2,4,144,128]{3,2,1,0:T(8,128)(2,1)S(1)}, u32[]{:S(2)}, u32[]{:S(2)}) collective-permute-start(f16[2,4,144,128]{3,2,1,0:T(8,128)(2,1)S(1)} %fusion), channel_id=1, source_target_pairs={{0,56},{4,12},{8,16},{12,4},{16,8},{20,28},{24,32},{28,20},{32,24}... | collective-permute-start | bytes 884744 | tf_op jit(solution)/shard_map/ppermute | solution.py:45
  52.6 8.8 %collective-permute-start.5 = (f16[4,144,128]{2,1,0:T(8,128)(2,1)S(1)}, f16[4,144,128]{2,1,0:T(8,128)(2,1)S(1)}, u32[]{:S(2)}, u32[]{:S(2)}) collective-permute-start(f16[4,144,128]{2,1,0:T(8,128)(2,1)S(1)} %multiply_convert_fusion.2), channel_id=1, source_target_pairs={{0,8},{4,60},{8,0},{12,20},{16,24},{20,12},{24,16},{28,36},{32,40}... | collective-permute-start | bytes 442376 | tf_op jit(solution)/shard_map/ppermute | solution.py:45
  58.4 7.1 %collective-permute-start.11 = (f16[1,4,144,128]{3,2,1,0:T(8,128)(2,1)S(1)}, f16[1,4,144,128]{3,2,1,0:T(8,128)(2,1)S(1)}, u32[]{:S(2)}, u32[]{:S(2)}) collective-permute-start(f16[1,4,144,128]{3,2,1,0:T(8,128)(2,1)S(1)} %fusion.3), channel_id=1, source_target_pairs={{0,24},{4,44},{8,48},{12,36},{16,40},{20,60},{24,0},{28,52},{32,56... | collective-permute-start | bytes 442376 | tf_op jit(solution)/shard_map/ppermute | solution.py:45
  61.5 5.3 %collective-permute-start.6 = (f16[2,144,128]{2,1,0:T(8,128)(2,1)S(1)}, f16[2,144,128]{2,1,0:T(8,128)(2,1)S(1)}, u32[]{:S(2)}, u32[]{:S(2)}) collective-permute-start(f16[2,144,128]{2,1,0:T(8,128)(2,1)S(1)} %fusion.6), channel_id=1, source_target_pairs={{0,56},{4,12},{8,16},{12,4},{16,8},{20,28},{24,32},{28,20},{32,24}... | collective-permute-start | bytes 221192 | tf_op jit(solution)/shard_map/ppermute | solution.py:45
  65.6 4.7 %collective-permute-start.12 = (f16[2,144,128]{2,1,0:T(8,128)(2,1)S(1)}, f16[2,144,128]{2,1,0:T(8,128)(2,1)S(1)}, u32[]{:S(2)}, u32[]{:S(2)}) collective-permute-start(f16[2,144,128]{2,1,0:T(8,128)(2,1)S(1)} %fusion.7), channel_id=1, source_target_pairs={{0,64},{4,196},{64,0},{68,132},{128,192},{132,68},{192,128},{196,4... | collective-permute-start | bytes 221192 | tf_op jit(solution)/shard_map/ppermute | solution.py:45
  66.8 5.9 %collective-permute-start.7 = (f16[1,144,128]{2,1,0:T(8,128)(2,1)S(1)}, f16[1,144,128]{2,1,0:T(8,128)(2,1)S(1)}, u32[]{:S(2)}, u32[]{:S(2)}) collective-permute-start(f16[1,144,128]{2,1,0:T(8,128)(2,1)S(1)} %fusion.11), channel_id=1, source_target_pairs={{0,24},{4,44},{8,48},{12,36},{16,40},{20,60},{24,0},{28,52},{32,56... | collective-permute-start | bytes 110600 | tf_op jit(solution)/shard_map/ppermute | solution.py:45
  70.3 5.6 %collective-permute-start.13 = (f16[1,144,128]{2,1,0:T(8,128)(2,1)S(1)}, f16[1,144,128]{2,1,0:T(8,128)(2,1)S(1)}, u32[]{:S(2)}, u32[]{:S(2)}) collective-permute-start(f16[1,144,128]{2,1,0:T(8,128)(2,1)S(1)} %fusion.10), channel_id=1, source_target_pairs={{0,192},{4,68},{64,128},{68,4},{128,64},{132,196},{192,0},{196,132... | collective-permute-start | bytes 110600 | tf_op jit(solution)/shard_map/ppermute | solution.py:45
  73.3 25.8 %collective-permute-start.8 = (f32[1,4,144,128]{3,2,1,0:T(8,128)S(1)}, f32[1,4,144,128]{3,2,1,0:T(8,128)S(1)}, u32[]{:S(2)}, u32[]{:S(2)}) collective-permute-start(f32[1,4,144,128]{3,2,1,0:T(8,128)S(1)} %maximum_bitcast_fusion), channel_id=1, source_target_pairs={{0,24},{4,44},{8,48},{12,36},{16,40},{20,60},{24,0},{28,52},{32,56... | collective-permute-start | bytes 884744 | tf_op jit(solution)/shard_map/ppermute | solution.py:45
  76.6 22.5 %collective-permute-start.14 = (f32[1,4,144,128]{3,2,1,0:T(8,128)S(1)}, f32[1,4,144,128]{3,2,1,0:T(8,128)}, u32[]{:S(2)}, u32[]{:S(2)}) collective-permute-start(f32[1,4,144,128]{3,2,1,0:T(8,128)S(1)} %maximum_bitcast_fusion.1), channel_id=1, source_target_pairs={{0,192},{4,68},{64,128},{68,4},{128,64},{132,196},{192,0},{196,132... | collective-permute-start | bytes 884744 | tf_op jit(solution)/shard_map/ppermute | solution.py:45
  99.2 17.3 %collective-permute-start.15 = (f32[2,4,144,128]{3,2,1,0:T(8,128)S(1)}, f32[2,4,144,128]{3,2,1,0:T(8,128)S(1)}, u32[]{:S(2)}, u32[]{:S(2)}) collective-permute-start(f32[2,4,144,128]{3,2,1,0:T(8,128)S(1)} %pad_maximum_fusion.a0), channel_id=1, source_target_pairs={{0,56},{4,12},{8,16},{12,4},{16,8},{20,28},{24,32},{28,20},{32,24}... | collective-permute-start | bytes 1769480 | tf_op jit(solution)/shard_map/ppermute | solution.py:45
  100.3 16.2 %collective-permute-start.16 = (f32[2,4,144,128]{3,2,1,0:T(8,128)S(1)}, f32[2,4,144,128]{3,2,1,0:T(8,128)S(1)}, u32[]{:S(2)}, u32[]{:S(2)}) collective-permute-start(f32[2,4,144,128]{3,2,1,0:T(8,128)S(1)} %pad_maximum_fusion.1.b0), channel_id=1, source_target_pairs={{0,64},{4,196},{64,0},{68,132},{128,192},{132,68},{192,128},{196,4... | collective-permute-start | bytes 1769480 | tf_op jit(solution)/shard_map/ppermute | solution.py:45
  101.8 13.3 %all-to-all-start.1 = ((f32[16,8,128]{2,1,0:T(8,128)}), f32[16,8,128]{2,1,0:T(8,128)S(1)}, u32[]{:S(2)}, u32[]{:S(2)}) async-start(f32[16,8,128]{2,1,0:T(8,128)} %broadcast_in_dim.30), calls=%async_computation.1 | async-start | bytes 131072 | tf_op jit(solution)/shard_map/all_to_all | solution.py:176
  117.6 5.3 %collective-permute-start.17 = (bf16[4,144,128]{2,1,0:T(8,128)(2,1)S(1)}, bf16[4,144,128]{2,1,0:T(8,128)(2,1)S(1)}, u32[]{:S(2)}, u32[]{:S(2)}) collective-permute-start(bf16[4,144,128]{2,1,0:T(8,128)(2,1)S(1)} %get-tuple-element.69.a), channel_id=1, source_target_pairs={{0,8},{4,60},{8,0},{12,20},{16,24},{20,12},{24,16},{28,36},{32,40}... | collective-permute-start | bytes 442376 | tf_op jit(solution)/shard_map/ppermute | solution.py:45
  118.0 5.7 %collective-permute-start.20 = (f32[72,256]{1,0:T(8,128)S(1)}, f32[72,256]{1,0:T(8,128)S(1)}, u32[]{:S(2)}, u32[]{:S(2)}) collective-permute-start(f32[72,256]{1,0:T(8,128)S(1)} %fusion.8), channel_id=1, source_target_pairs={{0,4},{4,0},{1,5},{5,1},{2,6},{6,2},{3,7},{7,3},{8,12},{12,8},{9,1... | collective-permute-start | bytes 221192 | tf_op jit(solution)/shard_map/ppermute | solution.py:38
  119.0 8.7 %collective-permute-start.19 = (bf16[1,4,144,128]{3,2,1,0:T(8,128)(2,1)S(1)}, bf16[1,4,144,128]{3,2,1,0:T(8,128)(2,1)S(1)}, u32[]{:S(2)}, u32[]{:S(2)}) collective-permute-start(bf16[1,4,144,128]{3,2,1,0:T(8,128)(2,1)S(1)} %bitcast.43), channel_id=1, source_target_pairs={{0,24},{4,44},{8,48},{12,36},{16,40},{20,60},{24,0},{28,52},{32,56... | collective-permute-start | bytes 442376 | tf_op jit(solution)/shard_map/ppermute | solution.py:45
  123.4 6.0 %collective-permute-start.18 = (bf16[1,8,144,128]{3,2,1,0:T(8,128)(2,1)S(1)}, bf16[1,8,144,128]{3,2,1,0:T(8,128)(2,1)S(1)}, u32[]{:S(2)}, u32[]{:S(2)}) collective-permute-start(bf16[1,8,144,128]{3,2,1,0:T(8,128)(2,1)S(1)} %bitcast.41), channel_id=1, source_target_pairs={{0,192},{4,68},{64,128},{68,4},{128,64},{132,196},{192,0},{196,132... | collective-permute-start | bytes 884744 | tf_op jit(solution)/shard_map/ppermute | solution.py:45
  127.7 6.0 %collective-permute-start.21 = (bf16[2,4,144,128]{3,2,1,0:T(8,128)(2,1)S(1)}, bf16[2,4,144,128]{3,2,1,0:T(8,128)(2,1)S(1)}, u32[]{:S(2)}, u32[]{:S(2)}) collective-permute-start(bf16[2,4,144,128]{3,2,1,0:T(8,128)(2,1)S(1)} %pad_maximum_fusion.6), channel_id=1, source_target_pairs={{0,56},{4,12},{8,16},{12,4},{16,8},{20,28},{24,32},{28,20},{32,24}... | collective-permute-start | bytes 884744 | tf_op jit(solution)/shard_map/ppermute | solution.py:45
  129.4 10.0 %collective-permute-start.24 = (bf16[2,8,144,128]{3,2,1,0:T(8,128)(2,1)S(1)}, bf16[2,8,144,128]{3,2,1,0:T(8,128)(2,1)S(1)}, u32[]{:S(2)}, u32[]{:S(2)}) collective-permute-start(bf16[2,8,144,128]{3,2,1,0:T(8,128)(2,1)S(1)} %pad_maximum_fusion.2.rest_0_), channel_id=1, source_target_pairs={{0,64},{4,196},{64,0},{68,132},{128,192},{132,68},{192,128},{196,4... | collective-permute-start | bytes 1769480 | tf_op jit(solution)/shard_map/ppermute | solution.py:45
  133.8 10.6 %collective-permute-start.25 = (bf16[4,4,144,128]{3,2,1,0:T(8,128)(2,1)S(1)}, bf16[4,4,144,128]{3,2,1,0:T(8,128)(2,1)S(1)}, u32[]{:S(2)}, u32[]{:S(2)}) collective-permute-start(bf16[4,4,144,128]{3,2,1,0:T(8,128)(2,1)S(1)} %pad_maximum_fusion.3.rest_1_), channel_id=1, source_target_pairs={{0,8},{4,60},{8,0},{12,20},{16,24},{20,12},{24,16},{28,36},{32,40}... | collective-permute-start | bytes 1769480 | tf_op jit(solution)/shard_map/ppermute | solution.py:45
  137.1 9.8 %collective-permute-start.22 = (bf16[2,8,144,128]{3,2,1,0:T(8,128)(2,1)S(1)}, bf16[2,8,144,128]{3,2,1,0:T(8,128)(2,1)S(1)}, u32[]{:S(2)}, u32[]{:S(2)}) collective-permute-start(bf16[2,8,144,128]{3,2,1,0:T(8,128)(2,1)S(1)} %pad_maximum_fusion.2.rest_0_), channel_id=1, source_target_pairs={{0,4},{4,0},{1,5},{5,1},{2,6},{6,2},{3,7},{7,3},{8,12},{12,8},{9,1... | collective-permute-start | bytes 1769480 | tf_op jit(solution)/shard_map/ppermute | solution.py:38
  139.1 7.9 %collective-permute-start.23 = (bf16[4,4,144,128]{3,2,1,0:T(8,128)(2,1)S(1)}, bf16[4,4,144,128]{3,2,1,0:T(8,128)(2,1)S(1)}, u32[]{:S(2)}, u32[]{:S(2)}) collective-permute-start(bf16[4,4,144,128]{3,2,1,0:T(8,128)(2,1)S(1)} %pad_maximum_fusion.3.rest_1_), channel_id=1, source_target_pairs={{0,4},{4,0},{1,5},{5,1},{2,6},{6,2},{3,7},{7,3},{8,12},{12,8},{9,1... | collective-permute-start | bytes 1769480 | tf_op jit(solution)/shard_map/ppermute | solution.py:38
  139.5 7.5 %collective-permute-start.26 = (bf16[2,8,144,128]{3,2,1,0:T(8,128)(2,1)S(1)}, bf16[2,8,144,128]{3,2,1,0:T(8,128)(2,1)S(1)}, u32[]{:S(2)}, u32[]{:S(2)}) collective-permute-start(bf16[2,8,144,128]{3,2,1,0:T(8,128)(2,1)S(1)} %collective-permute-done.24.rest_4_), channel_id=1, source_target_pairs={{0,4},{4,0},{1,5},{5,1},{2,6},{6,2},{3,7},{7,3},{8,12},{12,8},{9,1... | collective-permute-start | bytes 1769480 | tf_op jit(solution)/shard_map/ppermute | solution.py:38
  144.4 4.2 %collective-permute-start.27 = (bf16[4,4,144,128]{3,2,1,0:T(8,128)(2,1)S(1)}, bf16[4,4,144,128]{3,2,1,0:T(8,128)(2,1)S(1)}, u32[]{:S(2)}, u32[]{:S(2)}) collective-permute-start(bf16[4,4,144,128]{3,2,1,0:T(8,128)(2,1)S(1)} %collective-permute-done.25.rest_5_), channel_id=1, source_target_pairs={{0,4},{4,0},{1,5},{5,1},{2,6},{6,2},{3,7},{7,3},{8,12},{12,8},{9,1... | collective-permute-start | bytes 1769480 | tf_op jit(solution)/shard_map/ppermute | solution.py:38

commit v3 on v2

--- a/solution.py
+++ b/solution.py
@@ -61,12 +61,12 @@
     return (send * (1.0 / terms)).astype(jnp.float16)
 
 
-def halving_sum(send, keep, axis, terms):
+def halving_sum(came, keep, axis, terms):
     for step in range(len(MATES[axis])):
         if step:
             half = keep.shape[0] // 2
-            send, keep = narrowed(keep[half:], terms), keep[:half]
-        keep = keep + exchange(send, axis, step).astype(f32) * float(terms)
+            came, keep = exchange(narrowed(keep[half:], terms), axis, step), keep[:half]
+        keep = keep + came.astype(f32) * float(terms)
         terms *= 2
     return keep[0]
 
@@ -78,64 +78,89 @@
 
 
 def products(inputs, key_cotangent, core, h):
-    width = 1152
-
-    def kernel(me, a, b, theirs, mine, buf, cot, sem):
-        copies = [pltpu.make_async_copy(a.at[:, pl.ds(h * 2304 + i * width, width)], buf.at[i], sem.at[i]) for i in (0, 1)]
+    pieces = ((0, 384), (384, 1152), (1536, 768))
+
+    def kernel(me, a, b, theirs, mine, buf, cot, term, sem):
+        copies = []
         for i, which in ((0, 1 - me[0]), (1, me[0])):
             at = pl.ds(pl.multiple_of(which * 256, 256), 256)
-            copies.append(pltpu.make_async_copy(b.at[:, at], cot.at[:, pl.ds(i * 256, 256)], sem.at[2 + i]))
+            copies.append(pltpu.make_async_copy(b.at[:, at], cot.at[:, pl.ds(i * 256, 256)], sem.at[i]))
+        for i, (at, width) in enumerate(pieces):
+            copies.append(pltpu.make_async_copy(a.at[:, pl.ds(h * 2304 + at, width)], buf.at[:, pl.ds(at, width)], sem.at[2 + i]))
         for copy in copies:
             copy.start()
-        copies[2].wait()
-        copies[3].wait()
-        for i in (0, 1):
-            copies[i].wait()
-            term = lax.dot_general(buf[i], cot[...], (((0,), (0,)), ((), ())), preferred_element_type=f32)
-            theirs[pl.ds(i * width, width), :] = term[:, :256]
-            mine[pl.ds(i * width, width), :] = term[:, 256:]
+        copies[0].wait()
+        copies[1].wait()
+        away = []
+        for i, (at, width) in enumerate(pieces):
+            copies[2 + i].wait()
+            rows = pl.ds(at, width)
+            term[rows, :] = lax.dot_general(buf[:, at : at + width], cot[...], (((0,), (0,)), ((), ())), preferred_element_type=f32)
+            for j, out in enumerate((theirs, mine)):
+                away.append(pltpu.make_async_copy(term.at[rows, pl.ds(j * 256, 256)], out.at[rows, :], sem.at[5 + 2 * i + j]))
+                away[-1].start()
+        for copy in away:
+            copy.wait()
+
+    smem, anywhere = pl.BlockSpec(memory_space=pltpu.SMEM), pl.BlockSpec(memory_space=pl.ANY)
+    return pl.pallas_call(
+        kernel,
+        in_specs=[smem, anywhere, anywhere],
+        out_specs=[anywhere, anywhere],
+        out_shape=[jax.ShapeDtypeStruct((2304, 256), f32)] * 2,
+        scratch_shapes=[
+            pltpu.VMEM((768, 2304), jnp.bfloat16),
+            pltpu.VMEM((768, 512), jnp.bfloat16),
+            pltpu.VMEM((2304, 512), f32),
+            pltpu.SemaphoreType.DMA((11,)),
+        ],
+        compiler_params=pltpu.CompilerParams(vmem_limit_bytes=56 << 20),
+        cost_estimate=pl.CostEstimate(flops=2 * 768 * 2304 * 512, bytes_accessed=9 << 20, transcendentals=0),
+    )(core.reshape(1), inputs, key_cotangent)
+
+
+def packed(mine, theirs, order_x, order_z, h, partly):
+    def kernel(ox, oz, p, q, *rest):
+        outs, held, sem = rest[-6:-2], rest[-2], rest[-1]
+        copies = []
+        for t in (0, 1):
+            rows = pl.ds(t * 1152, 1152)
+            for j, source in enumerate((p, q)):
+                copies.append(pltpu.make_async_copy(source.at[rows, :], held.at[j, rows, :], sem.at[2 * t + j]))
+        for copy in copies:
+            copy.start()
+        if partly:
+            for i in range(4):
+
+                @pl.when(ox[i] // 2 != h)
+                def _(i=i):
+                    outs[0 if i > 1 else 2][i % 2] = rest[0 if i > 1 else 2][i % 2]
+                    outs[1][:, i] = rest[1][:, i]
+                    outs[3][:, i] = rest[3][:, i]
+
+        for t in (0, 1):
+            copies[2 * t].wait()
+            copies[2 * t + 1].wait()
+            for i in range(4):
+
+                @pl.when(ox[i] == 2 * h + t)
+                def _(i=i, t=t):
+                    for j in range(8):
+                        at = pl.ds(pl.multiple_of(t * 1152 + oz[j] * 144, 8), 144)
+                        outs[0 if i > 1 else 2][i % 2, j] = held[0, at, :128] + held[1, at, :128]
+                        outs[1 if j > 3 else 3][j % 4, i] = held[0, at, 128:] + held[1, at, 128:]
 
     smem, vmem = pl.BlockSpec(memory_space=pltpu.SMEM), pl.BlockSpec(memory_space=pltpu.VMEM)
     anywhere = pl.BlockSpec(memory_space=pl.ANY)
     return pl.pallas_call(
         kernel,
-        in_specs=[smem, anywhere, anywhere],
-        out_specs=[vmem, vmem],
-        out_shape=[jax.ShapeDtypeStruct((2304, 256), f32)] * 2,
-        scratch_shapes=[
-            pltpu.VMEM((2, 768, width), jnp.bfloat16),
-            pltpu.VMEM((768, 512), jnp.bfloat16),
-            pltpu.SemaphoreType.DMA((4,)),
-        ],
-        compiler_params=pltpu.CompilerParams(vmem_limit_bytes=46 << 20),
-        cost_estimate=pl.CostEstimate(flops=2 * 768 * 2304 * 512, bytes_accessed=9 << 20, transcendentals=0),
-    )(core.reshape(1), inputs, key_cotangent)
-
-
-def packed(mine, theirs, order_x, order_z, want_a, want_b):
-    def kernel(ox, oz, p0, p1, q0, q1, *outs):
-        for i in range(4):
-            for h, p, q in ((0, p0, q0), (1, p1, q1)):
-
-                @pl.when(ox[i] // 2 == h)
-                def _(i=i, h=h, p=p, q=q):
-                    for j in range(8):
-                        at = pl.ds(pl.multiple_of((ox[i] * 8 - h * 16 + oz[j]) * 144, 8), 144)
-                        if i // 2 == want_a:
-                            outs[0][i % 2, j] = p[at, :128] + q[at, :128]
-                        if j // 4 == want_b:
-                            outs[-1][j % 4, i] = p[at, 128:] + q[at, 128:]
-
-    smem, vmem = pl.BlockSpec(memory_space=pltpu.SMEM), pl.BlockSpec(memory_space=pltpu.VMEM)
-    shapes = [(2, 8, 144, 128)] * (want_a is not None) + [(4, 4, 144, 128)] * (want_b is not None)
-    return pl.pallas_call(
-        kernel,
-        in_specs=[smem, smem] + [vmem] * 4,
-        out_specs=[vmem] * len(shapes),
-        out_shape=[jax.ShapeDtypeStruct(shape, f32) for shape in shapes],
-        compiler_params=pltpu.CompilerParams(vmem_limit_bytes=8 << 20),
-        cost_estimate=pl.CostEstimate(flops=1024, bytes_accessed=4096, transcendentals=0),
-    )(order_x, order_z, *mine, *theirs)
+        in_specs=[smem, smem, anywhere, anywhere] + [vmem] * len(partly),
+        out_specs=[vmem] * 4,
+        out_shape=[jax.ShapeDtypeStruct((2, 8, 144, 128), f32), jax.ShapeDtypeStruct((4, 4, 144, 128), f32)] * 2,
+        scratch_shapes=[pltpu.VMEM((2, 2304, 256), f32), pltpu.SemaphoreType.DMA((4,))],
+        compiler_params=pltpu.CompilerParams(vmem_limit_bytes=50 << 20),
+        cost_estimate=pl.CostEstimate(flops=1024, bytes_accessed=4096, transcendentals=0),
+    )(order_x, order_z, mine, theirs, *partly)
 
 
 def written(pieces, orders, core):
@@ -171,9 +196,36 @@
     )(*orders, core.reshape(1), *pieces).reshape(D, 512)
 
 
-def summed_over(value, axes):
-    spread = jnp.broadcast_to(value, (16, 8, 128))
-    return jnp.sum(lax.all_to_all(spread, axes, 0, 0, tiled=True)[:, 0, 0])
+def spread_squares(grad_a, grad_b):
+    def kernel(a, b, out):
+        out[...] = jnp.full(out.shape, jnp.sum(a[...] * a[...] + b[...] * b[...]), f32)
+
+    return small_call(kernel, 16)(grad_a, grad_b)
+
+
+def spread_sum(parts):
+    def kernel(parts, out):
+        out[...] = jnp.broadcast_to(jnp.sum(parts[:, :1], axis=0, keepdims=True), out.shape)
+
+    return small_call(kernel, 16)(parts)
+
+
+def small_call(kernel, rows):
+    return pl.pallas_call(
+        kernel,
+        out_shape=jax.ShapeDtypeStruct((rows, 8, 128), f32),
+        compiler_params=pltpu.CompilerParams(vmem_limit_bytes=4 << 20),
+        cost_estimate=pl.CostEstimate(flops=1024, bytes_accessed=4096, transcendentals=0),
+    )
+
+
+def met(spread, axes):
+    return lax.all_to_all(spread, axes, 0, 0, tiled=True)
+
+
+def factor_of(parts):
+    norm_sq = jnp.sum(parts[:, 0, :], axis=0, keepdims=True)
+    return jnp.minimum(1.0, clip_rms * math.sqrt(D * KV) / (jnp.sqrt(norm_sq) + 1e-06))
 
 
 def per_row(scale):
@@ -194,22 +246,23 @@
     return master - learn_rate * (step_dir + weight_decay * master)
 
 
-def weights_of(planes_a, planes_b, order_x, factor):
+def weights_of(planes_a, planes_b, order_x, squares):
     def kernel(ox, f, a0, a1, b0, b1, wa, wb):
+        factor = factor_of(f[...])
         for source, out, place in ((a0, wa, (0, 1)), (a1, wa, (2, 3)), (b0, wb, (ox[0], ox[1])), (b1, wb, (ox[2], ox[3]))):
             for j in (0, 1):
-                news = moments(source[j, 0], f[0], source[j, 2], source[j, 3])
+                news = moments(source[j, 0], factor, source[j, 2], source[j, 3])
                 out[place[j]] = stepped(source[j, 1], *news).astype(jnp.bfloat16)
 
     smem, vmem = pl.BlockSpec(memory_space=pltpu.SMEM), pl.BlockSpec(memory_space=pltpu.VMEM)
     return pl.pallas_call(
         kernel,
-        in_specs=[smem] * 2 + [vmem] * 4,
+        in_specs=[smem] + [vmem] * 5,
         out_specs=[vmem, vmem],
         out_shape=[jax.ShapeDtypeStruct((4, 144, 128), jnp.bfloat16)] * 2,
         compiler_params=pltpu.CompilerParams(vmem_limit_bytes=8 << 20),
         cost_estimate=pl.CostEstimate(flops=1024, bytes_accessed=4096, transcendentals=0),
-    )(order_x, factor.reshape(1), *planes_a, *planes_b)
+    )(order_x, squares, *planes_a, *planes_b)
 
 
 def by_place(first, second, order):
@@ -228,7 +281,7 @@
     )(order, first, second)
 
 
-def own_results(left, right, state, factor):
+def own_results(left, right, state, squares):
     def largest(rows):
         top = jnp.broadcast_to(jnp.max(rows, axis=1, keepdims=True), (72, 128))
         at = lax.broadcasted_iota(jnp.int32, (72, 128), 0)
@@ -237,7 +290,7 @@
 
     def kernel(f, l, r, state, master, first_unit, second_unit, first_top, second_top):
         gradient = jnp.concatenate([l[...], r[...]], axis=1)
-        first_new, second_new = moments(gradient, f[0], state[1], state[2])
+        first_new, second_new = moments(gradient, factor_of(f[...])[:, :1], state[1], state[2])
         master[...] = stepped(state[0], first_new, second_new)
         for new, unit, top in ((first_new, first_unit, first_top), (second_new, second_unit, second_top)):
             rows = largest(jnp.abs(new))
@@ -247,15 +300,15 @@
             top[...] = picked[:, :18]
             unit[...] = new / rows[:, :1]
 
-    smem, vmem = pl.BlockSpec(memory_space=pltpu.SMEM), pl.BlockSpec(memory_space=pltpu.VMEM)
-    return pl.pallas_call(
-        kernel,
-        in_specs=[smem] + [vmem] * 3,
+    vmem = pl.BlockSpec(memory_space=pltpu.VMEM)
+    return pl.pallas_call(
+        kernel,
+        in_specs=[vmem] * 4,
         out_specs=[vmem] * 5,
         out_shape=[jax.ShapeDtypeStruct((72, 512), f32)] * 3 + [jax.ShapeDtypeStruct((1, 18), f32)] * 2,
         compiler_params=pltpu.CompilerParams(vmem_limit_bytes=8 << 20),
         cost_estimate=pl.CostEstimate(flops=1024, bytes_accessed=4096, transcendentals=0),
-    )(factor.reshape(1), left, right, state)
+    )(squares, left, right, state)
 
 
 def shards(inputs, key_cotangent, master, first_codes, second_codes, first_scale, second_scale):
@@ -264,16 +317,15 @@
     orders = (order_x, order_z, order_of(X, 1 - c), order_of(Z, 1 - c))
 
     terms = [products(inputs, key_cotangent, c, h) for h in (0, 1)]
-    theirs = [swap(t) for t, _ in terms]
-    mine = [m for _, m in terms]
-    send_b = narrowed(*packed(mine, theirs, order_x, order_z, None, 1), 2)
-    send_b, mine = lax.optimization_barrier((send_b, mine))
-    send_a = narrowed(*packed(mine, theirs, order_x, order_z, 1, None), 2)
-    send_a, mine = lax.optimization_barrier((send_a, mine))
-    keep_a, keep_b = packed(mine, theirs, order_x, order_z, 0, 0)
-
+    parts = ()
+    for h, (away, mine) in enumerate(terms):
+        parts = packed(mine, swap(away), order_x, order_z, h, parts)
+    send_a, send_b, keep_a, keep_b = parts
+
+    come_b = exchange(narrowed(send_b, 2), Z, 0)
+    come_a = exchange(narrowed(send_a, 2), X, 0)
     states = (master, first_codes, second_codes, first_scale, second_scale)
-    keep_a, states = lax.optimization_barrier((keep_a, states))
+    come_b, states = lax.optimization_barrier((come_b, states))
     master, first_codes, second_codes, first_scale, second_scale = states
     first_old = first_codes.astype(f32) / 127.0 * per_row(first_scale)
     second_old = second_codes.astype(f32) / 255.0 * per_row(second_scale)
@@ -282,18 +334,18 @@
     got = swap(lax.dynamic_slice_in_dim(state, (1 - c) * 256, 256, axis=2))
     both = jnp.concatenate([jnp.where(c == 0, own, got), jnp.where(c == 0, got, own)], axis=1)
 
-    over_x = halving_sum(send_a, keep_a, X, 2)
-    over_z = halving_sum(send_b, keep_b, Z, 2)
+    over_x = halving_sum(come_a, keep_a, X, 2)
+    over_z = halving_sum(come_b, keep_b, Z, 2)
     over_x, both = lax.optimization_barrier((over_x, both))
-    grad_a = halving_sum(narrowed(over_x[4:], 8), over_x[:4], Z, 8)
-    grad_b = halving_sum(narrowed(over_z[2:], 16), over_z[:2], X, 16)
+    grad_a = halving_sum(exchange(narrowed(over_x[4:], 8), Z, 0), over_x[:4], Z, 8)
+    grad_b = halving_sum(exchange(narrowed(over_z[2:], 16), X, 0), over_z[:2], X, 16)
 
     planes_a = jnp.concatenate([grad_a[None], both[:, :, :128]])[None]
     planes_b = jnp.concatenate([grad_b[None], both[:, :, 128:]])[None]
-    squares = summed_over(jnp.sum(grad_a * grad_a) + jnp.sum(grad_b * grad_b), (Z, C))
+    squares = met(spread_squares(grad_a, grad_b), (Z, C))
     met_a, met_b = exchange(planes_a, Z, 2), exchange(planes_b, X, 1)
     met_a, met_b, squares = lax.optimization_barrier((met_a, met_b, squares))
-    norm_sq = summed_over(squares, (X, Y))
+    squares = met(spread_sum(squares), (X, Y))
     near_planes_a = jnp.concatenate([planes_a, met_a])
     near_planes_b = jnp.concatenate([planes_b, met_b])
     far_planes_a = exchange(near_planes_a, Z, 1)
@@ -303,11 +355,10 @@
     came = swap(lax.dynamic_slice_in_dim(gradient, (1 - c) * 72, 72, axis=0))
     left, right = jnp.where(c == 0, kept, came), jnp.where(c == 0, came, kept)
 
-    factor = jnp.minimum(1.0, clip_rms * math.sqrt(D * KV) / (jnp.sqrt(norm_sq) + 1e-06))
-    weight_a, weight_b = weights_of((near_planes_a, far_planes_a), (near_planes_b, far_planes_b), order_x, factor)
+    weight_a, weight_b = weights_of((near_planes_a, far_planes_a), (near_planes_b, far_planes_b), order_x, squares)
     far_z = exchange(weight_b[None], Z, 2)
-    far_z, left, right, factor = lax.optimization_barrier((far_z, left, right, factor))
-    new_master, first_unit, second_unit, first_top, second_top = own_results(left, right, state, factor)
+    far_z, left, right, squares = lax.optimization_barrier((far_z, left, right, squares))
+    new_master, first_unit, second_unit, first_top, second_top = own_results(left, right, state, squares)
     results = (new_master, first_unit, second_unit, first_top.reshape(18, 1), second_top.reshape(18, 1))
 
     column_a = by_place(weight_a, exchange(weight_a, Z, 0), order_z)

time: 152 us -> 144 us (0.947)
  other arithmetic: 10.2 us -> 6.22 us
  starting transfers between devices: 49.4 us -> 46.8 us
  Pallas kernels: 24.1 us -> 26.7 us
  local copies, waits for them, and re-layouts: 8.44 us -> 6.38 us
  between operations: 3.21 us -> 1.18 us
    ppermute x20, waiting for transfers between devices: 24.4 us -> 28 us  [exchange(): return lax.ppermute(value, (axis, C), pairs)]
    ppermute x8, waiting for transfers between devices: 4.97 us -> 1.64 us  [swap(): return lax.ppermute(value, C, [(0, 1), (1, 0)])]
    pallas_call x7 -> x8, Pallas kernels: 20.6 us -> 23.3 us  [the longest x2 10.3 us: products(): pl.pallas_call(kernel, in_specs=[smem, anywhere, anywhere], out_specs=[an...]
    reduce_sum x4 -> x0, other arithmetic: 2.47 us -> none  [the longest x2 1.23 us: summed_over(): return jnp.sum(lax.all_to_all(spread, axes, 0, 0, tiled=True)[:, 0, 0])]
    ppermute x8, starting transfers between devices: 11.7 us -> 9.6 us  [swap(): return lax.ppermute(value, C, [(0, 1), (1, 0)])]
    another operation x2, other arithmetic: 2.01 us -> 0.12 us  [shards(): state = jnp.stack([master, first_old, second_old])]
    unnamed x14 -> x20, local copies, waits for them, and re-layouts: 5.26 us -> 4.47 us
  transfers between devices with their start and end apart: 29 -> 29, of which waited for: 15 -> 12; matrix products, arithmetic and copies ran while one was open for 8% -> 5% of each run, Pallas kernels for 4% -> 8%
where the time goes in v3:
time: 144 us
  starting transfers between devices  46.8 us (32%)
  waiting for transfers between devices  36.1 us (25%)
  Pallas kernels  26.7 us (19%)
  blocking collectives  20.2 us (14%)
  local copies, waits for them, and re-layouts  6.38 us (4%)
  other arithmetic  6.22 us (4%)
    ppermute x20, starting transfers between devices, exchange(): return lax.ppermute(value, (axis, C), pairs)  31.6 us
    ppermute x20, waiting for transfers between devices, exchange(): return lax.ppermute(value, (axis, C), pairs)  28 us
    all_to_all x1, blocking collectives, met(): return lax.all_to_all(spread, axes, 0, 0, tiled=True)  20.2 us
    pallas_call x2, Pallas kernels, products(): pl.pallas_call(kernel, in_specs=[smem, anywhere, anywhere], out_specs=[an...  10.3 us
    pallas_call x2, Pallas kernels, packed(): pl.pallas_call(kernel, in_specs=[smem, smem, anywhere, anywhere] + [vmem]...  10 us
    ppermute x8, starting transfers between devices, swap(): return lax.ppermute(value, C, [(0, 1), (1, 0)])  9.6 us
    all_to_all x1, waiting for transfers between devices, met(): return lax.all_to_all(spread, axes, 0, 0, tiled=True)  6.52 us
    all_to_all x1, starting transfers between devices, met(): return lax.all_to_all(spread, axes, 0, 0, tiled=True)  5.65 us
  transfers between devices with their start and end apart: 29, of which 12 were waited for; matrix products, arithmetic and copies ran while one was open for 5% of the time, Pallas kernels for 8%

profile of v3, /device:TPU:1, one launch (start us, length us, event | category | flops | bytes accessed | tf_op | source)
XLA Modules:
  0.0 143.7 jit_solution(14915955880068990836)
XLA Ops:
  0.6 5.2 %shard_map.155 = (f32[2304,256]{1,0:T(8,128)}, f32[2304,256]{1,0:T(8,128)}) custom-call(s32[1]{0:T(128)} %bitcast.4.me, bf16[768,4608]{1,0:T(8,128)(2,1)} %a.3, bf16[768,512]{1,0:T(8,128)(2,1)} %b.3), custom_call_target="tpu_custom_call" | custom-call | flops 1811939328 | bytes 9437184 | tf_op jit(solution)/shard_map/pallas_call | solution.py:106
  5.9 3.3 %collective-permute-start.1 = (f32[2304,256]{1,0:T(8,128)}, f32[2304,256]{1,0:T(8,128)}, u32[]{:S(2)}, u32[]{:S(2)}) collective-permute-start(f32[2304,256]{1,0:T(8,128)} %get-tuple-element.49), channel_id=1, source_target_pairs={{0,4},{4,0},{1,5},{5,1},{2,6},{6,2},{3,7},{7,3},{8,12},{12,8},{9,1... | collective-permute-start | bytes 7077896 | tf_op jit(solution)/shard_map/ppermute | solution.py:38
  9.2 5.1 %shard_map.154 = (f32[2304,256]{1,0:T(8,128)}, f32[2304,256]{1,0:T(8,128)}) custom-call(s32[1]{0:T(128)} %bitcast.4.me, bf16[768,4608]{1,0:T(8,128)(2,1)} %a.3, bf16[768,512]{1,0:T(8,128)(2,1)} %b.3), custom_call_target="tpu_custom_call" | custom-call | flops 1811939328 | bytes 9437184 | tf_op jit(solution)/shard_map/pallas_call | solution.py:106
  14.3 0.1 collective-permute-start
  14.4 0.8 fusion.14
  15.2 0.8 fusion.15
  15.9 4.2 %shard_map.156 = (f32[2,8,144,128]{3,2,1,0:T(8,128)S(1)}, f32[4,4,144,128]{3,2,1,0:T(8,128)S(1)}, f32[2,8,144,128]{3,2,1,0:T(8,128)S(1)}, f32[4,4,144,128]{3,2,1,0:T(8,128)}) custom-call(s32[4]{0:T(128)S(1)} %get-tuple-element.95.ox, s32[8]{0:T(128)S(1)} %get-tuple-element.93.oz.o, f32[2304,256]{1,0:T(8,128)} %get-tuple-element.48.p, ...), custom_call_target="tpu_custom_call" | custom-call | flops 1024 | bytes 4096 | tf_op jit(solution)/shard_map/pallas_call | solution.py:155
  20.1 1.0 copy-done
  21.1 1.0 copy-done.1
  22.2 1.0 copy-done.2
  23.2 1.4 copy-done.3
  24.6 5.9 %shard_map.157 = (f32[2,8,144,128]{3,2,1,0:T(8,128)S(1)}, f32[4,4,144,128]{3,2,1,0:T(8,128)S(1)}, f32[2,8,144,128]{3,2,1,0:T(8,128)S(1)}, f32[4,4,144,128]{3,2,1,0:T(8,128)}) custom-call(s32[4]{0:T(128)S(1)} %get-tuple-element.95.ox, s32[8]{0:T(128)S(1)} %get-tuple-element.93.oz.o, f32[2304,256]{1,0:T(8,128)} %get-tuple-element.46.p, f32[2304,256]{1,0:T(8,128)} %copy-done.3, ...), custom_call_target="tpu_custom_call" | custom-call | flops 1024 | bytes 4096 | tf_op jit(solution)/shard_map/pallas_call | solution.py:155
  30.4 0.9 multiply_convert_fusion.1
  31.4 0.7 collective-permute-start.2
  32.1 0.1 multiply_convert_fusion
  32.3 5.7 %collective-permute-start.4 = (f16[4,4,144,128]{3,2,1,0:T(8,128)(2,1)S(1)}, f16[4,4,144,128]{3,2,1,0:T(8,128)(2,1)}, u32[]{:S(2)}, u32[]{:S(2)}) collective-permute-start(f16[4,4,144,128]{3,2,1,0:T(8,128)(2,1)S(1)} %multiply_convert_fusion), channel_id=1, source_target_pairs={{0,8},{4,60},{8,0},{12,20},{16,24},{20,12},{24,16},{28,36},{32,40}... | collective-permute-start | bytes 1769480 | tf_op jit(solution)/shard_map/ppermute | solution.py:45
  37.9 3.7 %collective-permute-done.2 = f16[2,8,144,128]{3,2,1,0:T(8,128)(2,1)} collective-permute-done((f16[2,8,144,128]{3,2,1,0:T(8,128)(2,1)}, f16[2,8,144,128]{3,2,1,0:T(8,128)(2,1)}, u32[]{:S(2)}, u32[]{:S(2)}) %collective-permute-start.2) | collective-permute-done | bytes 589856 | tf_op jit(solution)/shard_map/ppermute | solution.py:45
  41.7 1.2 multiply_add_fusion.1
  42.9 0.8 fusion.1
  43.7 1.6 %collective-permute-done.4 = f16[4,4,144,128]{3,2,1,0:T(8,128)(2,1)} collective-permute-done((f16[4,4,144,128]{3,2,1,0:T(8,128)(2,1)S(1)}, f16[4,4,144,128]{3,2,1,0:T(8,128)(2,1)}, u32[]{:S(2)}, u32[]{:S(2)}) %collective-permute-start.4) | collective-permute-done | bytes 589856 | tf_op jit(solution)/shard_map/ppermute | solution.py:45
  45.4 0.1 mul.160
  45.9 0.1 collective-permute-start.5
  46.0 1.2 multiply_add_fusion
  47.2 1.5 %collective-permute-start.10 = (f16[2,4,144,128]{3,2,1,0:T(8,128)(2,1)S(1)}, f16[2,4,144,128]{3,2,1,0:T(8,128)(2,1)S(1)}, u32[]{:S(2)}, u32[]{:S(2)}) collective-permute-start(f16[2,4,144,128]{3,2,1,0:T(8,128)(2,1)S(1)} %fusion), channel_id=1, source_target_pairs={{0,56},{4,12},{8,16},{12,4},{16,8},{20,28},{24,32},{28,20},{32,24}... | collective-permute-start | bytes 884744 | tf_op jit(solution)/shard_map/ppermute | solution.py:45
  48.9 1.0 collective-permute-done.3
  49.9 1.0 fusion.2
  51.0 3.9 %collective-permute-start.6 = (f16[4,144,128]{2,1,0:T(8,128)(2,1)S(1)}, f16[4,144,128]{2,1,0:T(8,128)(2,1)S(1)}, u32[]{:S(2)}, u32[]{:S(2)}) collective-permute-start(f16[4,144,128]{2,1,0:T(8,128)(2,1)S(1)} %multiply_convert_fusion.2), channel_id=1, source_target_pairs={{0,8},{4,60},{8,0},{12,20},{16,24},{20,12},{24,16},{28,36},{32,40}... | collective-permute-start | bytes 442376 | tf_op jit(solution)/shard_map/ppermute | solution.py:45
  54.9 0.1 slice_add_fusion
  55.0 4.9 %collective-permute-start.11 = (f16[1,4,144,128]{3,2,1,0:T(8,128)(2,1)S(1)}, f16[1,4,144,128]{3,2,1,0:T(8,128)(2,1)S(1)}, u32[]{:S(2)}, u32[]{:S(2)}) collective-permute-start(f16[1,4,144,128]{3,2,1,0:T(8,128)(2,1)S(1)} %fusion.3), channel_id=1, source_target_pairs={{0,24},{4,44},{8,48},{12,36},{16,40},{20,60},{24,0},{28,52},{32,56... | collective-permute-start | bytes 442376 | tf_op jit(solution)/shard_map/ppermute | solution.py:45
  60.0 0.8 collective-permute-start.7
  60.8 1.7 %collective-permute-done.11 = f16[1,4,144,128]{3,2,1,0:T(8,128)(2,1)S(1)} collective-permute-done((f16[1,4,144,128]{3,2,1,0:T(8,128)(2,1)S(1)}, f16[1,4,144,128]{3,2,1,0:T(8,128)(2,1)S(1)}, u32[]{:S(2)}, u32[]{:S(2)}) %collective-permute-start.11) | collective-permute-done | bytes 147488 | tf_op jit(solution)/shard_map/ppermute | solution.py:45
  62.6 2.4 %collective-permute-start.12 = (f16[2,144,128]{2,1,0:T(8,128)(2,1)S(1)}, f16[2,144,128]{2,1,0:T(8,128)(2,1)S(1)}, u32[]{:S(2)}, u32[]{:S(2)}) collective-permute-start(f16[2,144,128]{2,1,0:T(8,128)(2,1)S(1)} %fusion.7), channel_id=1, source_target_pairs={{0,64},{4,196},{64,0},{68,132},{128,192},{132,68},{192,128},{196,4... | collective-permute-start | bytes 221192 | tf_op jit(solution)/shard_map/ppermute | solution.py:45
  65.0 0.7 collective-permute-done.7
  65.7 1.7 %collective-permute-start.8 = (f16[1,144,128]{2,1,0:T(8,128)(2,1)S(1)}, f16[1,144,128]{2,1,0:T(8,128)(2,1)S(1)}, u32[]{:S(2)}, u32[]{:S(2)}) collective-permute-start(f16[1,144,128]{2,1,0:T(8,128)(2,1)S(1)} %fusion.11), channel_id=1, source_target_pairs={{0,24},{4,44},{8,48},{12,36},{16,40},{20,60},{24,0},{28,52},{32,56... | collective-permute-start | bytes 110600 | tf_op jit(solution)/shard_map/ppermute | solution.py:45
  67.5 0.1 collective-permute-start.13
  67.6 4.0 %collective-permute-done.8 = f16[1,144,128]{2,1,0:T(8,128)(2,1)S(1)} collective-permute-done((f16[1,144,128]{2,1,0:T(8,128)(2,1)S(1)}, f16[1,144,128]{2,1,0:T(8,128)(2,1)S(1)}, u32[]{:S(2)}, u32[]{:S(2)}) %collective-permute-start.8) | collective-permute-done | bytes 36896 | tf_op jit(solution)/shard_map/ppermute | solution.py:45
  71.7 1.7 %collective-permute-start.9 = (f32[1,4,144,128]{3,2,1,0:T(8,128)S(1)}, f32[1,4,144,128]{3,2,1,0:T(8,128)S(1)}, u32[]{:S(2)}, u32[]{:S(2)}) collective-permute-start(f32[1,4,144,128]{3,2,1,0:T(8,128)S(1)} %maximum_bitcast_fusion), channel_id=1, source_target_pairs={{0,24},{4,44},{8,48},{12,36},{16,40},{20,60},{24,0},{28,52},{32,56... | collective-permute-start | bytes 884744 | tf_op jit(solution)/shard_map/ppermute | solution.py:45
  73.5 0.1 collective-permute-start.14
  73.6 0.1 shard_map.158
  73.7 20.2 %all_to_all.10.parts = f32[16,8,128]{2,1,0:T(8,128)S(1)} all-to-all(f32[16,8,128]{2,1,0:T(8,128)S(1)} %shard_map.158), channel_id=1, replica_groups=mesh['dp_0'=4,'dp_1'=8,'dp_2'=2,'mp'=4] {'dp_1','dp_2'}, dimensions={0} | all-to-all | bytes 131072 | tf_op jit(solution)/shard_map/all_to_all | solution.py:223
  94.0 0.1 collective-permute-start.15
  94.1 1.1 collective-permute-start.16
  95.3 0.7 shard_map.159
  95.9 5.6 %all-to-all-start.1 = ((f32[16,8,128]{2,1,0:T(8,128)}), f32[16,8,128]{2,1,0:T(8,128)S(1)}, u32[]{:S(2)}, u32[]{:S(2)}) async-start(f32[16,8,128]{2,1,0:T(8,128)} %shard_map.159), calls=%async_computation.1 | async-start | bytes 131072 | tf_op jit(solution)/shard_map/all_to_all | solution.py:223
  101.6 6.5 %all-to-all-done.1.f = f32[16,8,128]{2,1,0:T(8,128)S(1)} async-done(((f32[16,8,128]{2,1,0:T(8,128)}), f32[16,8,128]{2,1,0:T(8,128)S(1)}, u32[]{:S(2)}, u32[]{:S(2)}) %all-to-all-start.1) | async-done | bytes 65568 | tf_op jit(solution)/shard_map/all_to_all | solution.py:223
  108.1 1.0 shard_map.160
  109.2 1.6 %collective-permute-start.17 = (bf16[4,144,128]{2,1,0:T(8,128)(2,1)S(1)}, bf16[4,144,128]{2,1,0:T(8,128)(2,1)S(1)}, u32[]{:S(2)}, u32[]{:S(2)}) collective-permute-start(bf16[4,144,128]{2,1,0:T(8,128)(2,1)S(1)} %get-tuple-element.69.a), channel_id=1, source_target_pairs={{0,8},{4,60},{8,0},{12,20},{16,24},{20,12},{24,16},{28,36},{32,40}... | collective-permute-start | bytes 442376 | tf_op jit(solution)/shard_map/ppermute | solution.py:45
  110.8 2.0 %collective-permute-start.20 = (f32[72,256]{1,0:T(8,128)S(1)}, f32[72,256]{1,0:T(8,128)S(1)}, u32[]{:S(2)}, u32[]{:S(2)}) collective-permute-start(f32[72,256]{1,0:T(8,128)S(1)} %fusion.8), channel_id=1, source_target_pairs={{0,4},{4,0},{1,5},{5,1},{2,6},{6,2},{3,7},{7,3},{8,12},{12,8},{9,1... | collective-permute-start | bytes 221192 | tf_op jit(solution)/shard_map/ppermute | solution.py:38
  112.7 2.7 %collective-permute-start.19 = (bf16[1,4,144,128]{3,2,1,0:T(8,128)(2,1)S(1)}, bf16[1,4,144,128]{3,2,1,0:T(8,128)(2,1)S(1)}, u32[]{:S(2)}, u32[]{:S(2)}) collective-permute-start(bf16[1,4,144,128]{3,2,1,0:T(8,128)(2,1)S(1)} %bitcast.45), channel_id=1, source_target_pairs={{0,24},{4,44},{8,48},{12,36},{16,40},{20,60},{24,0},{28,52},{32,56... | collective-permute-start | bytes 442376 | tf_op jit(solution)/shard_map/ppermute | solution.py:45
  115.4 0.6 shard_map.161
  116.0 0.3 collective-permute-start.18
  116.4 6.2 %collective-permute-done.19 = bf16[1,4,144,128]{3,2,1,0:T(8,128)(2,1)S(1)} collective-permute-done((bf16[1,4,144,128]{3,2,1,0:T(8,128)(2,1)S(1)}, bf16[1,4,144,128]{3,2,1,0:T(8,128)(2,1)S(1)}, u32[]{:S(2)}, u32[]{:S(2)}) %collective-permute-start.19) | collective-permute-done | bytes 147488 | tf_op jit(solution)/shard_map/ppermute | solution.py:45
  122.6 0.1 collective-permute-start.21
  122.7 1.1 shard_map.162
  123.8 0.9 collective-permute-start.24
  124.8 3.5 %collective-permute-done.21 = bf16[2,4,144,128]{3,2,1,0:T(8,128)(2,1)S(1)} collective-permute-done((bf16[2,4,144,128]{3,2,1,0:T(8,128)(2,1)S(1)}, bf16[2,4,144,128]{3,2,1,0:T(8,128)(2,1)S(1)}, u32[]{:S(2)}, u32[]{:S(2)}) %collective-permute-start.21) | collective-permute-done | bytes 294944 | tf_op jit(solution)/shard_map/ppermute | solution.py:45
  128.3 1.0 collective-permute-start.25
  129.3 1.8 %collective-permute-start.22 = (bf16[2,8,144,128]{3,2,1,0:T(8,128)(2,1)S(1)}, bf16[2,8,144,128]{3,2,1,0:T(8,128)(2,1)S(1)}, u32[]{:S(2)}, u32[]{:S(2)}) collective-permute-start(bf16[2,8,144,128]{3,2,1,0:T(8,128)(2,1)S(1)} %pad_maximum_fusion.2.rest_0_), channel_id=1, source_target_pairs={{0,4},{4,0},{1,5},{5,1},{2,6},{6,2},{3,7},{7,3},{8,12},{12,8},{9,1... | collective-permute-start | bytes 1769480 | tf_op jit(solution)/shard_map/ppermute | solution.py:38
  131.1 2.7 %collective-permute-done.24.rest_4_ = bf16[2,8,144,128]{3,2,1,0:T(8,128)(2,1)S(1)} collective-permute-done((bf16[2,8,144,128]{3,2,1,0:T(8,128)(2,1)S(1)}, bf16[2,8,144,128]{3,2,1,0:T(8,128)(2,1)S(1)}, u32[]{:S(2)}, u32[]{:S(2)}) %collective-permute-start.24) | collective-permute-done | bytes 589856 | tf_op jit(solution)/shard_map/ppermute | solution.py:45
  133.9 1.7 %collective-permute-start.26 = (bf16[2,8,144,128]{3,2,1,0:T(8,128)(2,1)S(1)}, bf16[2,8,144,128]{3,2,1,0:T(8,128)(2,1)S(1)}, u32[]{:S(2)}, u32[]{:S(2)}) collective-permute-start(bf16[2,8,144,128]{3,2,1,0:T(8,128)(2,1)S(1)} %collective-permute-done.24.rest_4_), channel_id=1, source_target_pairs={{0,4},{4,0},{1,5},{5,1},{2,6},{6,2},{3,7},{7,3},{8,12},{12,8},{9,1... | collective-permute-start | bytes 1769480 | tf_op jit(solution)/shard_map/ppermute | solution.py:38
  135.5 2.8 %collective-permute-done.25.rest_5_ = bf16[4,4,144,128]{3,2,1,0:T(8,128)(2,1)S(1)} collective-permute-done((bf16[4,4,144,128]{3,2,1,0:T(8,128)(2,1)S(1)}, bf16[4,4,144,128]{3,2,1,0:T(8,128)(2,1)S(1)}, u32[]{:S(2)}, u32[]{:S(2)}) %collective-permute-start.25) | collective-permute-done | bytes 589856 | tf_op jit(solution)/shard_map/ppermute | solution.py:45
  138.4 0.6 collective-permute-start.27
  139.0 1.6 %collective-permute-done.27.rest_7_ = bf16[4,4,144,128]{3,2,1,0:T(8,128)(2,1)S(1)} collective-permute-done((bf16[4,4,144,128]{3,2,1,0:T(8,128)(2,1)S(1)}, bf16[4,4,144,128]{3,2,1,0:T(8,128)(2,1)S(1)}, u32[]{:S(2)}, u32[]{:S(2)}) %collective-permute-start.27) | collective-permute-done | bytes 589856 | tf_op jit(solution)/shard_map/ppermute | solution.py:38
  140.6 2.9 %shard_map.163 = bf16[4,8,144,512]{3,2,1,0:T(8,128)(2,1)} custom-call(s32[4]{0:T(128)S(1)} %get-tuple-element.95.ox, s32[8]{0:T(128)S(1)} %get-tuple-element.93.oz.o, s32[4]{0:T(128)S(1)} %get-tuple-element.94.px, s32[8]{0:T(128)S(1)} %get-tuple-element.92.pz, s32[1]{0:T(128)} %bitcast.4.me, bf16[2,8,144,128]{3,2,1,0:T(8,128)(2,1)S(1)} %pad_maximum_fusion.2.rest_0_, ...), custom_call_target="tpu_custom_call" | custom-call | flops 1024 | bytes 4096 | tf_op jit(solution)/shard_map/pallas_call | solution.py:188
  (68 shorter events, 1.2 us)
Async XLA Ops:
  5.9 10.1 %collective-permute-start.1 = (f32[2304,256]{1,0:T(8,128)}, f32[2304,256]{1,0:T(8,128)}, u32[]{:S(2)}, u32[]{:S(2)}) collective-permute-start(f32[2304,256]{1,0:T(8,128)} %get-tuple-element.49), channel_id=1, source_target_pairs={{0,4},{4,0},{1,5},{5,1},{2,6},{6,2},{3,7},{7,3},{8,12},{12,8},{9,1... | collective-permute-start | bytes 7077896 | tf_op jit(solution)/shard_map/ppermute | solution.py:38
  14.3 8.9 %collective-permute-start = (f32[2304,256]{1,0:T(8,128)}, f32[2304,256]{1,0:T(8,128)S(1)}, u32[]{:S(2)}, u32[]{:S(2)}) collective-permute-start(f32[2304,256]{1,0:T(8,128)} %get-tuple-element.47), channel_id=1, source_target_pairs={{0,4},{4,0},{1,5},{5,1},{2,6},{6,2},{3,7},{7,3},{8,12},{12,8},{9,1... | collective-permute-start | bytes 7077896 | tf_op jit(solution)/shard_map/ppermute | solution.py:38
  20.1 1.0 copy-start
  21.1 1.0 copy-start.1
  22.2 1.0 copy-start.2
  23.2 1.4 copy-start.3
  31.4 10.3 %collective-permute-start.2 = (f16[2,8,144,128]{3,2,1,0:T(8,128)(2,1)}, f16[2,8,144,128]{3,2,1,0:T(8,128)(2,1)}, u32[]{:S(2)}, u32[]{:S(2)}) collective-permute-start(f16[2,8,144,128]{3,2,1,0:T(8,128)(2,1)} %multiply_convert_fusion.1), channel_id=1, source_target_pairs={{0,64},{4,196},{64,0},{68,132},{128,192},{132,68},{192,128},{196,4... | collective-permute-start | bytes 1769480 | tf_op jit(solution)/shard_map/ppermute | solution.py:45
  32.3 13.0 %collective-permute-start.4 = (f16[4,4,144,128]{3,2,1,0:T(8,128)(2,1)S(1)}, f16[4,4,144,128]{3,2,1,0:T(8,128)(2,1)}, u32[]{:S(2)}, u32[]{:S(2)}) collective-permute-start(f16[4,4,144,128]{3,2,1,0:T(8,128)(2,1)S(1)} %multiply_convert_fusion), channel_id=1, source_target_pairs={{0,8},{4,60},{8,0},{12,20},{16,24},{20,12},{24,16},{28,36},{32,40}... | collective-permute-start | bytes 1769480 | tf_op jit(solution)/shard_map/ppermute | solution.py:45
  41.6 3.7 %copy-start.8 = (f32[18,1]{0,1:T(1,128)S(1)}, f32[18,1]{0,1:T(1,128)}, u32[]{:S(2)}) copy-start(f32[18,1]{0,1:T(1,128)} %param.17) | copy-start | bytes 220
  41.7 3.8 %copy-start.9 = (f32[18,1]{0,1:T(1,128)S(1)}, f32[18,1]{0,1:T(1,128)}, u32[]{:S(2)}) copy-start(f32[18,1]{0,1:T(1,128)} %param.16) | copy-start | bytes 220
  41.7 4.0 %copy-start.6 = (s32[72,512]{1,0:T(8,128)S(1)}, s32[72,512]{1,0:T(8,128)}, u32[]{:S(2)}) copy-start(s32[72,512]{1,0:T(8,128)} %param.15) | copy-start | bytes 442372
  41.7 4.0 %copy-start.7 = (s32[72,512]{1,0:T(8,128)S(1)}, s32[72,512]{1,0:T(8,128)}, u32[]{:S(2)}) copy-start(s32[72,512]{1,0:T(8,128)} %param.14) | copy-start | bytes 442372
  42.9 2.9 %copy-start.5 = (f32[72,512]{1,0:T(8,128)S(1)}, f32[72,512]{1,0:T(8,128)}, u32[]{:S(2)}) copy-start(f32[72,512]{1,0:T(8,128)} %param.13) | copy-start | bytes 442372
  43.7 2.3 %copy-start.4 = (f32[4,4,144,128]{3,2,1,0:T(8,128)S(1)}, f32[4,4,144,128]{3,2,1,0:T(8,128)}, u32[]{:S(2)}) copy-start(f32[4,4,144,128]{3,2,1,0:T(8,128)} %get-tuple-element.64) | copy-start | bytes 3538948
  43.7 6.2 %collective-permute-start.3 = (f16[1,8,144,128]{3,2,1,0:T(8,128)(2,1)}, f16[1,8,144,128]{3,2,1,0:T(8,128)(2,1)}, u32[]{:S(2)}, u32[]{:S(2)}) collective-permute-start(f16[1,8,144,128]{3,2,1,0:T(8,128)(2,1)} %fusion.1), channel_id=1, source_target_pairs={{0,192},{4,68},{64,128},{68,4},{128,64},{132,196},{192,0},{196,132... | collective-permute-start | bytes 884744 | tf_op jit(solution)/shard_map/ppermute | solution.py:45
  45.9 2.9 %collective-permute-start.5 = (f32[3,72,256]{2,1,0:T(8,128)S(1)}, f32[3,72,256]{2,1,0:T(8,128)S(1)}, u32[]{:S(2)}, u32[]{:S(2)}) collective-permute-start(f32[3,72,256]{2,1,0:T(8,128)S(1)} %constant_dynamic-slice_fusion), channel_id=1, source_target_pairs={{0,4},{4,0},{1,5},{5,1},{2,6},{6,2},{3,7},{7,3},{8,12},{12,8},{9,1... | collective-permute-start | bytes 663560 | tf_op jit(solution)/shard_map/ppermute | solution.py:38
  47.2 7.6 %collective-permute-start.10 = (f16[2,4,144,128]{3,2,1,0:T(8,128)(2,1)S(1)}, f16[2,4,144,128]{3,2,1,0:T(8,128)(2,1)S(1)}, u32[]{:S(2)}, u32[]{:S(2)}) collective-permute-start(f16[2,4,144,128]{3,2,1,0:T(8,128)(2,1)S(1)} %fusion), channel_id=1, source_target_pairs={{0,56},{4,12},{8,16},{12,4},{16,8},{20,28},{24,32},{28,20},{32,24}... | collective-permute-start | bytes 884744 | tf_op jit(solution)/shard_map/ppermute | solution.py:45
  51.0 9.0 %collective-permute-start.6 = (f16[4,144,128]{2,1,0:T(8,128)(2,1)S(1)}, f16[4,144,128]{2,1,0:T(8,128)(2,1)S(1)}, u32[]{:S(2)}, u32[]{:S(2)}) collective-permute-start(f16[4,144,128]{2,1,0:T(8,128)(2,1)S(1)} %multiply_convert_fusion.2), channel_id=1, source_target_pairs={{0,8},{4,60},{8,0},{12,20},{16,24},{20,12},{24,16},{28,36},{32,40}... | collective-permute-start | bytes 442376 | tf_op jit(solution)/shard_map/ppermute | solution.py:45
  55.0 7.5 %collective-permute-start.11 = (f16[1,4,144,128]{3,2,1,0:T(8,128)(2,1)S(1)}, f16[1,4,144,128]{3,2,1,0:T(8,128)(2,1)S(1)}, u32[]{:S(2)}, u32[]{:S(2)}) collective-permute-start(f16[1,4,144,128]{3,2,1,0:T(8,128)(2,1)S(1)} %fusion.3), channel_id=1, source_target_pairs={{0,24},{4,44},{8,48},{12,36},{16,40},{20,60},{24,0},{28,52},{32,56... | collective-permute-start | bytes 442376 | tf_op jit(solution)/shard_map/ppermute | solution.py:45
  60.0 5.7 %collective-permute-start.7 = (f16[2,144,128]{2,1,0:T(8,128)(2,1)S(1)}, f16[2,144,128]{2,1,0:T(8,128)(2,1)S(1)}, u32[]{:S(2)}, u32[]{:S(2)}) collective-permute-start(f16[2,144,128]{2,1,0:T(8,128)(2,1)S(1)} %fusion.6), channel_id=1, source_target_pairs={{0,56},{4,12},{8,16},{12,4},{16,8},{20,28},{24,32},{28,20},{32,24}... | collective-permute-start | bytes 221192 | tf_op jit(solution)/shard_map/ppermute | solution.py:45
  62.6 4.9 %collective-permute-start.12 = (f16[2,144,128]{2,1,0:T(8,128)(2,1)S(1)}, f16[2,144,128]{2,1,0:T(8,128)(2,1)S(1)}, u32[]{:S(2)}, u32[]{:S(2)}) collective-permute-start(f16[2,144,128]{2,1,0:T(8,128)(2,1)S(1)} %fusion.7), channel_id=1, source_target_pairs={{0,64},{4,196},{64,0},{68,132},{128,192},{132,68},{192,128},{196,4... | collective-permute-start | bytes 221192 | tf_op jit(solution)/shard_map/ppermute | solution.py:45
  65.7 5.9 %collective-permute-start.8 = (f16[1,144,128]{2,1,0:T(8,128)(2,1)S(1)}, f16[1,144,128]{2,1,0:T(8,128)(2,1)S(1)}, u32[]{:S(2)}, u32[]{:S(2)}) collective-permute-start(f16[1,144,128]{2,1,0:T(8,128)(2,1)S(1)} %fusion.11), channel_id=1, source_target_pairs={{0,24},{4,44},{8,48},{12,36},{16,40},{20,60},{24,0},{28,52},{32,56... | collective-permute-start | bytes 110600 | tf_op jit(solution)/shard_map/ppermute | solution.py:45
  67.5 5.9 %collective-permute-start.13 = (f16[1,144,128]{2,1,0:T(8,128)(2,1)S(1)}, f16[1,144,128]{2,1,0:T(8,128)(2,1)S(1)}, u32[]{:S(2)}, u32[]{:S(2)}) collective-permute-start(f16[1,144,128]{2,1,0:T(8,128)(2,1)S(1)} %fusion.10), channel_id=1, source_target_pairs={{0,192},{4,68},{64,128},{68,4},{128,64},{132,196},{192,0},{196,132... | collective-permute-start | bytes 110600 | tf_op jit(solution)/shard_map/ppermute | solution.py:45
  71.7 22.3 %collective-permute-start.9 = (f32[1,4,144,128]{3,2,1,0:T(8,128)S(1)}, f32[1,4,144,128]{3,2,1,0:T(8,128)S(1)}, u32[]{:S(2)}, u32[]{:S(2)}) collective-permute-start(f32[1,4,144,128]{3,2,1,0:T(8,128)S(1)} %maximum_bitcast_fusion), channel_id=1, source_target_pairs={{0,24},{4,44},{8,48},{12,36},{16,40},{20,60},{24,0},{28,52},{32,56... | collective-permute-start | bytes 884744 | tf_op jit(solution)/shard_map/ppermute | solution.py:45
  73.5 20.5 %collective-permute-start.14 = (f32[1,4,144,128]{3,2,1,0:T(8,128)S(1)}, f32[1,4,144,128]{3,2,1,0:T(8,128)S(1)}, u32[]{:S(2)}, u32[]{:S(2)}) collective-permute-start(f32[1,4,144,128]{3,2,1,0:T(8,128)S(1)} %maximum_bitcast_fusion.1), channel_id=1, source_target_pairs={{0,192},{4,68},{64,128},{68,4},{128,64},{132,196},{192,0},{196,132... | collective-permute-start | bytes 884744 | tf_op jit(solution)/shard_map/ppermute | solution.py:45
  94.0 14.1 %collective-permute-start.15 = (f32[2,4,144,128]{3,2,1,0:T(8,128)S(1)}, f32[2,4,144,128]{3,2,1,0:T(8,128)S(1)}, u32[]{:S(2)}, u32[]{:S(2)}) collective-permute-start(f32[2,4,144,128]{3,2,1,0:T(8,128)S(1)} %pad_maximum_fusion.a0), channel_id=1, source_target_pairs={{0,56},{4,12},{8,16},{12,4},{16,8},{20,28},{24,32},{28,20},{32,24}... | collective-permute-start | bytes 1769480 | tf_op jit(solution)/shard_map/ppermute | solution.py:45
  94.1 14.0 %collective-permute-start.16 = (f32[2,4,144,128]{3,2,1,0:T(8,128)S(1)}, f32[2,4,144,128]{3,2,1,0:T(8,128)S(1)}, u32[]{:S(2)}, u32[]{:S(2)}) collective-permute-start(f32[2,4,144,128]{3,2,1,0:T(8,128)S(1)} %pad_maximum_fusion.1.b0), channel_id=1, source_target_pairs={{0,64},{4,196},{64,0},{68,132},{128,192},{132,68},{192,128},{196,4... | collective-permute-start | bytes 1769480 | tf_op jit(solution)/shard_map/ppermute | solution.py:45
  95.9 12.2 %all-to-all-start.1 = ((f32[16,8,128]{2,1,0:T(8,128)}), f32[16,8,128]{2,1,0:T(8,128)S(1)}, u32[]{:S(2)}, u32[]{:S(2)}) async-start(f32[16,8,128]{2,1,0:T(8,128)} %shard_map.159), calls=%async_computation.1 | async-start | bytes 131072 | tf_op jit(solution)/shard_map/all_to_all | solution.py:223
  109.2 6.3 %collective-permute-start.17 = (bf16[4,144,128]{2,1,0:T(8,128)(2,1)S(1)}, bf16[4,144,128]{2,1,0:T(8,128)(2,1)S(1)}, u32[]{:S(2)}, u32[]{:S(2)}) collective-permute-start(bf16[4,144,128]{2,1,0:T(8,128)(2,1)S(1)} %get-tuple-element.69.a), channel_id=1, source_target_pairs={{0,8},{4,60},{8,0},{12,20},{16,24},{20,12},{24,16},{28,36},{32,40}... | collective-permute-start | bytes 442376 | tf_op jit(solution)/shard_map/ppermute | solution.py:45
  110.8 5.6 %collective-permute-start.20 = (f32[72,256]{1,0:T(8,128)S(1)}, f32[72,256]{1,0:T(8,128)S(1)}, u32[]{:S(2)}, u32[]{:S(2)}) collective-permute-start(f32[72,256]{1,0:T(8,128)S(1)} %fusion.8), channel_id=1, source_target_pairs={{0,4},{4,0},{1,5},{5,1},{2,6},{6,2},{3,7},{7,3},{8,12},{12,8},{9,1... | collective-permute-start | bytes 221192 | tf_op jit(solution)/shard_map/ppermute | solution.py:38
  112.7 9.8 %collective-permute-start.19 = (bf16[1,4,144,128]{3,2,1,0:T(8,128)(2,1)S(1)}, bf16[1,4,144,128]{3,2,1,0:T(8,128)(2,1)S(1)}, u32[]{:S(2)}, u32[]{:S(2)}) collective-permute-start(bf16[1,4,144,128]{3,2,1,0:T(8,128)(2,1)S(1)} %bitcast.45), channel_id=1, source_target_pairs={{0,24},{4,44},{8,48},{12,36},{16,40},{20,60},{24,0},{28,52},{32,56... | collective-permute-start | bytes 442376 | tf_op jit(solution)/shard_map/ppermute | solution.py:45
  116.0 7.8 %collective-permute-start.18 = (bf16[1,8,144,128]{3,2,1,0:T(8,128)(2,1)S(1)}, bf16[1,8,144,128]{3,2,1,0:T(8,128)(2,1)S(1)}, u32[]{:S(2)}, u32[]{:S(2)}) collective-permute-start(bf16[1,8,144,128]{3,2,1,0:T(8,128)(2,1)S(1)} %bitcast.43), channel_id=1, source_target_pairs={{0,192},{4,68},{64,128},{68,4},{128,64},{132,196},{192,0},{196,132... | collective-permute-start | bytes 884744 | tf_op jit(solution)/shard_map/ppermute | solution.py:45
  122.6 5.7 %collective-permute-start.21 = (bf16[2,4,144,128]{3,2,1,0:T(8,128)(2,1)S(1)}, bf16[2,4,144,128]{3,2,1,0:T(8,128)(2,1)S(1)}, u32[]{:S(2)}, u32[]{:S(2)}) collective-permute-start(bf16[2,4,144,128]{3,2,1,0:T(8,128)(2,1)S(1)} %pad_maximum_fusion.6), channel_id=1, source_target_pairs={{0,56},{4,12},{8,16},{12,4},{16,8},{20,28},{24,32},{28,20},{32,24}... | collective-permute-start | bytes 884744 | tf_op jit(solution)/shard_map/ppermute | solution.py:45
  123.8 10.0 %collective-permute-start.24 = (bf16[2,8,144,128]{3,2,1,0:T(8,128)(2,1)S(1)}, bf16[2,8,144,128]{3,2,1,0:T(8,128)(2,1)S(1)}, u32[]{:S(2)}, u32[]{:S(2)}) collective-permute-start(bf16[2,8,144,128]{3,2,1,0:T(8,128)(2,1)S(1)} %pad_maximum_fusion.2.rest_0_), channel_id=1, source_target_pairs={{0,64},{4,196},{64,0},{68,132},{128,192},{132,68},{192,128},{196,4... | collective-permute-start | bytes 1769480 | tf_op jit(solution)/shard_map/ppermute | solution.py:45
  128.3 10.0 %collective-permute-start.25 = (bf16[4,4,144,128]{3,2,1,0:T(8,128)(2,1)S(1)}, bf16[4,4,144,128]{3,2,1,0:T(8,128)(2,1)S(1)}, u32[]{:S(2)}, u32[]{:S(2)}) collective-permute-start(bf16[4,4,144,128]{3,2,1,0:T(8,128)(2,1)S(1)} %pad_maximum_fusion.3.rest_1_), channel_id=1, source_target_pairs={{0,8},{4,60},{8,0},{12,20},{16,24},{20,12},{24,16},{28,36},{32,40}... | collective-permute-start | bytes 1769480 | tf_op jit(solution)/shard_map/ppermute | solution.py:45
  129.3 9.7 %collective-permute-start.22 = (bf16[2,8,144,128]{3,2,1,0:T(8,128)(2,1)S(1)}, bf16[2,8,144,128]{3,2,1,0:T(8,128)(2,1)S(1)}, u32[]{:S(2)}, u32[]{:S(2)}) collective-permute-start(bf16[2,8,144,128]{3,2,1,0:T(8,128)(2,1)S(1)} %pad_maximum_fusion.2.rest_0_), channel_id=1, source_target_pairs={{0,4},{4,0},{1,5},{5,1},{2,6},{6,2},{3,7},{7,3},{8,12},{12,8},{9,1... | collective-permute-start | bytes 1769480 | tf_op jit(solution)/shard_map/ppermute | solution.py:38
  131.1 7.9 %collective-permute-start.23 = (bf16[4,4,144,128]{3,2,1,0:T(8,128)(2,1)S(1)}, bf16[4,4,144,128]{3,2,1,0:T(8,128)(2,1)S(1)}, u32[]{:S(2)}, u32[]{:S(2)}) collective-permute-start(bf16[4,4,144,128]{3,2,1,0:T(8,128)(2,1)S(1)} %pad_maximum_fusion.3.rest_1_), channel_id=1, source_target_pairs={{0,4},{4,0},{1,5},{5,1},{2,6},{6,2},{3,7},{7,3},{8,12},{12,8},{9,1... | collective-permute-start | bytes 1769480 | tf_op jit(solution)/shard_map/ppermute | solution.py:38
  133.9 5.1 %collective-permute-start.26 = (bf16[2,8,144,128]{3,2,1,0:T(8,128)(2,1)S(1)}, bf16[2,8,144,128]{3,2,1,0:T(8,128)(2,1)S(1)}, u32[]{:S(2)}, u32[]{:S(2)}) collective-permute-start(bf16[2,8,144,128]{3,2,1,0:T(8,128)(2,1)S(1)} %collective-permute-done.24.rest_4_), channel_id=1, source_target_pairs={{0,4},{4,0},{1,5},{5,1},{2,6},{6,2},{3,7},{7,3},{8,12},{12,8},{9,1... | collective-permute-start | bytes 1769480 | tf_op jit(solution)/shard_map/ppermute | solution.py:38
  138.4 2.3 %collective-permute-start.27 = (bf16[4,4,144,128]{3,2,1,0:T(8,128)(2,1)S(1)}, bf16[4,4,144,128]{3,2,1,0:T(8,128)(2,1)S(1)}, u32[]{:S(2)}, u32[]{:S(2)}) collective-permute-start(bf16[4,4,144,128]{3,2,1,0:T(8,128)(2,1)S(1)} %collective-permute-done.25.rest_5_), channel_id=1, source_target_pairs={{0,4},{4,0},{1,5},{5,1},{2,6},{6,2},{3,7},{7,3},{8,12},{12,8},{9,1... | collective-permute-start | bytes 1769480 | tf_op jit(solution)/shard_map/ppermute | solution.py:38

commit v4 on v3

--- a/solution.py
+++ b/solution.py
@@ -119,34 +119,27 @@
     )(core.reshape(1), inputs, key_cotangent)
 
 
-def packed(mine, theirs, order_x, order_z, h, partly):
-    def kernel(ox, oz, p, q, *rest):
-        outs, held, sem = rest[-6:-2], rest[-2], rest[-1]
+def packed(terms, theirs, order_x, order_z):
+    def kernel(ox, oz, p0, p1, q0, q1, *rest):
+        outs, held, sem = rest[:4], rest[4], rest[5]
         copies = []
-        for t in (0, 1):
-            rows = pl.ds(t * 1152, 1152)
-            for j, source in enumerate((p, q)):
-                copies.append(pltpu.make_async_copy(source.at[rows, :], held.at[j, rows, :], sem.at[2 * t + j]))
+        for h, pair in enumerate(((p0, q0), (p1, q1))):
+            for t in (0, 1):
+                for j, source in enumerate(pair):
+                    rows = pl.ds(t * 1152, 1152)
+                    target = held.at[j, pl.ds(h * 2304 + t * 1152, 1152), :]
+                    copies.append(pltpu.make_async_copy(source.at[rows, :], target, sem.at[len(copies)]))
         for copy in copies:
             copy.start()
-        if partly:
+        for x in range(4):
+            copies[2 * x].wait()
+            copies[2 * x + 1].wait()
             for i in range(4):
 
-                @pl.when(ox[i] // 2 != h)
-                def _(i=i):
-                    outs[0 if i > 1 else 2][i % 2] = rest[0 if i > 1 else 2][i % 2]
-                    outs[1][:, i] = rest[1][:, i]
-                    outs[3][:, i] = rest[3][:, i]
-
-        for t in (0, 1):
-            copies[2 * t].wait()
-            copies[2 * t + 1].wait()
-            for i in range(4):
-
-                @pl.when(ox[i] == 2 * h + t)
-                def _(i=i, t=t):
+                @pl.when(ox[i] == x)
+                def _(i=i, x=x):
                     for j in range(8):
-                        at = pl.ds(pl.multiple_of(t * 1152 + oz[j] * 144, 8), 144)
+                        at = pl.ds(pl.multiple_of(x * 1152 + oz[j] * 144, 8), 144)
                         outs[0 if i > 1 else 2][i % 2, j] = held[0, at, :128] + held[1, at, :128]
                         outs[1 if j > 3 else 3][j % 4, i] = held[0, at, 128:] + held[1, at, 128:]
 
@@ -154,13 +147,13 @@
     anywhere = pl.BlockSpec(memory_space=pl.ANY)
     return pl.pallas_call(
         kernel,
-        in_specs=[smem, smem, anywhere, anywhere] + [vmem] * len(partly),
+        in_specs=[smem, smem] + [anywhere] * 4,
         out_specs=[vmem] * 4,
         out_shape=[jax.ShapeDtypeStruct((2, 8, 144, 128), f32), jax.ShapeDtypeStruct((4, 4, 144, 128), f32)] * 2,
-        scratch_shapes=[pltpu.VMEM((2, 2304, 256), f32), pltpu.SemaphoreType.DMA((4,))],
-        compiler_params=pltpu.CompilerParams(vmem_limit_bytes=50 << 20),
-        cost_estimate=pl.CostEstimate(flops=1024, bytes_accessed=4096, transcendentals=0),
-    )(order_x, order_z, mine, theirs, *partly)
+        scratch_shapes=[pltpu.VMEM((2, 4608, 256), f32), pltpu.SemaphoreType.DMA((8,))],
+        compiler_params=pltpu.CompilerParams(vmem_limit_bytes=36 << 20),
+        cost_estimate=pl.CostEstimate(flops=1024, bytes_accessed=4096, transcendentals=0),
+    )(order_x, order_z, *[mine for _, mine in terms], *theirs)
 
 
 def written(pieces, orders, core):
@@ -317,10 +310,7 @@
     orders = (order_x, order_z, order_of(X, 1 - c), order_of(Z, 1 - c))
 
     terms = [products(inputs, key_cotangent, c, h) for h in (0, 1)]
-    parts = ()
-    for h, (away, mine) in enumerate(terms):
-        parts = packed(mine, swap(away), order_x, order_z, h, parts)
-    send_a, send_b, keep_a, keep_b = parts
+    send_a, send_b, keep_a, keep_b = packed(terms, [swap(away) for away, _ in terms], order_x, order_z)
 
     come_b = exchange(narrowed(send_b, 2), Z, 0)
     come_a = exchange(narrowed(send_a, 2), X, 0)

time: 144 us -> 137 us (0.951)
  Pallas kernels: 26.7 us -> 20.2 us
  local copies, waits for them, and re-layouts: 6.38 us -> 3.6 us
  waiting for transfers between devices: 36.1 us -> 38.8 us
    pallas_call x2 -> x1, Pallas kernels: 10 us -> 3.48 us  [packed(): pl.pallas_call(kernel, in_specs=[smem, smem] + [anywhere] * 4, out_specs=...]
    ppermute x8, waiting for transfers between devices: 1.64 us -> 4.96 us  [swap(): return lax.ppermute(value, C, [(0, 1), (1, 0)])]
    unnamed x20 -> x16, local copies, waits for them, and re-layouts: 4.47 us -> 1.7 us
    ppermute x20, starting transfers between devices: 31.6 us -> 29 us  [exchange(): return lax.ppermute(value, (axis, C), pairs)]
  transfers between devices with their start and end apart: 29 -> 29, of which waited for: 12 -> 13; matrix products, arithmetic and copies ran while one was open for 5% -> 5% of each run, Pallas kernels for 8% -> 6%
where the time goes in v4:
time: 137 us
  starting transfers between devices  45.8 us (33%)
  waiting for transfers between devices  38.8 us (28%)
  blocking collectives  21.4 us (16%)
  Pallas kernels  20.2 us (15%)
  other arithmetic  5.73 us (4%)
  local copies, waits for them, and re-layouts  3.6 us (3%)
    ppermute x20, starting transfers between devices, exchange(): return lax.ppermute(value, (axis, C), pairs)  29 us
    ppermute x20, waiting for transfers between devices, exchange(): return lax.ppermute(value, (axis, C), pairs)  27.3 us
    all_to_all x1, blocking collectives, met(): return lax.all_to_all(spread, axes, 0, 0, tiled=True)  21.4 us
    pallas_call x2, Pallas kernels, products(): pl.pallas_call(kernel, in_specs=[smem, anywhere, anywhere], out_specs=[an...  10.3 us
    ppermute x8, starting transfers between devices, swap(): return lax.ppermute(value, C, [(0, 1), (1, 0)])  10.1 us
    all_to_all x1, starting transfers between devices, met(): return lax.all_to_all(spread, axes, 0, 0, tiled=True)  6.68 us
    all_to_all x1, waiting for transfers between devices, met(): return lax.all_to_all(spread, axes, 0, 0, tiled=True)  6.52 us
    ppermute x8, waiting for transfers between devices, swap(): return lax.ppermute(value, C, [(0, 1), (1, 0)])  4.96 us
  transfers between devices with their start and end apart: 29, of which 13 were waited for; matrix products, arithmetic and copies ran while one was open for 5% of the time, Pallas kernels for 6%

profile of v4, /device:TPU:1, one launch (start us, length us, event | category | flops | bytes accessed | tf_op | source)
XLA Modules:
  0.0 136.8 jit_solution(12132316227423316439)
XLA Ops:
  0.6 5.1 %shard_map.154 = (f32[2304,256]{1,0:T(8,128)}, f32[2304,256]{1,0:T(8,128)}) custom-call(s32[1]{0:T(128)} %bitcast.4.me, bf16[768,4608]{1,0:T(8,128)(2,1)} %a.3, bf16[768,512]{1,0:T(8,128)(2,1)} %b.3), custom_call_target="tpu_custom_call" | custom-call | flops 1811939328 | bytes 9437184 | tf_op jit(solution)/shard_map/pallas_call | solution.py:106
  5.7 3.3 %collective-permute-start = (f32[2304,256]{1,0:T(8,128)}, f32[2304,256]{1,0:T(8,128)}, u32[]{:S(2)}, u32[]{:S(2)}) collective-permute-start(f32[2304,256]{1,0:T(8,128)} %get-tuple-element.44), channel_id=1, source_target_pairs={{0,4},{4,0},{1,5},{5,1},{2,6},{6,2},{3,7},{7,3},{8,12},{12,8},{9,1... | collective-permute-start | bytes 7077896 | tf_op jit(solution)/shard_map/ppermute | solution.py:38
  9.1 5.2 %shard_map.155 = (f32[2304,256]{1,0:T(8,128)}, f32[2304,256]{1,0:T(8,128)}) custom-call(s32[1]{0:T(128)} %bitcast.4.me, bf16[768,4608]{1,0:T(8,128)(2,1)} %a.3, bf16[768,512]{1,0:T(8,128)(2,1)} %b.3), custom_call_target="tpu_custom_call" | custom-call | flops 1811939328 | bytes 9437184 | tf_op jit(solution)/shard_map/pallas_call | solution.py:106
  14.3 0.1 collective-permute-start.1
  14.4 0.8 fusion.14
  15.2 0.8 fusion.15
  16.0 3.3 %collective-permute-done.1.q1 = f32[2304,256]{1,0:T(8,128)} collective-permute-done((f32[2304,256]{1,0:T(8,128)}, f32[2304,256]{1,0:T(8,128)}, u32[]{:S(2)}, u32[]{:S(2)}) %collective-permute-start.1) | collective-permute-done | bytes 2359328 | tf_op jit(solution)/shard_map/ppermute | solution.py:38
  19.3 1.7 %copy-done.1 = f32[2304,256]{1,0:T(8,128)S(1)} copy-done((f32[2304,256]{1,0:T(8,128)S(1)}, f32[2304,256]{1,0:T(8,128)}, u32[]{:S(2)}) %copy-start.1) | copy-done | bytes 2359320
  21.0 3.5 %shard_map.156 = (f32[2,8,144,128]{3,2,1,0:T(8,128)S(1)}, f32[4,4,144,128]{3,2,1,0:T(8,128)S(1)}, f32[2,8,144,128]{3,2,1,0:T(8,128)S(1)}, f32[4,4,144,128]{3,2,1,0:T(8,128)S(1)}) custom-call(s32[4]{0:T(128)S(1)} %get-tuple-element.87.ox, s32[8]{0:T(128)S(1)} %get-tuple-element.85.oz.o, f32[2304,256]{1,0:T(8,128)S(1)} %copy-done, f32[2304,256]{1,0:T(8,128)S(1)} %copy-done.1, ...), custom_call_target="tpu_custom_call" | custom-call | flops 1024 | bytes 4096 | tf_op jit(solution)/shard_map/pallas_call | solution.py:148
  24.5 0.1 multiply_convert_fusion.1
  24.6 0.8 collective-permute-start.2
  25.4 0.1 multiply_convert_fusion
  25.6 5.7 %collective-permute-start.4 = (f16[4,4,144,128]{3,2,1,0:T(8,128)(2,1)S(1)}, f16[4,4,144,128]{3,2,1,0:T(8,128)(2,1)}, u32[]{:S(2)}, u32[]{:S(2)}) collective-permute-start(f16[4,4,144,128]{3,2,1,0:T(8,128)(2,1)S(1)} %multiply_convert_fusion), channel_id=1, source_target_pairs={{0,8},{4,60},{8,0},{12,20},{16,24},{20,12},{24,16},{28,36},{32,40}... | collective-permute-start | bytes 1769480 | tf_op jit(solution)/shard_map/ppermute | solution.py:45
  31.2 3.5 %collective-permute-done.2 = f16[2,8,144,128]{3,2,1,0:T(8,128)(2,1)} collective-permute-done((f16[2,8,144,128]{3,2,1,0:T(8,128)(2,1)S(1)}, f16[2,8,144,128]{3,2,1,0:T(8,128)(2,1)}, u32[]{:S(2)}, u32[]{:S(2)}) %collective-permute-start.2) | collective-permute-done | bytes 589856 | tf_op jit(solution)/shard_map/ppermute | solution.py:45
  34.7 1.6 %multiply_add_fusion.1 = f32[2,8,144,128]{3,2,1,0:T(8,128)S(1)} fusion(f32[2,8,144,128]{3,2,1,0:T(8,128)} %copy-done.2, f16[2,8,144,128]{3,2,1,0:T(8,128)(2,1)} %collective-permute-done.2), kind=kLoop, calls=%fused_computation.2 | loop fusion | flops 884736 | bytes 2949120 | tf_op jit(solution)/shard_map/add | solution.py:69
  36.3 0.8 fusion.1
  37.1 1.5 %collective-permute-done.4 = f16[4,4,144,128]{3,2,1,0:T(8,128)(2,1)} collective-permute-done((f16[4,4,144,128]{3,2,1,0:T(8,128)(2,1)S(1)}, f16[4,4,144,128]{3,2,1,0:T(8,128)(2,1)}, u32[]{:S(2)}, u32[]{:S(2)}) %collective-permute-start.4) | collective-permute-done | bytes 589856 | tf_op jit(solution)/shard_map/ppermute | solution.py:45
  38.6 0.1 broadcast_in_dim.20
  38.7 0.1 mul.160
  38.8 0.1 broadcast_in_dim.19
  38.9 0.1 mul.154
  39.0 0.1 multiply_bitcast_fusion
  39.2 0.1 collective-permute-start.5
  39.3 1.2 multiply_add_fusion
  40.5 1.3 collective-permute-start.10
  42.0 1.4 collective-permute-done.3
  43.3 1.0 fusion.2
  44.4 3.9 %collective-permute-start.6 = (f16[4,144,128]{2,1,0:T(8,128)(2,1)S(1)}, f16[4,144,128]{2,1,0:T(8,128)(2,1)S(1)}, u32[]{:S(2)}, u32[]{:S(2)}) collective-permute-start(f16[4,144,128]{2,1,0:T(8,128)(2,1)S(1)} %multiply_convert_fusion.2), channel_id=1, source_target_pairs={{0,8},{4,60},{8,0},{12,20},{16,24},{20,12},{24,16},{28,36},{32,40}... | collective-permute-start | bytes 442376 | tf_op jit(solution)/shard_map/ppermute | solution.py:45
  48.4 4.4 %collective-permute-start.11 = (f16[1,4,144,128]{3,2,1,0:T(8,128)(2,1)S(1)}, f16[1,4,144,128]{3,2,1,0:T(8,128)(2,1)S(1)}, u32[]{:S(2)}, u32[]{:S(2)}) collective-permute-start(f16[1,4,144,128]{3,2,1,0:T(8,128)(2,1)S(1)} %fusion.3), channel_id=1, source_target_pairs={{0,24},{4,44},{8,48},{12,36},{16,40},{20,60},{24,0},{28,52},{32,56... | collective-permute-start | bytes 442376 | tf_op jit(solution)/shard_map/ppermute | solution.py:45
  52.9 1.0 collective-permute-start.7
  53.9 1.7 %collective-permute-done.11 = f16[1,4,144,128]{3,2,1,0:T(8,128)(2,1)S(1)} collective-permute-done((f16[1,4,144,128]{3,2,1,0:T(8,128)(2,1)S(1)}, f16[1,4,144,128]{3,2,1,0:T(8,128)(2,1)S(1)}, u32[]{:S(2)}, u32[]{:S(2)}) %collective-permute-start.11) | collective-permute-done | bytes 147488 | tf_op jit(solution)/shard_map/ppermute | solution.py:45
  55.7 4.2 %collective-permute-start.12 = (f16[2,144,128]{2,1,0:T(8,128)(2,1)S(1)}, f16[2,144,128]{2,1,0:T(8,128)(2,1)S(1)}, u32[]{:S(2)}, u32[]{:S(2)}) collective-permute-start(f16[2,144,128]{2,1,0:T(8,128)(2,1)S(1)} %fusion.7), channel_id=1, source_target_pairs={{0,64},{4,196},{64,0},{68,132},{128,192},{132,68},{192,128},{196,4... | collective-permute-start | bytes 221192 | tf_op jit(solution)/shard_map/ppermute | solution.py:45
  59.9 0.4 collective-permute-start.8
  60.4 1.3 collective-permute-done.12
  61.7 0.1 collective-permute-start.13
  61.8 4.1 %collective-permute-done.8 = f16[1,144,128]{2,1,0:T(8,128)(2,1)S(1)} collective-permute-done((f16[1,144,128]{2,1,0:T(8,128)(2,1)S(1)}, f16[1,144,128]{2,1,0:T(8,128)(2,1)S(1)}, u32[]{:S(2)}, u32[]{:S(2)}) %collective-permute-start.8) | collective-permute-done | bytes 36896 | tf_op jit(solution)/shard_map/ppermute | solution.py:45
  65.9 0.4 collective-permute-start.9
  66.4 0.5 collective-permute-start.14
  66.8 0.1 shard_map.157
  67.0 21.4 %all_to_all.10.parts = f32[16,8,128]{2,1,0:T(8,128)S(1)} all-to-all(f32[16,8,128]{2,1,0:T(8,128)S(1)} %shard_map.157), channel_id=1, replica_groups=mesh['dp_0'=4,'dp_1'=8,'dp_2'=2,'mp'=4] {'dp_1','dp_2'}, dimensions={0} | all-to-all | bytes 131072 | tf_op jit(solution)/shard_map/all_to_all | solution.py:216
  88.5 0.1 collective-permute-start.15
  88.6 0.1 collective-permute-start.16
  88.7 0.7 shard_map.158
  89.4 6.7 %all-to-all-start.1 = ((f32[16,8,128]{2,1,0:T(8,128)}), f32[16,8,128]{2,1,0:T(8,128)S(1)}, u32[]{:S(2)}, u32[]{:S(2)}) async-start(f32[16,8,128]{2,1,0:T(8,128)} %shard_map.158), calls=%async_computation.1 | async-start | bytes 131072 | tf_op jit(solution)/shard_map/all_to_all | solution.py:216
  96.0 6.5 %all-to-all-done.1.f = f32[16,8,128]{2,1,0:T(8,128)S(1)} async-done(((f32[16,8,128]{2,1,0:T(8,128)}), f32[16,8,128]{2,1,0:T(8,128)S(1)}, u32[]{:S(2)}, u32[]{:S(2)}) %all-to-all-start.1) | async-done | bytes 65568 | tf_op jit(solution)/shard_map/all_to_all | solution.py:216
  102.6 1.0 shard_map.159
  103.6 0.7 collective-permute-start.17
  104.3 1.1 collective-permute-start.20
  105.3 3.7 %collective-permute-start.19 = (bf16[1,4,144,128]{3,2,1,0:T(8,128)(2,1)S(1)}, bf16[1,4,144,128]{3,2,1,0:T(8,128)(2,1)S(1)}, u32[]{:S(2)}, u32[]{:S(2)}) collective-permute-start(bf16[1,4,144,128]{3,2,1,0:T(8,128)(2,1)S(1)} %bitcast.45), channel_id=1, source_target_pairs={{0,24},{4,44},{8,48},{12,36},{16,40},{20,60},{24,0},{28,52},{32,56... | collective-permute-start | bytes 442376 | tf_op jit(solution)/shard_map/ppermute | solution.py:45
  109.1 0.6 shard_map.160
  109.6 0.3 collective-permute-start.18
  110.0 5.5 %collective-permute-done.19 = bf16[1,4,144,128]{3,2,1,0:T(8,128)(2,1)S(1)} collective-permute-done((bf16[1,4,144,128]{3,2,1,0:T(8,128)(2,1)S(1)}, bf16[1,4,144,128]{3,2,1,0:T(8,128)(2,1)S(1)}, u32[]{:S(2)}, u32[]{:S(2)}) %collective-permute-start.19) | collective-permute-done | bytes 147488 | tf_op jit(solution)/shard_map/ppermute | solution.py:45
  115.5 0.1 collective-permute-start.21
  115.6 1.1 shard_map.161
  116.8 0.9 collective-permute-start.24
  117.7 3.5 %collective-permute-done.21 = bf16[2,4,144,128]{3,2,1,0:T(8,128)(2,1)S(1)} collective-permute-done((bf16[2,4,144,128]{3,2,1,0:T(8,128)(2,1)S(1)}, bf16[2,4,144,128]{3,2,1,0:T(8,128)(2,1)S(1)}, u32[]{:S(2)}, u32[]{:S(2)}) %collective-permute-start.21) | collective-permute-done | bytes 294944 | tf_op jit(solution)/shard_map/ppermute | solution.py:45
  121.3 0.4 collective-permute-start.25
  121.7 2.5 %collective-permute-start.22 = (bf16[2,8,144,128]{3,2,1,0:T(8,128)(2,1)S(1)}, bf16[2,8,144,128]{3,2,1,0:T(8,128)(2,1)S(1)}, u32[]{:S(2)}, u32[]{:S(2)}) collective-permute-start(bf16[2,8,144,128]{3,2,1,0:T(8,128)(2,1)S(1)} %pad_maximum_fusion.2.rest_0_), channel_id=1, source_target_pairs={{0,4},{4,0},{1,5},{5,1},{2,6},{6,2},{3,7},{7,3},{8,12},{12,8},{9,1... | collective-permute-start | bytes 1769480 | tf_op jit(solution)/shard_map/ppermute | solution.py:38
  124.2 2.6 %collective-permute-done.24.rest_4_ = bf16[2,8,144,128]{3,2,1,0:T(8,128)(2,1)S(1)} collective-permute-done((bf16[2,8,144,128]{3,2,1,0:T(8,128)(2,1)S(1)}, bf16[2,8,144,128]{3,2,1,0:T(8,128)(2,1)S(1)}, u32[]{:S(2)}, u32[]{:S(2)}) %collective-permute-start.24) | collective-permute-done | bytes 589856 | tf_op jit(solution)/shard_map/ppermute | solution.py:45
  126.8 2.2 %collective-permute-start.26 = (bf16[2,8,144,128]{3,2,1,0:T(8,128)(2,1)S(1)}, bf16[2,8,144,128]{3,2,1,0:T(8,128)(2,1)S(1)}, u32[]{:S(2)}, u32[]{:S(2)}) collective-permute-start(bf16[2,8,144,128]{3,2,1,0:T(8,128)(2,1)S(1)} %collective-permute-done.24.rest_4_), channel_id=1, source_target_pairs={{0,4},{4,0},{1,5},{5,1},{2,6},{6,2},{3,7},{7,3},{8,12},{12,8},{9,1... | collective-permute-start | bytes 1769480 | tf_op jit(solution)/shard_map/ppermute | solution.py:38
  129.0 2.3 %collective-permute-done.25.rest_5_ = bf16[4,4,144,128]{3,2,1,0:T(8,128)(2,1)S(1)} collective-permute-done((bf16[4,4,144,128]{3,2,1,0:T(8,128)(2,1)S(1)}, bf16[4,4,144,128]{3,2,1,0:T(8,128)(2,1)S(1)}, u32[]{:S(2)}, u32[]{:S(2)}) %collective-permute-start.25) | collective-permute-done | bytes 589856 | tf_op jit(solution)/shard_map/ppermute | solution.py:45
  131.3 0.8 collective-permute-start.27
  132.1 1.6 %collective-permute-done.27.rest_7_ = bf16[4,4,144,128]{3,2,1,0:T(8,128)(2,1)S(1)} collective-permute-done((bf16[4,4,144,128]{3,2,1,0:T(8,128)(2,1)S(1)}, bf16[4,4,144,128]{3,2,1,0:T(8,128)(2,1)S(1)}, u32[]{:S(2)}, u32[]{:S(2)}) %collective-permute-start.27) | collective-permute-done | bytes 589856 | tf_op jit(solution)/shard_map/ppermute | solution.py:38
  133.7 2.9 %shard_map.162 = bf16[4,8,144,512]{3,2,1,0:T(8,128)(2,1)} custom-call(s32[4]{0:T(128)S(1)} %get-tuple-element.87.ox, s32[8]{0:T(128)S(1)} %get-tuple-element.85.oz.o, s32[4]{0:T(128)S(1)} %get-tuple-element.86.px, s32[8]{0:T(128)S(1)} %get-tuple-element.84.pz, s32[1]{0:T(128)} %bitcast.4.me, bf16[2,8,144,128]{3,2,1,0:T(8,128)(2,1)S(1)} %pad_maximum_fusion.2.rest_0_, ...), custom_call_target="tpu_custom_call" | custom-call | flops 1024 | bytes 4096 | tf_op jit(solution)/shard_map/pallas_call | solution.py:181
  (63 shorter events, 0.9 us)
Async XLA Ops:
  5.7 10.2 %collective-permute-start = (f32[2304,256]{1,0:T(8,128)}, f32[2304,256]{1,0:T(8,128)}, u32[]{:S(2)}, u32[]{:S(2)}) collective-permute-start(f32[2304,256]{1,0:T(8,128)} %get-tuple-element.44), channel_id=1, source_target_pairs={{0,4},{4,0},{1,5},{5,1},{2,6},{6,2},{3,7},{7,3},{8,12},{12,8},{9,1... | collective-permute-start | bytes 7077896 | tf_op jit(solution)/shard_map/ppermute | solution.py:38
  9.1 10.2 %copy-start = (f32[2304,256]{1,0:T(8,128)S(1)}, f32[2304,256]{1,0:T(8,128)}, u32[]{:S(2)}) copy-start(f32[2304,256]{1,0:T(8,128)} %get-tuple-element.42.p0) | copy-start | bytes 7077892
  14.3 5.0 %collective-permute-start.1 = (f32[2304,256]{1,0:T(8,128)}, f32[2304,256]{1,0:T(8,128)}, u32[]{:S(2)}, u32[]{:S(2)}) collective-permute-start(f32[2304,256]{1,0:T(8,128)} %get-tuple-element.45), channel_id=1, source_target_pairs={{0,4},{4,0},{1,5},{5,1},{2,6},{6,2},{3,7},{7,3},{8,12},{12,8},{9,1... | collective-permute-start | bytes 7077896 | tf_op jit(solution)/shard_map/ppermute | solution.py:38
  19.3 1.7 %copy-start.1 = (f32[2304,256]{1,0:T(8,128)S(1)}, f32[2304,256]{1,0:T(8,128)}, u32[]{:S(2)}) copy-start(f32[2304,256]{1,0:T(8,128)} %get-tuple-element.43.p1) | copy-start | bytes 7077892
  24.4 1.1 copy-start.2
  24.6 10.1 %collective-permute-start.2 = (f16[2,8,144,128]{3,2,1,0:T(8,128)(2,1)S(1)}, f16[2,8,144,128]{3,2,1,0:T(8,128)(2,1)}, u32[]{:S(2)}, u32[]{:S(2)}) collective-permute-start(f16[2,8,144,128]{3,2,1,0:T(8,128)(2,1)S(1)} %multiply_convert_fusion.1), channel_id=1, source_target_pairs={{0,64},{4,196},{64,0},{68,132},{128,192},{132,68},{192,128},{196,4... | collective-permute-start | bytes 1769480 | tf_op jit(solution)/shard_map/ppermute | solution.py:45
  25.6 13.0 %collective-permute-start.4 = (f16[4,4,144,128]{3,2,1,0:T(8,128)(2,1)S(1)}, f16[4,4,144,128]{3,2,1,0:T(8,128)(2,1)}, u32[]{:S(2)}, u32[]{:S(2)}) collective-permute-start(f16[4,4,144,128]{3,2,1,0:T(8,128)(2,1)S(1)} %multiply_convert_fusion), channel_id=1, source_target_pairs={{0,8},{4,60},{8,0},{12,20},{16,24},{20,12},{24,16},{28,36},{32,40}... | collective-permute-start | bytes 1769480 | tf_op jit(solution)/shard_map/ppermute | solution.py:45
  34.7 3.9 %copy-start.6 = (f32[18,1]{0,1:T(1,128)S(1)}, f32[18,1]{0,1:T(1,128)}, u32[]{:S(2)}) copy-start(f32[18,1]{0,1:T(1,128)} %param.17) | copy-start | bytes 220
  34.7 4.1 %copy-start.7 = (f32[18,1]{0,1:T(1,128)S(1)}, f32[18,1]{0,1:T(1,128)}, u32[]{:S(2)}) copy-start(f32[18,1]{0,1:T(1,128)} %param.16) | copy-start | bytes 220
  34.7 4.2 %copy-start.4 = (s32[72,512]{1,0:T(8,128)S(1)}, s32[72,512]{1,0:T(8,128)}, u32[]{:S(2)}) copy-start(s32[72,512]{1,0:T(8,128)} %param.15) | copy-start | bytes 442372
  34.7 4.2 %copy-start.5 = (s32[72,512]{1,0:T(8,128)S(1)}, s32[72,512]{1,0:T(8,128)}, u32[]{:S(2)}) copy-start(s32[72,512]{1,0:T(8,128)} %param.14) | copy-start | bytes 442372
  36.3 2.7 %copy-start.3 = (f32[72,512]{1,0:T(8,128)S(1)}, f32[72,512]{1,0:T(8,128)}, u32[]{:S(2)}) copy-start(f32[72,512]{1,0:T(8,128)} %param.13) | copy-start | bytes 442372
  37.1 6.2 %collective-permute-start.3 = (f16[1,8,144,128]{3,2,1,0:T(8,128)(2,1)}, f16[1,8,144,128]{3,2,1,0:T(8,128)(2,1)}, u32[]{:S(2)}, u32[]{:S(2)}) collective-permute-start(f16[1,8,144,128]{3,2,1,0:T(8,128)(2,1)} %fusion.1), channel_id=1, source_target_pairs={{0,192},{4,68},{64,128},{68,4},{128,64},{132,196},{192,0},{196,132... | collective-permute-start | bytes 884744 | tf_op jit(solution)/shard_map/ppermute | solution.py:45
  39.2 2.7 %collective-permute-start.5 = (f32[3,72,256]{2,1,0:T(8,128)S(1)}, f32[3,72,256]{2,1,0:T(8,128)S(1)}, u32[]{:S(2)}, u32[]{:S(2)}) collective-permute-start(f32[3,72,256]{2,1,0:T(8,128)S(1)} %constant_dynamic-slice_fusion), channel_id=1, source_target_pairs={{0,4},{4,0},{1,5},{5,1},{2,6},{6,2},{3,7},{7,3},{8,12},{12,8},{9,1... | collective-permute-start | bytes 663560 | tf_op jit(solution)/shard_map/ppermute | solution.py:38
  40.5 7.8 %collective-permute-start.10 = (f16[2,4,144,128]{3,2,1,0:T(8,128)(2,1)S(1)}, f16[2,4,144,128]{3,2,1,0:T(8,128)(2,1)S(1)}, u32[]{:S(2)}, u32[]{:S(2)}) collective-permute-start(f16[2,4,144,128]{3,2,1,0:T(8,128)(2,1)S(1)} %fusion), channel_id=1, source_target_pairs={{0,56},{4,12},{8,16},{12,4},{16,8},{20,28},{24,32},{28,20},{32,24}... | collective-permute-start | bytes 884744 | tf_op jit(solution)/shard_map/ppermute | solution.py:45
  44.4 8.4 %collective-permute-start.6 = (f16[4,144,128]{2,1,0:T(8,128)(2,1)S(1)}, f16[4,144,128]{2,1,0:T(8,128)(2,1)S(1)}, u32[]{:S(2)}, u32[]{:S(2)}) collective-permute-start(f16[4,144,128]{2,1,0:T(8,128)(2,1)S(1)} %multiply_convert_fusion.2), channel_id=1, source_target_pairs={{0,8},{4,60},{8,0},{12,20},{16,24},{20,12},{24,16},{28,36},{32,40}... | collective-permute-start | bytes 442376 | tf_op jit(solution)/shard_map/ppermute | solution.py:45
  48.4 7.2 %collective-permute-start.11 = (f16[1,4,144,128]{3,2,1,0:T(8,128)(2,1)S(1)}, f16[1,4,144,128]{3,2,1,0:T(8,128)(2,1)S(1)}, u32[]{:S(2)}, u32[]{:S(2)}) collective-permute-start(f16[1,4,144,128]{3,2,1,0:T(8,128)(2,1)S(1)} %fusion.3), channel_id=1, source_target_pairs={{0,24},{4,44},{8,48},{12,36},{16,40},{20,60},{24,0},{28,52},{32,56... | collective-permute-start | bytes 442376 | tf_op jit(solution)/shard_map/ppermute | solution.py:45
  52.9 7.0 %collective-permute-start.7 = (f16[2,144,128]{2,1,0:T(8,128)(2,1)S(1)}, f16[2,144,128]{2,1,0:T(8,128)(2,1)S(1)}, u32[]{:S(2)}, u32[]{:S(2)}) collective-permute-start(f16[2,144,128]{2,1,0:T(8,128)(2,1)S(1)} %fusion.6), channel_id=1, source_target_pairs={{0,56},{4,12},{8,16},{12,4},{16,8},{20,28},{24,32},{28,20},{32,24}... | collective-permute-start | bytes 221192 | tf_op jit(solution)/shard_map/ppermute | solution.py:45
  55.7 5.9 %collective-permute-start.12 = (f16[2,144,128]{2,1,0:T(8,128)(2,1)S(1)}, f16[2,144,128]{2,1,0:T(8,128)(2,1)S(1)}, u32[]{:S(2)}, u32[]{:S(2)}) collective-permute-start(f16[2,144,128]{2,1,0:T(8,128)(2,1)S(1)} %fusion.7), channel_id=1, source_target_pairs={{0,64},{4,196},{64,0},{68,132},{128,192},{132,68},{192,128},{196,4... | collective-permute-start | bytes 221192 | tf_op jit(solution)/shard_map/ppermute | solution.py:45
  59.9 5.9 %collective-permute-start.8 = (f16[1,144,128]{2,1,0:T(8,128)(2,1)S(1)}, f16[1,144,128]{2,1,0:T(8,128)(2,1)S(1)}, u32[]{:S(2)}, u32[]{:S(2)}) collective-permute-start(f16[1,144,128]{2,1,0:T(8,128)(2,1)S(1)} %fusion.11), channel_id=1, source_target_pairs={{0,24},{4,44},{8,48},{12,36},{16,40},{20,60},{24,0},{28,52},{32,56... | collective-permute-start | bytes 110600 | tf_op jit(solution)/shard_map/ppermute | solution.py:45
  61.7 4.7 %collective-permute-start.13 = (f16[1,144,128]{2,1,0:T(8,128)(2,1)S(1)}, f16[1,144,128]{2,1,0:T(8,128)(2,1)S(1)}, u32[]{:S(2)}, u32[]{:S(2)}) collective-permute-start(f16[1,144,128]{2,1,0:T(8,128)(2,1)S(1)} %fusion.10), channel_id=1, source_target_pairs={{0,192},{4,68},{64,128},{68,4},{128,64},{132,196},{192,0},{196,132... | collective-permute-start | bytes 110600 | tf_op jit(solution)/shard_map/ppermute | solution.py:45
  65.9 22.5 %collective-permute-start.9 = (f32[1,4,144,128]{3,2,1,0:T(8,128)S(1)}, f32[1,4,144,128]{3,2,1,0:T(8,128)S(1)}, u32[]{:S(2)}, u32[]{:S(2)}) collective-permute-start(f32[1,4,144,128]{3,2,1,0:T(8,128)S(1)} %maximum_bitcast_fusion), channel_id=1, source_target_pairs={{0,24},{4,44},{8,48},{12,36},{16,40},{20,60},{24,0},{28,52},{32,56... | collective-permute-start | bytes 884744 | tf_op jit(solution)/shard_map/ppermute | solution.py:45
  66.4 22.0 %collective-permute-start.14 = (f32[1,4,144,128]{3,2,1,0:T(8,128)S(1)}, f32[1,4,144,128]{3,2,1,0:T(8,128)S(1)}, u32[]{:S(2)}, u32[]{:S(2)}) collective-permute-start(f32[1,4,144,128]{3,2,1,0:T(8,128)S(1)} %maximum_bitcast_fusion.1), channel_id=1, source_target_pairs={{0,192},{4,68},{64,128},{68,4},{128,64},{132,196},{192,0},{196,132... | collective-permute-start | bytes 884744 | tf_op jit(solution)/shard_map/ppermute | solution.py:45
  88.5 14.1 %collective-permute-start.15 = (f32[2,4,144,128]{3,2,1,0:T(8,128)S(1)}, f32[2,4,144,128]{3,2,1,0:T(8,128)S(1)}, u32[]{:S(2)}, u32[]{:S(2)}) collective-permute-start(f32[2,4,144,128]{3,2,1,0:T(8,128)S(1)} %pad_maximum_fusion.a0), channel_id=1, source_target_pairs={{0,56},{4,12},{8,16},{12,4},{16,8},{20,28},{24,32},{28,20},{32,24}... | collective-permute-start | bytes 1769480 | tf_op jit(solution)/shard_map/ppermute | solution.py:45
  88.6 14.0 %collective-permute-start.16 = (f32[2,4,144,128]{3,2,1,0:T(8,128)S(1)}, f32[2,4,144,128]{3,2,1,0:T(8,128)S(1)}, u32[]{:S(2)}, u32[]{:S(2)}) collective-permute-start(f32[2,4,144,128]{3,2,1,0:T(8,128)S(1)} %pad_maximum_fusion.1.b0), channel_id=1, source_target_pairs={{0,64},{4,196},{64,0},{68,132},{128,192},{132,68},{192,128},{196,4... | collective-permute-start | bytes 1769480 | tf_op jit(solution)/shard_map/ppermute | solution.py:45
  89.4 13.2 %all-to-all-start.1 = ((f32[16,8,128]{2,1,0:T(8,128)}), f32[16,8,128]{2,1,0:T(8,128)S(1)}, u32[]{:S(2)}, u32[]{:S(2)}) async-start(f32[16,8,128]{2,1,0:T(8,128)} %shard_map.158), calls=%async_computation.1 | async-start | bytes 131072 | tf_op jit(solution)/shard_map/all_to_all | solution.py:216
  103.6 5.4 %collective-permute-start.17 = (bf16[4,144,128]{2,1,0:T(8,128)(2,1)S(1)}, bf16[4,144,128]{2,1,0:T(8,128)(2,1)S(1)}, u32[]{:S(2)}, u32[]{:S(2)}) collective-permute-start(bf16[4,144,128]{2,1,0:T(8,128)(2,1)S(1)} %get-tuple-element.61.a), channel_id=1, source_target_pairs={{0,8},{4,60},{8,0},{12,20},{16,24},{20,12},{24,16},{28,36},{32,40}... | collective-permute-start | bytes 442376 | tf_op jit(solution)/shard_map/ppermute | solution.py:45
  104.3 5.7 %collective-permute-start.20 = (f32[72,256]{1,0:T(8,128)S(1)}, f32[72,256]{1,0:T(8,128)S(1)}, u32[]{:S(2)}, u32[]{:S(2)}) collective-permute-start(f32[72,256]{1,0:T(8,128)S(1)} %fusion.8), channel_id=1, source_target_pairs={{0,4},{4,0},{1,5},{5,1},{2,6},{6,2},{3,7},{7,3},{8,12},{12,8},{9,1... | collective-permute-start | bytes 221192 | tf_op jit(solution)/shard_map/ppermute | solution.py:38
  105.3 10.2 %collective-permute-start.19 = (bf16[1,4,144,128]{3,2,1,0:T(8,128)(2,1)S(1)}, bf16[1,4,144,128]{3,2,1,0:T(8,128)(2,1)S(1)}, u32[]{:S(2)}, u32[]{:S(2)}) collective-permute-start(bf16[1,4,144,128]{3,2,1,0:T(8,128)(2,1)S(1)} %bitcast.45), channel_id=1, source_target_pairs={{0,24},{4,44},{8,48},{12,36},{16,40},{20,60},{24,0},{28,52},{32,56... | collective-permute-start | bytes 442376 | tf_op jit(solution)/shard_map/ppermute | solution.py:45
  109.6 7.1 %collective-permute-start.18 = (bf16[1,8,144,128]{3,2,1,0:T(8,128)(2,1)S(1)}, bf16[1,8,144,128]{3,2,1,0:T(8,128)(2,1)S(1)}, u32[]{:S(2)}, u32[]{:S(2)}) collective-permute-start(bf16[1,8,144,128]{3,2,1,0:T(8,128)(2,1)S(1)} %bitcast.43), channel_id=1, source_target_pairs={{0,192},{4,68},{64,128},{68,4},{128,64},{132,196},{192,0},{196,132... | collective-permute-start | bytes 884744 | tf_op jit(solution)/shard_map/ppermute | solution.py:45
  115.5 5.7 %collective-permute-start.21 = (bf16[2,4,144,128]{3,2,1,0:T(8,128)(2,1)S(1)}, bf16[2,4,144,128]{3,2,1,0:T(8,128)(2,1)S(1)}, u32[]{:S(2)}, u32[]{:S(2)}) collective-permute-start(bf16[2,4,144,128]{3,2,1,0:T(8,128)(2,1)S(1)} %pad_maximum_fusion.6), channel_id=1, source_target_pairs={{0,56},{4,12},{8,16},{12,4},{16,8},{20,28},{24,32},{28,20},{32,24}... | collective-permute-start | bytes 884744 | tf_op jit(solution)/shard_map/ppermute | solution.py:45
  116.8 10.0 %collective-permute-start.24 = (bf16[2,8,144,128]{3,2,1,0:T(8,128)(2,1)S(1)}, bf16[2,8,144,128]{3,2,1,0:T(8,128)(2,1)S(1)}, u32[]{:S(2)}, u32[]{:S(2)}) collective-permute-start(bf16[2,8,144,128]{3,2,1,0:T(8,128)(2,1)S(1)} %pad_maximum_fusion.2.rest_0_), channel_id=1, source_target_pairs={{0,64},{4,196},{64,0},{68,132},{128,192},{132,68},{192,128},{196,4... | collective-permute-start | bytes 1769480 | tf_op jit(solution)/shard_map/ppermute | solution.py:45
  121.3 10.0 %collective-permute-start.25 = (bf16[4,4,144,128]{3,2,1,0:T(8,128)(2,1)S(1)}, bf16[4,4,144,128]{3,2,1,0:T(8,128)(2,1)S(1)}, u32[]{:S(2)}, u32[]{:S(2)}) collective-permute-start(bf16[4,4,144,128]{3,2,1,0:T(8,128)(2,1)S(1)} %pad_maximum_fusion.3.rest_1_), channel_id=1, source_target_pairs={{0,8},{4,60},{8,0},{12,20},{16,24},{20,12},{24,16},{28,36},{32,40}... | collective-permute-start | bytes 1769480 | tf_op jit(solution)/shard_map/ppermute | solution.py:45
  121.7 10.4 %collective-permute-start.22 = (bf16[2,8,144,128]{3,2,1,0:T(8,128)(2,1)S(1)}, bf16[2,8,144,128]{3,2,1,0:T(8,128)(2,1)S(1)}, u32[]{:S(2)}, u32[]{:S(2)}) collective-permute-start(bf16[2,8,144,128]{3,2,1,0:T(8,128)(2,1)S(1)} %pad_maximum_fusion.2.rest_0_), channel_id=1, source_target_pairs={{0,4},{4,0},{1,5},{5,1},{2,6},{6,2},{3,7},{7,3},{8,12},{12,8},{9,1... | collective-permute-start | bytes 1769480 | tf_op jit(solution)/shard_map/ppermute | solution.py:38
  124.2 7.9 %collective-permute-start.23 = (bf16[4,4,144,128]{3,2,1,0:T(8,128)(2,1)S(1)}, bf16[4,4,144,128]{3,2,1,0:T(8,128)(2,1)S(1)}, u32[]{:S(2)}, u32[]{:S(2)}) collective-permute-start(bf16[4,4,144,128]{3,2,1,0:T(8,128)(2,1)S(1)} %pad_maximum_fusion.3.rest_1_), channel_id=1, source_target_pairs={{0,4},{4,0},{1,5},{5,1},{2,6},{6,2},{3,7},{7,3},{8,12},{12,8},{9,1... | collective-permute-start | bytes 1769480 | tf_op jit(solution)/shard_map/ppermute | solution.py:38
  126.8 5.3 %collective-permute-start.26 = (bf16[2,8,144,128]{3,2,1,0:T(8,128)(2,1)S(1)}, bf16[2,8,144,128]{3,2,1,0:T(8,128)(2,1)S(1)}, u32[]{:S(2)}, u32[]{:S(2)}) collective-permute-start(bf16[2,8,144,128]{3,2,1,0:T(8,128)(2,1)S(1)} %collective-permute-done.24.rest_4_), channel_id=1, source_target_pairs={{0,4},{4,0},{1,5},{5,1},{2,6},{6,2},{3,7},{7,3},{8,12},{12,8},{9,1... | collective-permute-start | bytes 1769480 | tf_op jit(solution)/shard_map/ppermute | solution.py:38
  131.3 2.4 %collective-permute-start.27 = (bf16[4,4,144,128]{3,2,1,0:T(8,128)(2,1)S(1)}, bf16[4,4,144,128]{3,2,1,0:T(8,128)(2,1)S(1)}, u32[]{:S(2)}, u32[]{:S(2)}) collective-permute-start(bf16[4,4,144,128]{3,2,1,0:T(8,128)(2,1)S(1)} %collective-permute-done.25.rest_5_), channel_id=1, source_target_pairs={{0,4},{4,0},{1,5},{5,1},{2,6},{6,2},{3,7},{7,3},{8,12},{12,8},{9,1... | collective-permute-start | bytes 1769480 | tf_op jit(solution)/shard_map/ppermute | solution.py:38
